TPU v7x, 32 devices: a whole 2x2x4 slice. The times are simulated.
32 devices in a mesh: axial: 16 (over z, x, core), azim: 2 (over y).
Axes of the slice: x: 2, y: 2, z: 4, core: 2. Of those that a mesh axis runs over, the one named last changes fastest.
Arguments:
- adjoint_source: float32 [32, 4, 5, 15, 128], P('axial', 'azim'), may hold values from -0.6 to 0.6
- adjoint_prev: float32 [32, 4, 5, 15, 128], P('axial', 'azim'), may hold values from -1.8 to 1.8
- diag_inverse: bfloat16 [32, 4, 5, 5, 15, 128], P('axial', 'azim'), may hold values from -0.1 to 1
- coupling: float32 [3, 32, 4, 15, 128], P(None, 'axial', 'azim'), may hold values from 0.1 to 1.03
- spectral: float32 [15, 15], replicated, may hold values from -0.6 to 0.6
- face_map: int32 [512], P('azim'), may hold values from 0 to 511, each once
Outputs:
- adjoint: float32 [32, 4, 5, 15, 128], P('axial', 'azim')
Inputs may be any that keep to these rules, and one draw needn't show every extreme that they name: `face_map`: each rudder interface cell is named by exactly one propeller interface cell.
All inputs are finite; a program needn't handle non-finite values.
Results may differ from a plain program's by a relative error of at most 0.0003.
Values sent between devices are 32-bit elements; how exact they have to be, the bound alone decides.
No kernel may reach another device: no remote copies, remote signals or barrier semaphores. Data moves between devices by JAX's collectives and lax.ppermute only.
A program may use at most 64 MiB of HBM per device.

v0:
```python
import jax
import jax.numpy as jnp
from jax import lax
from jax.sharding import PartitionSpec as P

ITERS = 2


def entering(x, axis, combine, identity, reverse):
    size, here = (lax.axis_size(axis), lax.axis_index(axis))
    everything = jax.tree.map(lambda part: lax.all_gather(part, axis), x)
    start = jax.tree.map(
        lambda part, zero: jnp.broadcast_to(jnp.asarray(zero, part.dtype), part.shape), x, identity
    )

    def step(k, before):
        at = size - 1 - k if reverse else k
        reached = at > here if reverse else at < here
        new = combine(before, jax.tree.map(lambda part: part[at], everything))
        return jax.tree.map(lambda a, b: jnp.where(reached, a, b), new, before)

    return lax.fori_loop(0, size, step, start)


def with_halo(cells, sides, width):
    for axis, dim in sides:
        count = lax.axis_size(axis)
        head = lax.slice_in_dim(cells, 0, width, axis=dim)
        tail = lax.slice_in_dim(cells, cells.shape[dim] - width, cells.shape[dim], axis=dim)
        cells = jnp.concatenate(
            [
                lax.ppermute(tail, axis, [(i, (i + 1) % count) for i in range(count)]),
                cells,
                lax.ppermute(head, axis, [((i + 1) % count, i) for i in range(count)]),
            ],
            axis=dim,
        )
    return cells


def apply_inverse(inverse, vector):
    return jnp.sum(inverse.astype(jnp.float32) * vector[:, None], axis=2)


def make_rhs(source, lower_rim, upper_rim, previous, side_coef, spectral):
    coupled = jnp.einsum("hk,...kr->...hr", spectral, previous, precision=lax.Precision.HIGHEST)
    return source + jnp.expand_dims(side_coef, -3) * (lower_rim + upper_rim) - coupled


def forward_section(right_side, inverse, lower_coef, arriving):

    def forward_plane_step(carried, plane_items):
        plane_source, plane_inverse, plane_coef = plane_items
        fresh = apply_inverse(
            plane_inverse, plane_source + jnp.expand_dims(plane_coef, -3) * carried
        )
        return (fresh, fresh)

    unused, values = lax.scan(forward_plane_step, arriving, (right_side, inverse, lower_coef))
    return values


def backward_section(front_vals, inverse, upper_coef, arriving):

    def backward_plane_step(carried, plane_items):
        plane_front, plane_inverse, plane_coef = plane_items
        fresh = plane_front - jnp.expand_dims(plane_coef, -3) * apply_inverse(
            plane_inverse, carried
        )
        return (fresh, fresh)

    unused, values = lax.scan(
        backward_plane_step, arriving, (front_vals, inverse, upper_coef), reverse=True
    )
    return values


def mat_apply(matrix, vector):
    return jnp.sum(matrix * vector[:, None], axis=2)


def mat_mul(left, right):
    return jnp.sum(left[:, :, :, None] * right[:, None], axis=2)


def combine_maps(earlier, later):
    return (mat_mul(later[0], earlier[0]), mat_apply(later[0], earlier[1]) + later[1])


def compose_planes(matrices, vectors, unit, reverse):

    def compose_plane_step(carried, plane_items):
        plane_mat, plane_vec = plane_items
        return ((mat_mul(plane_mat, carried[0]), mat_apply(plane_mat, carried[1]) + plane_vec), 0)

    start = (unit, jnp.zeros(vectors.shape[1:], jnp.float32))
    composed, unused = lax.scan(compose_plane_step, start, (matrices, vectors), reverse=reverse)
    return composed


def split_rows(count_rows, pieces):
    step_rows = count_rows // pieces
    return [(0, step_rows)]


def forward_prefix(matrix, vector, unit, pieces):
    outcome = []
    for row_start, count_rows in split_rows(matrix.shape[0], pieces):
        element = (matrix, vector)
        identity = (unit, jnp.zeros_like(element[1]))
        result = entering(element, "axial", combine_maps, identity, False)
        outcome.append(result[1])
    return outcome[0]


def backward_prefix(matrix, vector, unit, pieces):
    outcome = []
    for row_start, count_rows in split_rows(matrix.shape[0], pieces):
        element = (matrix, vector)
        identity = (unit, jnp.zeros_like(element[1]))
        result = entering(element, "axial", combine_maps, identity, True)
        outcome.append(result[1])
    return outcome[0]


def shards(adjoint_source, adjoint_prev, diag_inverse, coupling, spectral, face_map):
    devices = lax.axis_size("axial")
    section = devices // 2
    position = lax.axis_index("axial")
    offset_in = jnp.where(position >= section, position - section, position)
    azim_rows = adjoint_source.shape[1]
    fields, instances, radial = (
        adjoint_source.shape[2],
        adjoint_source.shape[3],
        adjoint_source.shape[4],
    )
    lower_coef, upper_coef, side_coef = (coupling[0], coupling[1], coupling[2])
    pieces = 1
    unit = jnp.eye(fields, dtype=jnp.float32)[None, :, :, None, None] * jnp.ones(
        (azim_rows, 1, 1, instances, radial), jnp.float32
    )
    inverse_wide = diag_inverse.astype(jnp.float32)
    current = adjoint_prev
    for sweep_index in range(ITERS):
        padded = with_halo(current, (("azim", 1),), 1)
        right_side = make_rhs(
            adjoint_source, padded[:, :-2], padded[:, 2:], current, side_coef, spectral
        )
        plane_flat = jnp.transpose(current[0], (1, 2, 0, 3)).reshape(
            fields * instances, azim_rows * radial
        )
        gathered = lax.all_gather(plane_flat, "azim", axis=1, tiled=True)
        picked = (
            jnp.take(gathered, face_map, axis=1)
            .reshape(fields, instances, azim_rows, radial)
            .transpose(2, 0, 1, 3)
        )
        forward_mat = inverse_wide * lower_coef[:, :, None, None]
        forward_vec = jnp.sum(inverse_wide * right_side[:, :, None], axis=3)
        local_mat, local_vec = compose_planes(forward_mat, forward_vec, unit, False)
        closed = offset_in == section - 1
        local_mat = jnp.where(closed, jnp.zeros_like(local_mat), local_mat)
        local_vec = jnp.where(closed, jnp.zeros_like(local_vec), local_vec)
        arriving = forward_prefix(local_mat, local_vec, unit, pieces)
        front_vals = forward_section(right_side, diag_inverse, lower_coef, arriving)
        backward_mat = -(inverse_wide * upper_coef[:, :, None, None])
        local_mat, local_vec = compose_planes(backward_mat, front_vals, unit, True)
        facing = position == section
        local_mat = jnp.where(facing, jnp.zeros_like(local_mat), local_mat)
        local_vec = jnp.where(facing, picked, local_vec)
        arriving = backward_prefix(local_mat, local_vec, unit, pieces)
        current = backward_section(front_vals, diag_inverse, upper_coef, arriving)
    return current


def solution(mesh):
    placed = (
        P("axial", "azim", None, None, None),
        P("axial", "azim", None, None, None),
        P("axial", "azim", None, None, None, None),
        P(None, "axial", "azim", None, None),
        P(),
        P("azim"),
    )
    return jax.shard_map(
        shards,
        mesh=mesh,
        in_specs=placed,
        out_specs=P("axial", "azim", None, None, None),
        check_vma=False,
    )
```

profile of v0, /device:TPU:0, one launch (start us, length us, event | category | flops | bytes accessed | tf_op | source)
XLA Modules:
  0.0 590.3 jit_solution(2012911691397199846)
XLA Ops:
  7.5 3.0 collective-permute-start
  11.5 1.9 collective-permute-done
  13.4 1.7 collective-permute-done.1
  15.0 1.2 fusion.26
  17.3 2.7 while.180
  21.8 5.6 all_gather.60
  28.5 32.4 %all-gather.19.cloned.1.call-done = f32[32,5,15,128]{3,2,1,0:T(8,128)} async-done(((f32[2,5,15,128]{3,2,1,0:T(8,128)}), f32[32,5,15,128]{3,2,1,0:T(8,128)}) %all-gather.19.cloned.1.call-update) | async-done | bytes 1228816 | tf_op jit(solution)/shard_map/all_gather | solution.py:11
  60.9 64.5 %all-gather.17.cloned.1.call-done = f32[32,5,5,15,128]{4,3,2,1,0:T(8,128)} async-done(((f32[2,5,5,15,128]{4,3,2,1,0:T(8,128)}), f32[32,5,5,15,128]{4,3,2,1,0:T(8,128)}) %all-gather.17.cloned.1.call-update) | async-done | bytes 6144016 | tf_op jit(solution)/shard_map/all_gather | solution.py:11
  125.4 32.4 %while.181 = (s32[]{:T(128)}, f32[2,5,15,128]{3,2,1,0:T(8,128)S(1)}, s32[]{:T(128)}, f32[16,2,5,5,15,128]{5,4,3,2,1,0:T(8,128)}, f32[16,2,5,15,128]{4,3,2,1,0:T(8,128)}, /*index=5*/s32[]{:T(128)}, s32[]{:T(128)}) while((s32[]{:T(128)}, f32[2,5,15,128]{3,2,1,0:T(8,128)S(1)}, s32[]{:T(128)}, f32[16,2,5,5,15,128]{5,4,3,2,1,0:T(8,128)}, ...), condition=%wide.region_7.8_spmd.clone, body=%wide.region_5.7_spmd.clone.sunk | while | flops 249604 | bytes 998506 | solution.py:22
  125.4 1.1 fusion.58
  127.4 1.1 fusion.58
  129.5 1.1 fusion.58
  131.5 1.1 fusion.58
  133.5 1.1 fusion.58
  135.5 1.1 fusion.58
  137.6 1.1 fusion.58
  139.6 1.1 fusion.58
  141.6 1.1 fusion.58
  143.7 1.1 fusion.58
  145.7 1.1 fusion.58
  147.7 1.1 fusion.58
  149.7 1.1 fusion.58
  151.8 1.1 fusion.58
  153.8 1.1 fusion.58
  155.8 1.1 fusion.58
  158.8 2.7 while.182
  163.2 36.6 %all-gather.23.cloned.1.call-done = f32[32,5,15,128]{3,2,1,0:T(8,128)} async-done(((f32[2,5,15,128]{3,2,1,0:T(8,128)}), f32[32,5,15,128]{3,2,1,0:T(8,128)}) %all-gather.23.cloned.1.call-update) | async-done | bytes 1228816 | tf_op jit(solution)/shard_map/all_gather | solution.py:11
  199.8 64.4 %all-gather.21.cloned.1.call-done = f32[32,5,5,15,128]{4,3,2,1,0:T(8,128)} async-done(((f32[2,5,5,15,128]{4,3,2,1,0:T(8,128)}), f32[32,5,5,15,128]{4,3,2,1,0:T(8,128)}) %all-gather.21.cloned.1.call-update) | async-done | bytes 6144016 | tf_op jit(solution)/shard_map/all_gather | solution.py:11
  264.2 32.6 %while.183 = (s32[]{:T(128)}, f32[2,5,15,128]{3,2,1,0:T(8,128)S(1)}, s32[]{:T(128)}, f32[16,2,5,5,15,128]{5,4,3,2,1,0:T(8,128)}, f32[16,2,5,15,128]{4,3,2,1,0:T(...) while((s32[]{:T(128)}, f32[2,5,15,128]{3,2,1,0:T(8,128)S(1)}, s32[]{:T(128)}, ...), condition=%wide.region_17.19_spmd.clone, body=%wide.region_15.18_spmd.clone.sunk | while | flops 249608 | bytes 998568 | solution.py:22
  297.7 1.5 collective-permute-start.2
  299.8 3.1 collective-permute-done.2
  303.0 1.2 collective-permute-done.3
  305.2 2.7 while.184
  309.7 5.6 all_gather.69
  316.3 29.8 %all-gather.27.cloned.1.call-done = f32[32,5,15,128]{3,2,1,0:T(8,128)} async-done(((f32[2,5,15,128]{3,2,1,0:T(8,128)}), f32[32,5,15,128]{3,2,1,0:T(8,128)}) %all-gather.27.cloned.1.call-update) | async-done | bytes 1228816 | tf_op jit(solution)/shard_map/all_gather | solution.py:11
  346.1 64.4 %all-gather.25.cloned.1.call-done = f32[32,5,5,15,128]{4,3,2,1,0:T(8,128)} async-done(((f32[2,5,5,15,128]{4,3,2,1,0:T(8,128)}), f32[32,5,5,15,128]{4,3,2,1,0:T(8,128)}) %all-gather.25.cloned.1.call-update) | async-done | bytes 6144016 | tf_op jit(solution)/shard_map/all_gather | solution.py:11
  410.5 32.4 %while.185 = (s32[]{:T(128)}, f32[2,5,15,128]{3,2,1,0:T(8,128)S(1)}, s32[]{:T(128)}, f32[16,2,5,5,15,128]{5,4,3,2,1,0:T(8,128)}, f32[16,2,5,15,128]{4,3,2,1,0:T(8,128)}, /*index=5*/s32[]{:T(128)}, s32[]{:T(128)}) while((s32[]{:T(128)}, f32[2,5,15,128]{3,2,1,0:T(8,128)S(1)}, s32[]{:T(128)}, ...), condition=%wide.region_28.30_spmd.clone, body=%wide.region_26.29_spmd.clone.sunk | while | flops 249604 | bytes 998506 | solution.py:22
  410.5 1.1 fusion.62
  414.5 1.1 fusion.62
  416.6 1.1 fusion.62
  420.6 1.1 fusion.62
  426.7 1.1 fusion.62
  430.8 1.1 fusion.62
  432.8 1.1 fusion.62
  443.9 2.7 while.186
  448.3 36.6 %all-gather.31.cloned.1.call-done = f32[32,5,15,128]{3,2,1,0:T(8,128)} async-done(((f32[2,5,15,128]{3,2,1,0:T(8,128)}), f32[32,5,15,128]{3,2,1,0:T(8,128)}) %all-gather.31.cloned.1.call-update) | async-done | bytes 1228816 | tf_op jit(solution)/shard_map/all_gather | solution.py:11
  484.9 64.5 %all-gather.29.cloned.1.call-done = f32[32,5,5,15,128]{4,3,2,1,0:T(8,128)} async-done(((f32[2,5,5,15,128]{4,3,2,1,0:T(8,128)}), f32[32,5,5,15,128]{4,3,2,1,0:T(8,128)}) %all-gather.29.cloned.1.call-update) | async-done | bytes 6144016 | tf_op jit(solution)/shard_map/all_gather | solution.py:11
  549.4 32.5 %while.187 = (s32[]{:T(128)}, f32[2,5,15,128]{3,2,1,0:T(8,128)S(1)}, s32[]{:T(128)}, f32[16,2,5,5,15,128]{5,4,3,2,1,0:T(8,128)}, f32[16,2,5,15,128]{4,3,2,1,0:T(...) while((s32[]{:T(128)}, f32[2,5,15,128]{3,2,1,0:T(8,128)S(1)}, s32[]{:T(128)}, ...), condition=%wide.region_38.40_spmd.clone, body=%wide.region_36.39_spmd.clone.sunk | while | flops 249608 | bytes 998568 | solution.py:22
  (335 shorter events, 133.9 us)
Async XLA Ops:
  6.5 8.5 %copy-start = (f32[15,15]{1,0:T(8,128)S(1)}, f32[15,15]{1,0:T(8,128)}, u32[]{:S(2)}) copy-start(f32[15,15]{1,0:T(8,128)} %param.36) | copy-start | bytes 2704
  6.5 9.8 %copy-start.1 = (bf16[2,2,5,5,15,128]{5,1,4,3,2,0:T(2,128)(2,1)S(1)}, bf16[2,2,5,5,15,128]{5,1,4,3,2,0:T(2,128)(2,1)}, u32[]{:S(2)}) copy-start(bf16[2,2,5,5,15,128]{5,1,4,3,2,0:T(2,128)(2,1)} %param.34) | copy-start | bytes 1152004
  6.5 54.3 %all-gather.19.cloned.1.call-start = ((), (), s32[]{:S(2)}) async-start(), calls=%async_computation.1 | async-start | bytes 1392640 | tf_op jit(solution)/shard_map/all_gather | solution.py:11
  7.5 5.8 collective-permute-start
  10.6 4.4 collective-permute-start.1
  17.2 4.4 slice-start
  20.0 7.4 %copy-start.4 = (s32[256]{0:T(256)S(1)}, s32[256]{0:T(256)}, u32[]{:S(2)}) copy-start(s32[256]{0:T(256)} %param.37) | copy-start | bytes 3076
  20.7 104.7 %all-gather.17.cloned.1.call-start = ((), (), s32[]{:S(2)}) async-start(), calls=%async_computation | async-start | bytes 6963200 | tf_op jit(solution)/shard_map/all_gather | solution.py:11
  21.6 178.3 %all-gather.23.cloned.1.call-start = ((), (), s32[]{:S(2)}) async-start(), calls=%async_computation.3 | async-start | bytes 1392640 | tf_op jit(solution)/shard_map/all_gather | solution.py:11
  162.3 101.9 %all-gather.21.cloned.1.call-start = ((), (), s32[]{:S(2)}) async-start(), calls=%async_computation.2 | async-start | bytes 6963200 | tf_op jit(solution)/shard_map/all_gather | solution.py:11
  163.2 182.9 %all-gather.27.cloned.1.call-start = ((), (), s32[]{:S(2)}) async-start(), calls=%async_computation.5 | async-start | bytes 1392640 | tf_op jit(solution)/shard_map/all_gather | solution.py:11
  296.9 7.3 %copy-start.2 = (f32[2,2,5,15,128]{4,1,3,2,0:T(2,128)S(1)}, f32[2,2,5,15,128]{4,1,3,2,0:T(2,128)}, u32[]{:S(2)}) copy-start(f32[2,2,5,15,128]{4,1,3,2,0:T(2,128)} %param.32) | copy-start | bytes 460804
  297.7 5.2 collective-permute-start.2
  299.3 4.9 collective-permute-start.3
  308.6 101.9 %all-gather.25.cloned.1.call-start = ((), (), s32[]{:S(2)}) async-start(), calls=%async_computation.4 | async-start | bytes 6963200 | tf_op jit(solution)/shard_map/all_gather | solution.py:11
  309.4 175.4 %all-gather.31.cloned.1.call-start = ((), (), s32[]{:S(2)}) async-start(), calls=%async_computation.7 | async-start | bytes 1392640 | tf_op jit(solution)/shard_map/all_gather | solution.py:11
  447.4 102.0 %all-gather.29.cloned.1.call-start = ((), (), s32[]{:S(2)}) async-start(), calls=%async_computation.6 | async-start | bytes 6963200 | tf_op jit(solution)/shard_map/all_gather | solution.py:11
  582.8 0.7 copy-start.3
Sparse Core Ops, SparseCore 0:
  20.8 40.0 all-gather.18
  63.1 62.2 all-gather.16
  162.4 37.3 all-gather.22
  201.9 62.2 all-gather.20
  308.7 37.3 all-gather.26
  348.2 62.2 all-gather.24
  447.5 37.3 all-gather.30
  487.2 62.2 all-gather.28
where the time goes:
time: 596 us; the launch traced here: 590 us
  waiting for transfers between devices  401 us (67%)
  other arithmetic  146 us (24%)
  between operations  14 us (2%)
  blocking collectives  11.3 us (2%)
  local copies, waits for them, and re-layouts  7.46 us (1%)
    all_gather x8, waiting for transfers between devices, entering(): everything = jax.tree.map(lambda part: lax.all_gather(part, axis), x)  393 us
    reduce_sum x72, other arithmetic, mat_apply(): return jnp.sum(matrix * vector[:, None], axis=2)  69.5 us
    select_n x64, other arithmetic, step(): return jax.tree.map(lambda a, b: jnp.where(reached, a, b), new, before)  59.5 us
  transfers between devices with their start and end apart: 12, of which 12 were waited for; matrix products, arithmetic and copies ran while one was open for 1% of the time, Pallas kernels for 0%

commit v1 on v0

v1 whole, which is shorter than its diff:
```python
import functools

import jax
import jax.numpy as jnp
from jax import lax
from jax.experimental import pallas as pl
from jax.experimental.pallas import tpu as pltpu
from jax.sharding import PartitionSpec as P

F = 5
HP = 16
LANES = 128
LOWER, UPPER, SIDE, SOURCE, RIGHT, ITEMS = 25, 26, 27, 28, 33, 38
HIGHEST = lax.Precision.HIGHEST


def params():
    return pltpu.CompilerParams(vmem_limit_bytes=48 * 2**20)


def matvec(matrix, vector):
    out = []
    for f in range(F):
        terms = [matrix(f * F + g) * vector[g] for g in range(F)]
        out.append((terms[0] + terms[1]) + (terms[2] + terms[3]) + terms[4])
    return out


def pack_kernel(
    n, azim, source, prev, left, right, diag, coupling, spectral, face, *rest
):
    facing, (out, cells, turned, mix, prod) = rest[:azim], rest[azim:]
    planes, rows, _, inst, _ = source.shape
    mine = lax.axis_index("azim")
    part = LANES // n
    per_row = LANES // part
    halves = HP // per_row
    count = rows * planes * ITEMS
    cells[:, HP - 1, :] = jnp.zeros((count, LANES), jnp.float32)
    mix[...] = jnp.zeros_like(mix)
    mix[0:inst, 0:inst] = spectral[...]
    prod[HP - 1 :, :] = jnp.zeros((1, prod.shape[1]), jnp.float32)
    for a in range(planes):
        for j in range(rows):
            for f in range(F):
                at = ((a * rows + j) * F + f) * LANES
                prod[0:inst, at : at + LANES] = prev[a, j, f]
    prod[...] = jnp.dot(mix[...], prod[...], precision=HIGHEST, preferred_element_type=jnp.float32)
    picked = []
    for j in range(rows):
        cell = jnp.broadcast_to(face[j : j + 1, :], (inst, LANES))
        accs = [jnp.zeros((inst, LANES), jnp.float32)] * F
        for k in range(azim):
            origin = lax.rem(mine - k + azim, azim) * rows
            for p in range(rows):
                here = lax.shift_right_logical(cell, 7) == origin + p
                accs = [
                    jnp.where(here, jnp.take_along_axis(facing[k][p, f], cell & 127, axis=1), accs[f])
                    for f in range(F)
                ]
        picked.append(accs)
    for j in range(rows):
        for a in range(planes):
            base = (j * planes + a) * ITEMS
            for f in range(F):
                for g in range(F):
                    cells[base + f * F + g, 0:inst, :] = diag[a, j, f, g].astype(jnp.float32)
            for k in range(3):
                cells[base + LOWER + k, 0:inst, :] = coupling[k, a, j]
            side = coupling[2, a, j]
            for f in range(F):
                at = ((a * rows + j) * F + f) * LANES
                lower = left[a, f] if j == 0 else prev[a, j - 1, f]
                upper = right[a, f] if j == rows - 1 else prev[a, j + 1, f]
                value = source[a, j, f] + side * (lower + upper) - prod[0:inst, at : at + LANES]
                if a == planes - 1:
                    value = value - coupling[1, a, j] * picked[j][f]
                cells[base + SOURCE + f, 0:inst, :] = source[a, j, f]
                cells[base + RIGHT + f, 0:inst, :] = value
    flat = cells.reshape(count * HP, LANES)
    for h in range(HP):
        block = flat[pl.ds(h, count, stride=HP), :].T
        for d in range(n):
            turned[d, h // per_row, (h % per_row) * part : (h % per_row + 1) * part, :] = block[
                d * part : (d + 1) * part
            ]
    for d in range(n):
        for half in range(halves):
            block = turned[d, half].T
            for j in range(rows):
                out[d, j, half] = block[j * planes * ITEMS : (j + 1) * planes * ITEMS]


def reader(lines, group, planes):
    step = planes * ITEMS

    def read(a, k):
        return lines[pl.ds((a // planes) * group * step + (a % planes) * ITEMS + k, group, stride=step), :]

    return read


def sweep(read, right, last, group, fronts, emit):
    carried = [jnp.zeros((group, LANES), jnp.float32)] * F
    for a in range(last):
        lower = read(a, LOWER)
        vector = right(a)
        if a:
            vector = [vector[g] + lower * carried[g] for g in range(F)]
        carried = matvec(functools.partial(read, a), vector)
        if a < last - 1:
            for f in range(F):
                fronts[a, f] = carried[f]
    emit(last - 1, carried)
    for a in reversed(range(last - 1)):
        upper = read(a, UPPER)
        applied = matvec(functools.partial(read, a), carried)
        carried = [fronts[a, f] - upper * applied[f] for f in range(F)]
        emit(a, carried)


def first_kernel(planes, group, halves, lines, out, swapped, fronts):
    read = reader(lines, group, planes)
    last = lines.shape[0] // (group * planes * ITEMS) * planes

    def emit(a, values):
        for f in range(F):
            at = (a * F + f) * group
            out[at : at + group, :] = values[f]
            swapped[at : at + halves, :] = values[f][halves:]
            swapped[at + halves : at + group, :] = values[f][:halves]

    sweep(read, lambda a: [read(a, RIGHT + f) for f in range(F)], last, group, fronts, emit)


def second_kernel(
    planes, group, halves, part, azim, lines, value, swapped, from_left, from_right, spectral, face,
    crossed, partner, out, fronts, mix, spread, prod,
):
    read = reader(lines, group, planes)
    last = lines.shape[0] // (group * planes * ITEMS) * planes
    inst = spectral.shape[0]
    wide = halves * LANES
    mix[...] = jnp.zeros_like(mix)
    mix[0:inst, 0:inst] = spectral[...]
    lane = lax.broadcasted_iota(jnp.int32, (HP, wide), 1)
    instance = lax.broadcasted_iota(jnp.int32, (HP, wide), 0)
    shift = part.bit_length() - 1
    chosen = jnp.where(lax.shift_right_logical(lane, shift) == instance, 1.0, 0.0)
    over = lax.dot_general(
        mix[...], chosen, (((0,), (0,)), ((), ())), precision=HIGHEST, preferred_element_type=jnp.float32
    )
    over = lax.dot_general(
        chosen, over, (((0,), (0,)), ((), ())), precision=HIGHEST, preferred_element_type=jnp.float32
    )
    same = (lax.broadcasted_iota(jnp.int32, (wide, wide), 0) & (part - 1)) == (
        lax.broadcasted_iota(jnp.int32, (wide, wide), 1) & (part - 1)
    )
    spread[...] = jnp.where(same, over, 0.0)
    count = value.shape[0] // halves
    whole = jnp.concatenate(
        [value[pl.ds(half, count, stride=halves), :] for half in range(halves)], axis=1
    )
    mixed = jnp.dot(whole, spread[...], precision=HIGHEST, preferred_element_type=jnp.float32)
    for half in range(halves):
        prod[pl.ds(half, count, stride=halves), :] = mixed[:, half * LANES : (half + 1) * LANES]
    rows = group // halves
    count = F * group
    mine, axial = lax.axis_index("azim"), lax.axis_index("axial")
    owners = last // planes
    me = lax.rem(axial, owners)
    chip, core = lax.shift_right_logical(me, 1), me & 1
    lane_at = lax.broadcasted_iota(jnp.int32, (count, LANES), 1)
    row_cell = lax.broadcasted_iota(jnp.int32, (F, rows, halves, LANES), 1).reshape(count, LANES)
    cells, accs = [], []
    for j in range(rows):
        own = jnp.broadcast_to(face[j : j + 1, :], (count, LANES))
        cell = jnp.take_along_axis(own, me * part + (lane_at & (part - 1)), axis=1)
        cells.append((lax.shift_right_logical(cell, shift) - row_cell * owners, (lane_at & (LANES - part)) + (cell & (part - 1))))
        accs.append(jnp.zeros((count, LANES), jnp.float32))
    for side, buffer in enumerate((crossed, partner)):
        sender = core ^ side
        for k in range(buffer.shape[0]):
            for q in range(2):
                for i in range(azim):
                    owner = (chip ^ (2 * k + sender)) * 2 + (sender ^ q)
                    block = lax.rem(mine - i + azim, azim) * (rows * owners) + owner
                    values = buffer[k, q, i]
                    for j in range(rows):
                        accs[j] = jnp.where(
                            cells[j][0] == block, jnp.take_along_axis(values, cells[j][1], axis=1), accs[j]
                        )
    picked = [
        [
            sum(accs[j][(f * rows + p) * halves : (f * rows + p + 1) * halves] for p in range(rows))
            for f in range(F)
        ]
        for j in range(rows)
    ]
    first = lax.broadcasted_iota(jnp.int32, (group, LANES), 0) < halves

    def right(a):
        side = read(a, SIDE)
        result = []
        for f in range(F):
            at = (a * F + f) * group
            halo = jnp.where(first, from_left[at : at + group, :], from_right[at : at + group, :])
            around = swapped[at : at + group, :] + halo
            entry = read(a, SOURCE + f) + side * around - prod[at : at + group, :]
            if a == last - 1:
                face_rows = jnp.concatenate([picked[j][f] for j in range(rows)], axis=0)
                entry = entry - read(a, UPPER) * face_rows
            result.append(entry)
        return result

    def emit(a, values):
        for f in range(F):
            at = (a * F + f) * group
            out[at : at + group, :] = values[f]

    sweep(read, right, last, group, fronts, emit)


def unpack_kernel(halves, part, value, out, turned):
    n, count, _ = value.shape
    planes, rows, _, inst, _ = out.shape
    per_row = LANES // part
    for d in range(n):
        block = value[d].T
        for h8 in range(per_row):
            turned[h8, d * part : (d + 1) * part, :] = block[h8 * part : (h8 + 1) * part]
    for h8 in range(per_row):
        block = turned[h8].T
        for a in range(planes):
            for f in range(F):
                for j in range(rows):
                    for half in range(halves):
                        h = half * per_row + h8
                        at = ((a * F + f) * rows + j) * halves + half
                        if h < inst:
                            out[a, j, f, h : h + 1, :] = block[at : at + 1]


def shards(adjoint_source, adjoint_prev, diag_inverse, coupling, spectral, face_map):
    n, azim = lax.axis_size("axial") // 2, lax.axis_size("azim")
    planes, rows, _, inst, radial = adjoint_source.shape
    part = radial // n
    halves = HP * part // LANES
    group = rows * halves
    axial = [list(range(n)), list(range(n, 2 * n))]
    both = ("axial", "azim")
    f32 = jnp.float32
    last = n * planes

    def around(up, down):
        forward = [(i, (i + 1) % azim) for i in range(azim)]
        backward = [((i + 1) % azim, i) for i in range(azim)]
        if azim == 2 and up is down:
            got = lax.ppermute(up, "azim", forward)
            return got, got
        return lax.ppermute(up, "azim", forward), lax.ppermute(down, "azim", backward)

    face = face_map.reshape(rows, radial)
    if azim == 2:
        other, _ = around(adjoint_prev, adjoint_prev)
        left, right = other[:, rows - 1], other[:, 0]
    else:
        left, right = around(adjoint_prev[:, rows - 1], adjoint_prev[:, 0])
    facing = [
        lax.ppermute(
            adjoint_prev[0],
            both,
            [(n * azim + y, (n - 1) * azim + (y + k) % azim) for y in range(azim)],
        )
        for k in range(azim)
    ]
    count = rows * planes * ITEMS
    packed = pl.pallas_call(
        functools.partial(pack_kernel, n, azim),
        out_shape=jax.ShapeDtypeStruct((n, rows, halves, planes * ITEMS, LANES), f32),
        scratch_shapes=[
            pltpu.VMEM((count, HP, LANES), f32),
            pltpu.VMEM((n, halves, LANES, count), f32),
            pltpu.VMEM((HP, HP), f32),
            pltpu.VMEM((HP, planes * rows * F * LANES), f32),
        ],
        compiler_params=params(),
        name="pack",
    )(adjoint_source, adjoint_prev, left, right, diag_inverse, coupling, spectral, face, *facing)
    lines = lax.all_to_all(packed, "axial", 0, 0, axis_index_groups=axial, tiled=True)
    lines = lines.reshape(n * group * planes * ITEMS, LANES)
    shape = jax.ShapeDtypeStruct((last * F * group, LANES), f32)
    scratch = pltpu.VMEM((last, F, group, LANES), f32)
    value, swapped = pl.pallas_call(
        functools.partial(first_kernel, planes, group, halves),
        out_shape=(shape, shape),
        scratch_shapes=[scratch],
        compiler_params=params(),
        name="first_sweep",
    )(lines)
    from_left, from_right = around(swapped, swapped)
    piece = value[: F * group]
    pieces = [piece] + [
        lax.ppermute(piece, "azim", [(y, (y + k) % azim) for y in range(azim)]) for k in range(1, azim)
    ]
    piece = jnp.stack(pieces)
    core = [(i, i ^ 1) for i in range(2 * n)]
    chip = jnp.stack([piece, lax.ppermute(piece, "axial", core)])
    chips = n // 2
    crossed = jnp.stack(
        [
            lax.ppermute(
                chip,
                "axial",
                [(n + 2 * c + b, 2 * (c ^ (2 * k + b)) + b) for c in range(chips) for b in range(2)],
            )
            for k in range(chips // 2)
        ]
    )
    partner = lax.ppermute(crossed, "axial", core)
    value = pl.pallas_call(
        functools.partial(second_kernel, planes, group, halves, part, azim),
        out_shape=shape,
        scratch_shapes=[
            scratch,
            pltpu.VMEM((HP, HP), f32),
            pltpu.VMEM((halves * LANES, halves * LANES), f32),
            pltpu.VMEM((last * F * group, LANES), f32),
        ],
        compiler_params=params(),
        name="second_sweep",
    )(lines, value, swapped, from_left, from_right, spectral, face, crossed, partner)
    value = lax.all_to_all(
        value.reshape(n, planes * F * group, LANES), "axial", 0, 0, axis_index_groups=axial, tiled=True
    )
    return pl.pallas_call(
        functools.partial(unpack_kernel, halves, part),
        out_shape=jax.ShapeDtypeStruct(adjoint_source.shape, f32),
        scratch_shapes=[pltpu.VMEM((LANES // part, LANES, planes * F * group), f32)],
        compiler_params=params(),
        name="unpack",
    )(value)


def solution(mesh):
    placed = (
        P("axial", "azim", None, None, None),
        P("axial", "azim", None, None, None),
        P("axial", "azim", None, None, None, None),
        P(None, "axial", "azim", None, None),
        P(),
        P("azim"),
    )
    return jax.shard_map(
        shards,
        mesh=mesh,
        in_specs=placed,
        out_specs=P("axial", "azim", None, None, None),
        check_vma=False,
    )
```

time: 596 us -> 62.7 us (0.11)
  waiting for transfers between devices: 401 us -> 10.7 us
  other arithmetic: 146 us -> 0.02 us
  blocking collectives: 11.3 us -> 32.3 us
  between operations: 14 us -> 0.19 us
    all_gather x8 -> x0, waiting for transfers between devices: 393 us -> none  [entering(): everything = jax.tree.map(lambda part: lax.all_gather(part, axis), x)]
    reduce_sum x90 -> x0, other arithmetic: 80.1 us -> none  [the longest x72 69.5 us: mat_apply(): return jnp.sum(matrix * vector[:, None], axis=2)]
    select_n x75 -> x0, other arithmetic: 64.3 us -> none  [the longest x64 59.5 us: step(): return jax.tree.map(lambda a, b: jnp.where(reached, a, b), new, before)]
    all_to_all x0 -> x2, blocking collectives: none -> 32.3 us  [the longest x1 24.4 us: shards(): lax.all_to_all(packed, 'axial', 0, 0, axis_index_groups=axial, tiled=True)]
    all_gather x2 -> x0, blocking collectives: 11.3 us -> none  [shards(): gathered = lax.all_gather(plane_flat, 'azim', axis=1, tiled=True)]
  transfers between devices with their start and end apart: 12 -> 9, of which waited for: 12 -> 5; matrix products, arithmetic and copies ran while one was open for 1% -> 5% of each run, Pallas kernels for 0% -> 0%
where the time goes in v1:
time: 62.7 us; the launch traced here: 62.4 us
  blocking collectives  32.3 us (52%)
  waiting for transfers between devices  10.7 us (17%)
  starting transfers between devices  10.2 us (16%)
  local copies, waits for them, and re-layouts  5.44 us (9%)
  Pallas kernels  3.57 us (6%)
    all_to_all x1, blocking collectives, shards(): lax.all_to_all(packed, 'axial', 0, 0, axis_index_groups=axial, tiled=True)  24.4 us
    all_to_all x1, blocking collectives, shards(): lax.all_to_all(value.reshape(n, planes * F * group, LANES), 'axial', 0, 0...  7.84 us
    ppermute x2, waiting for transfers between devices, shards(): lax.ppermute(chip, 'axial', [(n + 2 * c + b, 2 * (c ^ 2 * k + b) + b) for...  6.06 us
    ppermute x2, starting transfers between devices, around(): got = lax.ppermute(up, 'azim', forward)  4.57 us
    unnamed x11, local copies, waits for them, and re-layouts  3.81 us
    ppermute x2, starting transfers between devices, shards(): lax.ppermute(chip, 'axial', [(n + 2 * c + b, 2 * (c ^ 2 * k + b) + b) for...  2.57 us
    ppermute x1, waiting for transfers between devices, shards(): lax.ppermute(piece, 'azim', [(y, (y + k) % azim) for y in range(azim)])  2.23 us
    ppermute x1, starting transfers between devices, shards(): lax.ppermute(piece, 'azim', [(y, (y + k) % azim) for y in range(azim)])  1.53 us
  transfers between devices with their start and end apart: 9, of which 5 were waited for; matrix products, arithmetic and copies ran while one was open for 5% of the time, Pallas kernels for 0%

profile of v1, /device:TPU:0, one launch (start us, length us, event | category | flops | bytes accessed | tf_op | source)
XLA Modules:
  0.0 62.4 jit_solution(14442104438433153638)
XLA Ops:
  0.0 0.0 copy-start.2
  0.0 0.0 copy-start
  0.0 0.0 copy-start.1
  0.0 1.0 %copy.21 = f32[2,2,5,15,128]{4,3,2,0,1:T(8,128)S(1)} copy(f32[2,2,5,15,128]{4,1,3,2,0:T(2,128)} %param.7) | data formatting | bytes 307200 | tf_op args[1]
  1.0 3.0 %collective-permute-start = (f32[2,2,5,15,128]{4,3,2,0,1:T(8,128)S(1)}, f32[2,2,5,15,128]{4,3,2,0,1:T(8,128)S(1)}, u32[]{:S(2)}, u32[]{:S(2)}) collective-permute-start(f32[2,2,5,15,128]{4,3,2,0,1:T(8,128)S(1)} %copy.21), channel_id=1, source_target_pairs={{0,1},{1,0},{2,3},{3,2},{4,5},{5,4},{6,7},{7,6},{8,9},{9,8},{10,11... | collective-permute-start | bytes 460808 | tf_op jit(solution)/shard_map/ppermute | solution.py:259
  4.0 0.9 %copy.24.prev = f32[2,2,5,15,128]{4,3,2,1,0:T(8,128)S(1)} copy(f32[2,2,5,15,128]{4,1,3,2,0:T(2,128)} %param.7) | data formatting | bytes 307200 | tf_op args[1]
  5.0 0.7 %collective-permute-start.2 = (f32[2,5,15,128]{3,2,1,0:T(8,128)S(1)}, f32[2,5,15,128]{3,2,1,0:T(8,128)S(1)}, u32[]{:S(2)}, u32[]{:S(2)}) collective-permute-start(f32[2,5,15,128]{3,2,1,0:T(8,128)S(1)} %slice_bitcast_fusion), channel_id=1, source_target_pairs={{16,15},{17,14}} | collective-permute-start | bytes 230408 | tf_op jit(solution)/shard_map/ppermute | solution.py:270
  5.6 0.7 %collective-permute-start.1 = (f32[2,5,15,128]{3,2,1,0:T(8,128)S(1)}, f32[2,5,15,128]{3,2,1,0:T(8,128)S(1)}, u32[]{:S(2)}, u32[]{:S(2)}) collective-permute-start(f32[2,5,15,128]{3,2,1,0:T(8,128)S(1)} %slice_bitcast_fusion), channel_id=1, source_target_pairs={{16,14},{17,15}} | collective-permute-start | bytes 230408 | tf_op jit(solution)/shard_map/ppermute | solution.py:270
  6.3 0.9 %copy.26.coupling = f32[3,2,2,15,128]{4,3,2,1,0:T(8,128)S(1)} copy(f32[3,2,2,15,128]{4,2,3,1,0:T(2,128)} %param.9) | data formatting | bytes 184320 | tf_op args[3]
  7.2 0.9 %copy.23.source = f32[2,2,5,15,128]{4,3,2,1,0:T(8,128)S(1)} copy(f32[2,2,5,15,128]{4,1,3,2,0:T(2,128)} %param.6) | data formatting | bytes 307200 | tf_op args[0]
  8.2 0.0 copy-done.2
  8.2 0.1 copy.25.diag
  8.2 0.0 collective-permute-done
  8.3 0.0 collective-permute-done.2.rest_1_
  8.3 0.0 collective-permute-done.1.rest_0_
  8.3 0.0 copy-done
  8.3 0.0 copy-done.1
  8.3 1.5 %pack.1 = f32[8,2,2,76,128]{4,3,2,1,0:T(8,128)S(1)} custom-call(f32[2,2,5,15,128]{4,3,2,1,0:T(8,128)S(1)} %copy.23.source, f32[2,2,5,15,128]{4,3,2,1,0:T(8,128)S(1)} %copy.24.prev, f32[2,5,15,128]{3,2,1,0:T(8,128)S(1)} %get-tuple-element.12.left, f32[2,5,15,128]{3,2,1,0:T(8,128)S(1)} %get-tuple-element.11.right, ...), custom_call_target="tpu_custom_call" | custom-call | tf_op jit(solution)/shard_map/pack/pallas_call | solution.py:278
  9.8 0.6 %copy.27 = f32[8,2,2,76,128]{4,2,3,1,0:T(2,128)S(1)} copy(f32[8,2,2,76,128]{4,3,2,1,0:T(8,128)S(1)} %pack.1) | data formatting | bytes 2490368 | tf_op jit(solution)/shard_map/pack/pallas_call | solution.py:278
  10.5 24.4 %all_to_all.10 = f32[8,2,2,76,128]{4,2,3,1,0:T(2,128)S(1)} all-to-all(f32[8,2,2,76,128]{4,2,3,1,0:T(2,128)S(1)} %copy.27), channel_id=1, replica_groups={{0,2,4,6,8,10,12,14},{16,18,20,22,24,26,28,30},{1,3,5,7,9,11,13,15},{17..., dimensions={0} | all-to-all | bytes 2490368 | tf_op jit(solution)/shard_map/all_to_all | solution.py:290
  34.9 0.1 copy.28
  35.0 0.1 reshape.10.lines
  35.1 0.3 first_sweep.1
  35.5 1.5 %collective-permute-start.4 = (f32[20,128]{1,0:T(8,128)S(1)}, f32[20,128]{1,0:T(8,128)S(1)}, u32[]{:S(2)}, u32[]{:S(2)}) collective-permute-start(f32[20,128]{1,0:T(8,128)S(1)} %get-tuple-element.10), channel_id=1, source_target_pairs={{0,1},{1,0},{2,3},{3,2},{4,5},{5,4},{6,7},{7,6},{8,9},{9,8},{10,11... | collective-permute-start | bytes 30728 | tf_op jit(solution)/shard_map/ppermute | solution.py:304
  37.0 2.2 %collective-permute-done.4 = f32[20,128]{1,0:T(8,128)S(1)} collective-permute-done((f32[20,128]{1,0:T(8,128)S(1)}, f32[20,128]{1,0:T(8,128)S(1)}, u32[]{:S(2)}, u32[]{:S(2)}) %collective-permute-start.4) | collective-permute-done | bytes 10272 | tf_op jit(solution)/shard_map/ppermute | solution.py:304
  39.2 0.0 collective-permute-start.5
  39.3 1.2 %collective-permute-done.5 = f32[2,20,128]{2,1,0:T(8,128)S(1)} collective-permute-done((f32[2,20,128]{2,1,0:T(8,128)S(1)}, f32[2,20,128]{2,1,0:T(8,128)S(1)}, u32[]{:S(2)}, u32[]{:S(2)}) %collective-permute-start.5) | collective-permute-done | bytes 20512 | tf_op jit(solution)/shard_map/ppermute | solution.py:308
  40.4 1.3 %collective-permute-start.7 = (f32[2,2,20,128]{3,2,1,0:T(8,128)S(1)}, f32[2,2,20,128]{3,2,1,0:T(8,128)S(1)}, u32[]{:S(2)}, u32[]{:S(2)}) collective-permute-start(f32[2,2,20,128]{3,2,1,0:T(8,128)S(1)} %pad_maximum_fusion.1), channel_id=1, source_target_pairs={{16,8},{18,14},{20,12},{22,10},{24,0},{26,6},{28,4},{30,2},{17,9},... | collective-permute-start | bytes 122888 | tf_op jit(solution)/shard_map/ppermute | solution.py:312
  41.7 1.3 %collective-permute-start.6 = (f32[2,2,20,128]{3,2,1,0:T(8,128)S(1)}, f32[2,2,20,128]{3,2,1,0:T(8,128)S(1)}, u32[]{:S(2)}, u32[]{:S(2)}) collective-permute-start(f32[2,2,20,128]{3,2,1,0:T(8,128)S(1)} %pad_maximum_fusion.1), channel_id=1, source_target_pairs={{16,0},{18,6},{20,4},{22,2},{24,8},{26,14},{28,12},{30,10},{17,1},... | collective-permute-start | bytes 122888 | tf_op jit(solution)/shard_map/ppermute | solution.py:312
  43.0 1.5 %collective-permute-start.3 = (f32[320,128]{1,0:T(8,128)S(1)}, f32[320,128]{1,0:T(8,128)S(1)}, u32[]{:S(2)}, u32[]{:S(2)}) collective-permute-start(f32[320,128]{1,0:T(8,128)S(1)} %get-tuple-element.8.swapped), channel_id=1, source_target_pairs={{0,1},{1,0},{2,3},{3,2},{4,5},{5,4},{6,7},{7,6},{8,9},{9,8},{10,11... | collective-permute-start | bytes 491528 | tf_op jit(solution)/shard_map/ppermute | solution.py:259
  44.6 4.0 %collective-permute-done.7 = f32[2,2,20,128]{3,2,1,0:T(8,128)S(1)} collective-permute-done((f32[2,2,20,128]{3,2,1,0:T(8,128)S(1)}, f32[2,2,20,128]{3,2,1,0:T(8,128)S(1)}, u32[]{:S(2)}, u32[]{:S(2)}) %collective-permute-start.7) | collective-permute-done | bytes 40992 | tf_op jit(solution)/shard_map/ppermute | solution.py:312
  48.6 2.0 %collective-permute-done.6 = f32[2,2,20,128]{3,2,1,0:T(8,128)S(1)} collective-permute-done((f32[2,2,20,128]{3,2,1,0:T(8,128)S(1)}, f32[2,2,20,128]{3,2,1,0:T(8,128)S(1)}, u32[]{:S(2)}, u32[]{:S(2)}) %collective-permute-start.6) | collective-permute-done | bytes 40992 | tf_op jit(solution)/shard_map/ppermute | solution.py:312
  50.6 0.2 collective-permute-start.8
  50.8 1.2 %collective-permute-done.8.partner = f32[2,2,2,20,128]{4,3,2,1,0:T(8,128)S(1)} collective-permute-done((f32[2,2,2,20,128]{4,3,2,1,0:T(8,128)S(1)}, f32[2,2,2,20,128]{4,3,2,1,0:T(8,128)S(1)}, u32[]{:S(2)}, u32[]{:S(2)}) %collective-permute-start.8) | collective-permute-done | bytes 81952 | tf_op jit(solution)/shard_map/ppermute | solution.py:320
  52.0 0.0 collective-permute-done.3.from_left.from_right
  52.0 1.4 %second_sweep.1 = f32[320,128]{1,0:T(8,128)S(1)} custom-call(f32[2432,128]{1,0:T(8,128)S(1)} %reshape.10.lines, f32[320,128]{1,0:T(8,128)S(1)} %get-tuple-element.7.value, f32[320,128]{1,0:T(8,128)S(1)} %get-tuple-element.8.swapped, f32[320,128]{1,0:T(8,128)S(1)} %collective-permute-done.3.from_left.from_right, ...), custom_call_target="tpu_custom_call" | custom-call | tf_op jit(solution)/shard_map/second_sweep/pallas_call | solution.py:321
  53.4 7.8 %all_to_all.11.value = f32[8,40,128]{2,1,0:T(8,128)S(1)} all-to-all(f32[8,40,128]{2,1,0:T(8,128)S(1)} %bitcast.16), channel_id=1, replica_groups={{0,2,4,6,8,10,12,14},{16,18,20,22,24,26,28,30},{1,3,5,7,9,11,13,15},{17..., dimensions={0} | all-to-all | bytes 327680 | tf_op jit(solution)/shard_map/all_to_all | solution.py:333
  61.3 0.3 unpack.1
  61.6 0.7 %copy.29 = f32[2,2,5,15,128]{4,1,3,2,0:T(2,128)} copy(f32[2,2,5,15,128]{4,3,2,1,0:T(8,128)S(1)} %unpack.1) | data formatting | bytes 307200 | tf_op jit(solution)/shard_map/unpack/pallas_call | solution.py:336
  (6 shorter events, 0.0 us)
Async XLA Ops:
  0.0 8.2 %copy-start.2 = (bf16[2,2,5,5,15,128]{5,1,4,3,2,0:T(2,128)(2,1)S(1)}, bf16[2,2,5,5,15,128]{5,1,4,3,2,0:T(2,128)(2,1)}, u32[]{:S(2)}) copy-start(bf16[2,2,5,5,15,128]{5,1,4,3,2,0:T(2,128)(2,1)} %param.8) | copy-start | bytes 1152004
  0.0 8.3 %copy-start = (f32[15,15]{1,0:T(8,128)S(1)}, f32[15,15]{1,0:T(8,128)}, u32[]{:S(2)}) copy-start(f32[15,15]{1,0:T(8,128)} %spectral.3) | copy-start | bytes 2704
  0.0 8.3 %copy-start.1 = (s32[256]{0:T(256)S(1)}, s32[256]{0:T(256)}, u32[]{:S(2)}) copy-start(s32[256]{0:T(256)} %param.11) | copy-start | bytes 3076
  1.0 7.3 %collective-permute-start = (f32[2,2,5,15,128]{4,3,2,0,1:T(8,128)S(1)}, f32[2,2,5,15,128]{4,3,2,0,1:T(8,128)S(1)}, u32[]{:S(2)}, u32[]{:S(2)}) collective-permute-start(f32[2,2,5,15,128]{4,3,2,0,1:T(8,128)S(1)} %copy.21), channel_id=1, source_target_pairs={{0,1},{1,0},{2,3},{3,2},{4,5},{5,4},{6,7},{7,6},{8,9},{9,8},{10,11... | collective-permute-start | bytes 460808 | tf_op jit(solution)/shard_map/ppermute | solution.py:259
  5.0 3.3 %collective-permute-start.2 = (f32[2,5,15,128]{3,2,1,0:T(8,128)S(1)}, f32[2,5,15,128]{3,2,1,0:T(8,128)S(1)}, u32[]{:S(2)}, u32[]{:S(2)}) collective-permute-start(f32[2,5,15,128]{3,2,1,0:T(8,128)S(1)} %slice_bitcast_fusion), channel_id=1, source_target_pairs={{16,15},{17,14}} | collective-permute-start | bytes 230408 | tf_op jit(solution)/shard_map/ppermute | solution.py:270
  5.6 2.6 %collective-permute-start.1 = (f32[2,5,15,128]{3,2,1,0:T(8,128)S(1)}, f32[2,5,15,128]{3,2,1,0:T(8,128)S(1)}, u32[]{:S(2)}, u32[]{:S(2)}) collective-permute-start(f32[2,5,15,128]{3,2,1,0:T(8,128)S(1)} %slice_bitcast_fusion), channel_id=1, source_target_pairs={{16,14},{17,15}} | collective-permute-start | bytes 230408 | tf_op jit(solution)/shard_map/ppermute | solution.py:270
  35.5 3.8 %collective-permute-start.4 = (f32[20,128]{1,0:T(8,128)S(1)}, f32[20,128]{1,0:T(8,128)S(1)}, u32[]{:S(2)}, u32[]{:S(2)}) collective-permute-start(f32[20,128]{1,0:T(8,128)S(1)} %get-tuple-element.10), channel_id=1, source_target_pairs={{0,1},{1,0},{2,3},{3,2},{4,5},{5,4},{6,7},{7,6},{8,9},{9,8},{10,11... | collective-permute-start | bytes 30728 | tf_op jit(solution)/shard_map/ppermute | solution.py:304
  39.2 1.2 %collective-permute-start.5 = (f32[2,20,128]{2,1,0:T(8,128)S(1)}, f32[2,20,128]{2,1,0:T(8,128)S(1)}, u32[]{:S(2)}, u32[]{:S(2)}) collective-permute-start(f32[2,20,128]{2,1,0:T(8,128)S(1)} %get-tuple-element.14), channel_id=1, source_target_pairs={{0,2},{2,0},{4,6},{6,4},{8,10},{10,8},{12,14},{14,12},{16,18},{18,... | collective-permute-start | bytes 61448 | tf_op jit(solution)/shard_map/ppermute | solution.py:308
  40.4 8.1 %collective-permute-start.7 = (f32[2,2,20,128]{3,2,1,0:T(8,128)S(1)}, f32[2,2,20,128]{3,2,1,0:T(8,128)S(1)}, u32[]{:S(2)}, u32[]{:S(2)}) collective-permute-start(f32[2,2,20,128]{3,2,1,0:T(8,128)S(1)} %pad_maximum_fusion.1), channel_id=1, source_target_pairs={{16,8},{18,14},{20,12},{22,10},{24,0},{26,6},{28,4},{30,2},{17,9},... | collective-permute-start | bytes 122888 | tf_op jit(solution)/shard_map/ppermute | solution.py:312
  41.7 8.9 %collective-permute-start.6 = (f32[2,2,20,128]{3,2,1,0:T(8,128)S(1)}, f32[2,2,20,128]{3,2,1,0:T(8,128)S(1)}, u32[]{:S(2)}, u32[]{:S(2)}) collective-permute-start(f32[2,2,20,128]{3,2,1,0:T(8,128)S(1)} %pad_maximum_fusion.1), channel_id=1, source_target_pairs={{16,0},{18,6},{20,4},{22,2},{24,8},{26,14},{28,12},{30,10},{17,1},... | collective-permute-start | bytes 122888 | tf_op jit(solution)/shard_map/ppermute | solution.py:312
  43.0 9.0 %collective-permute-start.3 = (f32[320,128]{1,0:T(8,128)S(1)}, f32[320,128]{1,0:T(8,128)S(1)}, u32[]{:S(2)}, u32[]{:S(2)}) collective-permute-start(f32[320,128]{1,0:T(8,128)S(1)} %get-tuple-element.8.swapped), channel_id=1, source_target_pairs={{0,1},{1,0},{2,3},{3,2},{4,5},{5,4},{6,7},{7,6},{8,9},{9,8},{10,11... | collective-permute-start | bytes 491528 | tf_op jit(solution)/shard_map/ppermute | solution.py:259
  50.6 1.4 %collective-permute-start.8 = (f32[2,2,2,20,128]{4,3,2,1,0:T(8,128)S(1)}, f32[2,2,2,20,128]{4,3,2,1,0:T(8,128)S(1)}, u32[]{:S(2)}, u32[]{:S(2)}) collective-permute-start(f32[2,2,2,20,128]{4,3,2,1,0:T(8,128)S(1)} %pad_maximum_fusion.crossed), channel_id=1, source_target_pairs={{0,2},{2,0},{4,6},{6,4},{8,10},{10,8},{12,14},{14,12},{16,18},{18,... | collective-permute-start | bytes 245768 | tf_op jit(solution)/shard_map/ppermute | solution.py:320

commit v2 on v1

--- a/solution.py
+++ b/solution.py
@@ -10,7 +10,7 @@
 F = 5
 HP = 16
 LANES = 128
-LOWER, UPPER, SIDE, SOURCE, RIGHT, ITEMS = 25, 26, 27, 28, 33, 38
+LOWER, UPPER, SIDE, SOURCE, ITEMS = 25, 26, 27, 28, 33
 HIGHEST = lax.Precision.HIGHEST
 
 
@@ -26,17 +26,73 @@
     return out
 
 
-def pack_kernel(
-    n, azim, source, prev, left, right, diag, coupling, spectral, face, *rest
-):
-    facing, (out, cells, turned, mix, prod) = rest[:azim], rest[azim:]
-    planes, rows, _, inst, _ = source.shape
-    mine = lax.axis_index("azim")
+def turn(n, rows, size, cells, turned, emit):
+    me = lax.rem(lax.axis_index("axial"), n)
     part = LANES // n
     per_row = LANES // part
     halves = HP // per_row
-    count = rows * planes * ITEMS
-    cells[:, HP - 1, :] = jnp.zeros((count, LANES), jnp.float32)
+    count = rows * size
+    flat = cells.reshape(count * HP, LANES)
+    for h in range(HP):
+        block = flat[pl.ds(h, count, stride=HP), :].T
+        for d in range(n):
+            turned[d, h // per_row, (h % per_row) * part : (h % per_row + 1) * part, :] = block[
+                d * part : (d + 1) * part
+            ]
+    for k in range(n):
+        for half in range(halves):
+            block = turned[me ^ k, half].T
+            for j in range(rows):
+                at = (j * halves + half) * size
+                emit(k, at, block[j * size : (j + 1) * size])
+
+
+def pack_kernel(n, source_in, prev_in, diag_in, coupling_in, spectral_in, face_in, *rest):
+    outs, (source, prev, coupling, spectral, face) = rest[:n], rest[n : n + 5]
+    cells, turned, diag, sems = rest[n + 5 :]
+    copies = [
+        pltpu.make_async_copy(a, b, sems.at[i])
+        for i, (a, b) in enumerate(
+            (
+                (diag_in, diag),
+                (coupling_in, coupling),
+                (source_in, source),
+                (prev_in, prev),
+                (spectral_in, spectral),
+                (face_in, face),
+            )
+        )
+    ]
+    for copy in copies:
+        copy.start()
+    planes, _, inst, rows, _ = source.shape
+    size = planes * ITEMS
+    cells[:, HP - 1, :] = jnp.zeros((rows * size, LANES), jnp.float32)
+    for copy in copies:
+        copy.wait()
+    for j in range(rows):
+        for a in range(planes):
+            base = (j * planes + a) * ITEMS
+            for f in range(F):
+                for g in range(F):
+                    cells[base + f * F + g, 0:inst, :] = diag[a, f, g, :, j, :].astype(jnp.float32)
+            for k in range(3):
+                cells[base + LOWER + k, 0:inst, :] = coupling[k, a, :, j, :]
+            for f in range(F):
+                cells[base + SOURCE + f, 0:inst, :] = source[a, f, :, j, :]
+
+    def emit(k, at, block):
+        outs[k][at : at + size, :] = block
+
+    turn(n, rows, size, cells, turned, emit)
+
+
+def right_kernel(n, azim, source, prev, left, right, coupling, spectral, face, *rest):
+    facing, outs = rest[:azim], rest[azim + n : azim + 2 * n]
+    cells, turned, mix, prod, held, sems = rest[azim + 2 * n :]
+    planes, _, inst, rows, _ = source.shape
+    mine = lax.axis_index("azim")
+    cells[:, HP - 1, :] = jnp.zeros((rows * planes * F, LANES), jnp.float32)
     mix[...] = jnp.zeros_like(mix)
     mix[0:inst, 0:inst] = spectral[...]
     prod[HP - 1 :, :] = jnp.zeros((1, prod.shape[1]), jnp.float32)
@@ -44,7 +100,7 @@
         for j in range(rows):
             for f in range(F):
                 at = ((a * rows + j) * F + f) * LANES
-                prod[0:inst, at : at + LANES] = prev[a, j, f]
+                prod[0:inst, at : at + LANES] = prev[a, f, :, j, :]
     prod[...] = jnp.dot(mix[...], prod[...], precision=HIGHEST, preferred_element_type=jnp.float32)
     picked = []
     for j in range(rows):
@@ -55,47 +111,44 @@
             for p in range(rows):
                 here = lax.shift_right_logical(cell, 7) == origin + p
                 accs = [
-                    jnp.where(here, jnp.take_along_axis(facing[k][p, f], cell & 127, axis=1), accs[f])
+                    jnp.where(here, jnp.take_along_axis(facing[k][0, f, :, p, :], cell & 127, axis=1), accs[f])
                     for f in range(F)
                 ]
         picked.append(accs)
     for j in range(rows):
         for a in range(planes):
-            base = (j * planes + a) * ITEMS
-            for f in range(F):
-                for g in range(F):
-                    cells[base + f * F + g, 0:inst, :] = diag[a, j, f, g].astype(jnp.float32)
-            for k in range(3):
-                cells[base + LOWER + k, 0:inst, :] = coupling[k, a, j]
-            side = coupling[2, a, j]
+            side = coupling[2, a, :, j, :]
             for f in range(F):
                 at = ((a * rows + j) * F + f) * LANES
-                lower = left[a, f] if j == 0 else prev[a, j - 1, f]
-                upper = right[a, f] if j == rows - 1 else prev[a, j + 1, f]
-                value = source[a, j, f] + side * (lower + upper) - prod[0:inst, at : at + LANES]
+                lower = left[a, f, :, rows - 1, :] if j == 0 else prev[a, f, :, j - 1, :]
+                upper = right[a, f, :, 0, :] if j == rows - 1 else prev[a, f, :, j + 1, :]
+                value = source[a, f, :, j, :] + side * (lower + upper) - prod[0:inst, at : at + LANES]
                 if a == planes - 1:
-                    value = value - coupling[1, a, j] * picked[j][f]
-                cells[base + SOURCE + f, 0:inst, :] = source[a, j, f]
-                cells[base + RIGHT + f, 0:inst, :] = value
-    flat = cells.reshape(count * HP, LANES)
-    for h in range(HP):
-        block = flat[pl.ds(h, count, stride=HP), :].T
-        for d in range(n):
-            turned[d, h // per_row, (h % per_row) * part : (h % per_row + 1) * part, :] = block[
-                d * part : (d + 1) * part
-            ]
-    for d in range(n):
-        for half in range(halves):
-            block = turned[d, half].T
-            for j in range(rows):
-                out[d, j, half] = block[j * planes * ITEMS : (j + 1) * planes * ITEMS]
-
-
-def reader(lines, group, planes):
-    step = planes * ITEMS
+                    value = value - coupling[1, a, :, j, :] * picked[j][f]
+                cells[(j * planes + a) * F + f, 0:inst, :] = value
+    size, count = planes * F, held.shape[1]
+
+    def emit(k, at, block):
+        held[k, at : at + size, :] = block
+
+    turn(n, rows, size, cells, turned, emit)
+    copies = [
+        pltpu.make_async_copy(
+            held.at[k], outs[k].at[pl.ds(outs[k].shape[0] - count, count), :], sems.at[k]
+        )
+        for k in range(n)
+    ]
+    for copy in copies:
+        copy.start()
+    for copy in copies:
+        copy.wait()
+
+
+def reader(lines, group, planes, items):
+    step = planes * items
 
     def read(a, k):
-        return lines[pl.ds((a // planes) * group * step + (a % planes) * ITEMS + k, group, stride=step), :]
+        return lines[pl.ds((a // planes) * group * step + (a % planes) * items + k, group, stride=step), :]
 
     return read
 
@@ -119,9 +172,18 @@
         emit(a, carried)
 
 
-def first_kernel(planes, group, halves, lines, out, swapped, fronts):
-    read = reader(lines, group, planes)
-    last = lines.shape[0] // (group * planes * ITEMS) * planes
+def first_kernel(planes, group, halves, order, *refs):
+    n = len(order)
+    blocks, (lines, out, swapped, right_lines, fronts) = refs[:n], refs[n:]
+    me = lax.rem(lax.axis_index("axial"), n)
+    start = 0
+    for target in (lines, right_lines):
+        size = target.shape[0] // n
+        for k, block in zip(order, blocks):
+            target[pl.ds(pl.multiple_of((me ^ k) * size, 8), size), :] = block[start : start + size]
+        start += size
+    read = reader(lines, group, planes, ITEMS)
+    read_right = reader(right_lines, group, planes, F)
 
     def emit(a, values):
         for f in range(F):
@@ -130,14 +192,14 @@
             swapped[at : at + halves, :] = values[f][halves:]
             swapped[at + halves : at + group, :] = values[f][:halves]
 
-    sweep(read, lambda a: [read(a, RIGHT + f) for f in range(F)], last, group, fronts, emit)
+    sweep(read, lambda a: [read_right(a, f) for f in range(F)], n * planes, group, fronts, emit)
 
 
 def second_kernel(
     planes, group, halves, part, azim, lines, value, swapped, from_left, from_right, spectral, face,
     crossed, partner, out, fronts, mix, spread, prod,
 ):
-    read = reader(lines, group, planes)
+    read = reader(lines, group, planes, ITEMS)
     last = lines.shape[0] // (group * planes * ITEMS) * planes
     inst = spectral.shape[0]
     wide = halves * LANES
@@ -221,29 +283,32 @@
     sweep(read, right, last, group, fronts, emit)
 
 
-def unpack_kernel(halves, part, value, out, turned):
+def unpack_kernel(halves, part, value, out, turned, block):
     n, count, _ = value.shape
-    planes, rows, _, inst, _ = out.shape
+    planes, _, inst, rows, _ = out.shape
     per_row = LANES // part
     for d in range(n):
-        block = value[d].T
+        part_rows = value[d].T
         for h8 in range(per_row):
-            turned[h8, d * part : (d + 1) * part, :] = block[h8 * part : (h8 + 1) * part]
+            turned[h8, d * part : (d + 1) * part, :] = part_rows[h8 * part : (h8 + 1) * part]
     for h8 in range(per_row):
-        block = turned[h8].T
+        block[h8] = turned[h8].T
         for a in range(planes):
             for f in range(F):
-                for j in range(rows):
-                    for half in range(halves):
-                        h = half * per_row + h8
-                        at = ((a * F + f) * rows + j) * halves + half
-                        if h < inst:
-                            out[a, j, f, h : h + 1, :] = block[at : at + 1]
+                for half in range(halves):
+                    h = half * per_row + h8
+                    at = (a * F + f) * rows * halves + half
+                    if h < inst:
+                        out[a, f, h] = block[h8, pl.ds(at, rows, stride=halves), :]
 
 
 def shards(adjoint_source, adjoint_prev, diag_inverse, coupling, spectral, face_map):
     n, azim = lax.axis_size("axial") // 2, lax.axis_size("azim")
     planes, rows, _, inst, radial = adjoint_source.shape
+    source = adjoint_source.transpose(0, 2, 3, 1, 4)
+    prev = adjoint_prev.transpose(0, 2, 3, 1, 4)
+    diag = diag_inverse.transpose(0, 2, 3, 4, 1, 5)
+    coupling = coupling.transpose(0, 1, 3, 2, 4)
     part = radial // n
     halves = HP * part // LANES
     group = rows * halves
@@ -255,49 +320,79 @@
     def around(up, down):
         forward = [(i, (i + 1) % azim) for i in range(azim)]
         backward = [((i + 1) % azim, i) for i in range(azim)]
-        if azim == 2 and up is down:
+        if azim == 2:
             got = lax.ppermute(up, "azim", forward)
             return got, got
         return lax.ppermute(up, "azim", forward), lax.ppermute(down, "azim", backward)
 
+    size, count = planes * ITEMS, planes * F
+    hbm, vmem = pl.BlockSpec(memory_space=pltpu.HBM), pl.BlockSpec(memory_space=pltpu.VMEM)
+
+    def like(x, *lead):
+        return jax.ShapeDtypeStruct(lead or x.shape, x.dtype)
+
     face = face_map.reshape(rows, radial)
-    if azim == 2:
-        other, _ = around(adjoint_prev, adjoint_prev)
-        left, right = other[:, rows - 1], other[:, 0]
-    else:
-        left, right = around(adjoint_prev[:, rows - 1], adjoint_prev[:, 0])
+    left, right = around(prev, prev)
     facing = [
         lax.ppermute(
-            adjoint_prev[0],
-            both,
-            [(n * azim + y, (n - 1) * azim + (y + k) % azim) for y in range(azim)],
+            prev, both, [(n * azim + y, (n - 1) * azim + (y + k) % azim) for y in range(azim)]
         )
         for k in range(azim)
     ]
-    count = rows * planes * ITEMS
-    packed = pl.pallas_call(
-        functools.partial(pack_kernel, n, azim),
-        out_shape=jax.ShapeDtypeStruct((n, rows, halves, planes * ITEMS, LANES), f32),
+    size, count = planes * ITEMS, planes * F
+    block = jax.ShapeDtypeStruct((group * (size + count), LANES), f32)
+    hbm, vmem, anywhere = (
+        pl.BlockSpec(memory_space=space) for space in (pltpu.HBM, pltpu.VMEM, pl.ANY)
+    )
+
+    def like(x):
+        return jax.ShapeDtypeStruct(x.shape, x.dtype)
+
+    inputs = (source, prev, diag, coupling, spectral, face)
+    *packed, source, prev, coupling, spectral, face = pl.pallas_call(
+        functools.partial(pack_kernel, n),
+        in_specs=[hbm] * 6,
+        out_shape=[block] * n + [like(x) for x in (source, prev, coupling, spectral, face)],
         scratch_shapes=[
-            pltpu.VMEM((count, HP, LANES), f32),
-            pltpu.VMEM((n, halves, LANES, count), f32),
-            pltpu.VMEM((HP, HP), f32),
-            pltpu.VMEM((HP, planes * rows * F * LANES), f32),
+            pltpu.VMEM((rows * size, HP, LANES), f32),
+            pltpu.VMEM((n, halves, LANES, rows * size), f32),
+            pltpu.VMEM(diag.shape, diag.dtype),
+            pltpu.SemaphoreType.DMA((6,)),
         ],
         compiler_params=params(),
         name="pack",
-    )(adjoint_source, adjoint_prev, left, right, diag_inverse, coupling, spectral, face, *facing)
-    lines = lax.all_to_all(packed, "axial", 0, 0, axis_index_groups=axial, tiled=True)
-    lines = lines.reshape(n * group * planes * ITEMS, LANES)
+    )(*(pltpu.with_memory_space_constraint(x, pltpu.HBM) for x in inputs))
+    packed = pl.pallas_call(
+        functools.partial(right_kernel, n, azim),
+        in_specs=[vmem] * (7 + azim) + [anywhere] * n,
+        out_specs=[anywhere] * n,
+        out_shape=[block] * n,
+        scratch_shapes=[
+            pltpu.VMEM((rows * count, HP, LANES), f32),
+            pltpu.VMEM((n, halves, LANES, rows * count), f32),
+            pltpu.VMEM((HP, HP), f32),
+            pltpu.VMEM((HP, rows * count * LANES), f32),
+            pltpu.VMEM((n, group * count, LANES), f32),
+            pltpu.SemaphoreType.DMA((n,)),
+        ],
+        input_output_aliases={7 + azim + k: k for k in range(n)},
+        compiler_params=params(),
+        name="right_side",
+    )(source, prev, left, right, coupling, spectral, face, *facing, *packed)
+    order = sorted(range(n), key=lambda k: (k & 1, -bin(k & ~1).count("1"), k))
+    blocks = [
+        lax.ppermute(packed[k], "axial", [(i, i ^ k) for i in range(2 * n)]) if k else packed[k]
+        for k in order
+    ]
     shape = jax.ShapeDtypeStruct((last * F * group, LANES), f32)
     scratch = pltpu.VMEM((last, F, group, LANES), f32)
-    value, swapped = pl.pallas_call(
-        functools.partial(first_kernel, planes, group, halves),
-        out_shape=(shape, shape),
-        scratch_shapes=[scratch],
+    lines, value, swapped = pl.pallas_call(
+        functools.partial(first_kernel, planes, group, halves, order),
+        out_shape=(jax.ShapeDtypeStruct((n * group * size, LANES), f32), shape, shape),
+        scratch_shapes=[pltpu.VMEM((n * group * count, LANES), f32), scratch],
         compiler_params=params(),
         name="first_sweep",
-    )(lines)
+    )(*blocks)
     from_left, from_right = around(swapped, swapped)
     piece = value[: F * group]
     pieces = [piece] + [
@@ -333,13 +428,17 @@
     value = lax.all_to_all(
         value.reshape(n, planes * F * group, LANES), "axial", 0, 0, axis_index_groups=axial, tiled=True
     )
-    return pl.pallas_call(
+    out = pl.pallas_call(
         functools.partial(unpack_kernel, halves, part),
-        out_shape=jax.ShapeDtypeStruct(adjoint_source.shape, f32),
-        scratch_shapes=[pltpu.VMEM((LANES // part, LANES, planes * F * group), f32)],
+        out_shape=jax.ShapeDtypeStruct(source.shape, f32),
+        scratch_shapes=[
+            pltpu.VMEM((LANES // part, LANES, planes * F * group), f32),
+            pltpu.VMEM((LANES // part, planes * F * group, LANES), f32),
+        ],
         compiler_params=params(),
         name="unpack",
     )(value)
+    return out.transpose(0, 3, 1, 2, 4)
 
 
 def solution(mesh):

time: 62.7 us -> 56.7 us (0.904)
  blocking collectives: 32.3 us -> 7.84 us
  waiting for transfers between devices: 10.7 us -> 21.4 us
  starting transfers between devices: 10.2 us -> 19.4 us
  local copies, waits for them, and re-layouts: 5.44 us -> 0.01 us
  Pallas kernels: 3.57 us -> 7.65 us
    all_to_all x1 -> x0, blocking collectives: 24.4 us -> none  [shards(): lax.all_to_all(packed, 'axial', 0, 0, axis_index_groups=axial, tiled=True)]
    ppermute x2 -> x9, waiting for transfers between devices: 0.01 us -> 11 us  [the longest x7 11 us: shards(): lax.ppermute(packed[k], 'axial', [(i, i ^ k) for i in range(2 * n)])]
    ppermute x2 -> x9, starting transfers between devices: 1.33 us -> 10 us  [the longest x7 8.67 us: shards(): lax.ppermute(packed[k], 'axial', [(i, i ^ k) for i in range(2 * n)])]
    unnamed x11 -> x0, local copies, waits for them, and re-layouts: 3.81 us -> none
    pallas_call x2 -> x3, Pallas kernels: 1.82 us -> 5.23 us  [the longest x1 3.35 us: shards(): pl.pallas_call(functools.partial(pack_kernel, n), in_specs=[hbm] * 6, out...]
    pallas_call x2 -> x0, local copies, waits for them, and re-layouts: 1.39 us -> none  [the longest x1 0.74 us: shards(): pl.pallas_call(functools.partial(unpack_kernel, halves, part), out_shape=...]
    ppermute x2, waiting for transfers between devices: 0.01 us -> 0.81 us  [around(): got = lax.ppermute(up, 'azim', forward)]
    ppermute x2, waiting for transfers between devices: 6.06 us -> 5.3 us  [shards(): lax.ppermute(chip, 'axial', [(n + 2 * c + b, 2 * (c ^ 2 * k + b) + b) for...]
  transfers between devices with their start and end apart: 9 -> 16, of which waited for: 5 -> 10; matrix products, arithmetic and copies ran while one was open for 5% -> 0% of each run, Pallas kernels for 0% -> 6%
where the time goes in v2:
time: 56.7 us; the launch traced here: 56.4 us
  waiting for transfers between devices  21.4 us (38%)
  starting transfers between devices  19.4 us (34%)
  blocking collectives  7.84 us (14%)
  Pallas kernels  7.65 us (13%)
    ppermute x7, waiting for transfers between devices, shards(): lax.ppermute(packed[k], 'axial', [(i, i ^ k) for i in range(2 * n)])  11 us
    ppermute x7, starting transfers between devices, shards(): lax.ppermute(packed[k], 'axial', [(i, i ^ k) for i in range(2 * n)])  8.67 us
    all_to_all x1, blocking collectives, shards(): lax.all_to_all(value.reshape(n, planes * F * group, LANES), 'axial', 0, 0...  7.84 us
    ppermute x2, waiting for transfers between devices, shards(): lax.ppermute(chip, 'axial', [(n + 2 * c + b, 2 * (c ^ 2 * k + b) + b) for...  5.3 us
    ppermute x2, starting transfers between devices, around(): got = lax.ppermute(up, 'azim', forward)  4.62 us
    pallas_call x1, Pallas kernels, shards(): pl.pallas_call(functools.partial(pack_kernel, n), in_specs=[hbm] * 6, out...  3.35 us
    ppermute x2, starting transfers between devices, shards(): lax.ppermute(chip, 'axial', [(n + 2 * c + b, 2 * (c ^ 2 * k + b) + b) for...  2.57 us
    ppermute x1, waiting for transfers between devices, shards(): lax.ppermute(piece, 'azim', [(y, (y + k) % azim) for y in range(azim)])  2.18 us
  transfers between devices with their start and end apart: 16, of which 10 were waited for; matrix products, arithmetic and copies ran while one was open for 0% of the time, Pallas kernels for 6%

profile of v2, /device:TPU:0, one launch (start us, length us, event | category | flops | bytes accessed | tf_op | source)
XLA Modules:
  0.0 56.4 jit_solution(13143047913903158436)
XLA Ops:
  0.0 0.7 %collective-permute-start.2 = (f32[2,5,15,2,128]{4,3,2,1,0:T(2,128)}, f32[2,5,15,2,128]{4,3,2,1,0:T(2,128)S(1)}, u32[]{:S(2)}, u32[]{:S(2)}) collective-permute-start(f32[2,5,15,2,128]{4,3,2,1,0:T(2,128)} %bitcast.18), channel_id=1, source_target_pairs={{16,15},{17,14}} | collective-permute-start | bytes 460808 | tf_op jit(solution)/shard_map/ppermute | solution.py:337
  0.7 0.7 %collective-permute-start.1 = (f32[2,5,15,2,128]{4,3,2,1,0:T(2,128)}, f32[2,5,15,2,128]{4,3,2,1,0:T(2,128)S(1)}, u32[]{:S(2)}, u32[]{:S(2)}) collective-permute-start(f32[2,5,15,2,128]{4,3,2,1,0:T(2,128)} %bitcast.19), channel_id=1, source_target_pairs={{16,14},{17,15}} | collective-permute-start | bytes 460808 | tf_op jit(solution)/shard_map/ppermute | solution.py:337
  1.3 3.0 %collective-permute-start = (f32[2,5,15,2,128]{4,3,2,1,0:T(2,128)}, f32[2,5,15,2,128]{4,3,2,1,0:T(2,128)S(1)}, u32[]{:S(2)}, u32[]{:S(2)}) collective-permute-start(f32[2,5,15,2,128]{4,3,2,1,0:T(2,128)} %bitcast.20), channel_id=1, source_target_pairs={{0,1},{1,0},{2,3},{3,2},{4,5},{5,4},{6,7},{7,6},{8,9},{9,8},{10,11... | collective-permute-start | bytes 460808 | tf_op jit(solution)/shard_map/ppermute | solution.py:324
  4.4 3.4 %pack.1 = (f32[304,128]{1,0:T(8,128)S(1)}, f32[304,128]{1,0:T(8,128)S(1)}, f32[304,128]{1,0:T(8,128)S(1)}, f32[304,128]{1,0:T(8,128)S(1)}, f32[304,128]{1,0:T(8,...) custom-call(f32[2,5,15,2,128]{4,3,2,1,0:T(2,128)} %bitcast.17, ...), custom_call_target="tpu_custom_call" | custom-call | tf_op jit(solution)/shard_map/pack/pallas_call | solution.py:352
  7.7 0.0 collective-permute-done.2.rest_1_
  7.7 0.0 collective-permute-done.1.rest_0_
  7.8 0.8 %collective-permute-done.left.right = f32[2,5,15,2,128]{4,3,2,1,0:T(2,128)S(1)} collective-permute-done((f32[2,5,15,2,128]{4,3,2,1,0:T(2,128)}, f32[2,5,15,2,128]{4,3,2,1,0:T(2,128)S(1)}, u32[]{:S(2)}, u32[]{:S(2)}) %collective-permute-start) | collective-permute-done | bytes 153632 | tf_op jit(solution)/shard_map/ppermute | solution.py:324
  8.6 1.5 %right_side.1 = (f32[304,128]{1,0:T(8,128)S(1)}, f32[304,128]{1,0:T(8,128)S(1)}, f32[304,128]{1,0:T(8,128)S(1)}, f32[304,128]{1,0:T(8,128)S(1)}, f32[304,128]{1,...) custom-call(f32[2,5,15,2,128]{4,3,2,1,0:T(2,128)S(1)} %get-tuple-ele, ...), custom_call_target="tpu_custom_call", output_to_operand_aliasing={{0}: (9, {}), {1}: (10, {}), {2}: (11, {}), {3}: (12, {}), ... | custom-call | tf_op jit(solution)/shard_map/right_side/pallas_call | solution.py:365
  10.0 5.5 %collective-permute-start.3 = (f32[304,128]{1,0:T(8,128)S(1)}, f32[304,128]{1,0:T(8,128)S(1)}, u32[]{:S(2)}, u32[]{:S(2)}) collective-permute-start(f32[304,128]{1,0:T(8,128)S(1)} %get-tuple-element.42), channel_id=1, source_target_pairs={{0,12},{2,14},{4,8},{6,10},{8,4},{10,6},{12,0},{14,2},{16,28},{18,... | collective-permute-start | bytes 466952 | tf_op jit(solution)/shard_map/ppermute | solution.py:384
  15.5 0.0 collective-permute-start.4
  15.5 0.6 %collective-permute-start.5 = (f32[304,128]{1,0:T(8,128)S(1)}, f32[304,128]{1,0:T(8,128)S(1)}, u32[]{:S(2)}, u32[]{:S(2)}) collective-permute-start(f32[304,128]{1,0:T(8,128)S(1)} %get-tuple-element.44), channel_id=1, source_target_pairs={{0,8},{2,10},{4,12},{6,14},{8,0},{10,2},{12,4},{14,6},{16,24},{18,... | collective-permute-start | bytes 466952 | tf_op jit(solution)/shard_map/ppermute | solution.py:384
  16.1 1.7 %collective-permute-start.6 = (f32[304,128]{1,0:T(8,128)S(1)}, f32[304,128]{1,0:T(8,128)S(1)}, u32[]{:S(2)}, u32[]{:S(2)}) collective-permute-start(f32[304,128]{1,0:T(8,128)S(1)} %get-tuple-element.46), channel_id=1, source_target_pairs={{0,14},{2,12},{4,10},{6,8},{8,6},{10,4},{12,2},{14,0},{16,30},{18,... | collective-permute-start | bytes 466952 | tf_op jit(solution)/shard_map/ppermute | solution.py:384
  17.9 0.8 %collective-permute-start.7 = (f32[304,128]{1,0:T(8,128)S(1)}, f32[304,128]{1,0:T(8,128)S(1)}, u32[]{:S(2)}, u32[]{:S(2)}) collective-permute-start(f32[304,128]{1,0:T(8,128)S(1)} %get-tuple-element.47), channel_id=1, source_target_pairs={{0,6},{2,4},{4,2},{6,0},{8,14},{10,12},{12,10},{14,8},{16,22},{18,... | collective-permute-start | bytes 466952 | tf_op jit(solution)/shard_map/ppermute | solution.py:384
  18.7 1.6 %collective-permute-done.3.refs_0_ = f32[304,128]{1,0:T(8,128)S(1)} collective-permute-done((f32[304,128]{1,0:T(8,128)S(1)}, f32[304,128]{1,0:T(8,128)S(1)}, u32[]{:S(2)}, u32[]{:S(2)}) %collective-permute-start.3) | collective-permute-done | bytes 155680 | tf_op jit(solution)/shard_map/ppermute | solution.py:384
  20.3 0.0 collective-permute-start.8
  20.3 3.7 %collective-permute-done.4.refs_1_ = f32[304,128]{1,0:T(8,128)S(1)} collective-permute-done((f32[304,128]{1,0:T(8,128)S(1)}, f32[304,128]{1,0:T(8,128)S(1)}, u32[]{:S(2)}, u32[]{:S(2)}) %collective-permute-start.4) | collective-permute-done | bytes 155680 | tf_op jit(solution)/shard_map/ppermute | solution.py:384
  24.0 0.0 collective-permute-start.9
  24.0 0.0 collective-permute-done.5.refs_2_
  24.0 2.6 %collective-permute-done.6.refs_4_ = f32[304,128]{1,0:T(8,128)S(1)} collective-permute-done((f32[304,128]{1,0:T(8,128)S(1)}, f32[304,128]{1,0:T(8,128)S(1)}, u32[]{:S(2)}, u32[]{:S(2)}) %collective-permute-start.6) | collective-permute-done | bytes 155680 | tf_op jit(solution)/shard_map/ppermute | solution.py:384
  26.6 3.1 %collective-permute-done.7.refs_5_ = f32[304,128]{1,0:T(8,128)S(1)} collective-permute-done((f32[304,128]{1,0:T(8,128)S(1)}, f32[304,128]{1,0:T(8,128)S(1)}, u32[]{:S(2)}, u32[]{:S(2)}) %collective-permute-start.7) | collective-permute-done | bytes 155680 | tf_op jit(solution)/shard_map/ppermute | solution.py:384
  29.7 0.0 collective-permute-done.8.refs_6_
  29.7 0.0 collective-permute-done.9.refs_7_
  29.7 0.4 first_sweep.1
  30.2 1.6 %collective-permute-start.11 = (f32[20,128]{1,0:T(8,128)S(1)}, f32[20,128]{1,0:T(8,128)S(1)}, u32[]{:S(2)}, u32[]{:S(2)}) collective-permute-start(f32[20,128]{1,0:T(8,128)S(1)} %get-tuple-element.54), channel_id=1, source_target_pairs={{0,1},{1,0},{2,3},{3,2},{4,5},{5,4},{6,7},{7,6},{8,9},{9,8},{10,11... | collective-permute-start | bytes 30728 | tf_op jit(solution)/shard_map/ppermute | solution.py:399
  31.7 2.2 %collective-permute-done.11 = f32[20,128]{1,0:T(8,128)S(1)} collective-permute-done((f32[20,128]{1,0:T(8,128)S(1)}, f32[20,128]{1,0:T(8,128)S(1)}, u32[]{:S(2)}, u32[]{:S(2)}) %collective-permute-start.11) | collective-permute-done | bytes 10272 | tf_op jit(solution)/shard_map/ppermute | solution.py:399
  33.9 0.0 collective-permute-start.12
  33.9 1.2 %collective-permute-done.12 = f32[2,20,128]{2,1,0:T(8,128)S(1)} collective-permute-done((f32[2,20,128]{2,1,0:T(8,128)S(1)}, f32[2,20,128]{2,1,0:T(8,128)S(1)}, u32[]{:S(2)}, u32[]{:S(2)}) %collective-permute-start.12) | collective-permute-done | bytes 20512 | tf_op jit(solution)/shard_map/ppermute | solution.py:403
  35.1 1.3 %collective-permute-start.14 = (f32[2,2,20,128]{3,2,1,0:T(8,128)S(1)}, f32[2,2,20,128]{3,2,1,0:T(8,128)S(1)}, u32[]{:S(2)}, u32[]{:S(2)}) collective-permute-start(f32[2,2,20,128]{3,2,1,0:T(8,128)S(1)} %pad_maximum_fusion.1), channel_id=1, source_target_pairs={{16,8},{18,14},{20,12},{22,10},{24,0},{26,6},{28,4},{30,2},{17,9},... | collective-permute-start | bytes 122888 | tf_op jit(solution)/shard_map/ppermute | solution.py:407
  36.4 1.3 %collective-permute-start.13 = (f32[2,2,20,128]{3,2,1,0:T(8,128)S(1)}, f32[2,2,20,128]{3,2,1,0:T(8,128)S(1)}, u32[]{:S(2)}, u32[]{:S(2)}) collective-permute-start(f32[2,2,20,128]{3,2,1,0:T(8,128)S(1)} %pad_maximum_fusion.1), channel_id=1, source_target_pairs={{16,0},{18,6},{20,4},{22,2},{24,8},{26,14},{28,12},{30,10},{17,1},... | collective-permute-start | bytes 122888 | tf_op jit(solution)/shard_map/ppermute | solution.py:407
  37.7 1.6 %collective-permute-start.10 = (f32[320,128]{1,0:T(8,128)S(1)}, f32[320,128]{1,0:T(8,128)S(1)}, u32[]{:S(2)}, u32[]{:S(2)}) collective-permute-start(f32[320,128]{1,0:T(8,128)S(1)} %get-tuple-element.52.swapped), channel_id=1, source_target_pairs={{0,1},{1,0},{2,3},{3,2},{4,5},{5,4},{6,7},{7,6},{8,9},{9,8},{10,11... | collective-permute-start | bytes 491528 | tf_op jit(solution)/shard_map/ppermute | solution.py:324
  39.3 4.1 %collective-permute-done.14 = f32[2,2,20,128]{3,2,1,0:T(8,128)S(1)} collective-permute-done((f32[2,2,20,128]{3,2,1,0:T(8,128)S(1)}, f32[2,2,20,128]{3,2,1,0:T(8,128)S(1)}, u32[]{:S(2)}, u32[]{:S(2)}) %collective-permute-start.14) | collective-permute-done | bytes 40992 | tf_op jit(solution)/shard_map/ppermute | solution.py:407
  43.4 1.2 %collective-permute-done.13 = f32[2,2,20,128]{3,2,1,0:T(8,128)S(1)} collective-permute-done((f32[2,2,20,128]{3,2,1,0:T(8,128)S(1)}, f32[2,2,20,128]{3,2,1,0:T(8,128)S(1)}, u32[]{:S(2)}, u32[]{:S(2)}) %collective-permute-start.13) | collective-permute-done | bytes 40992 | tf_op jit(solution)/shard_map/ppermute | solution.py:407
  44.6 0.6 %collective-permute-start.15 = (f32[2,2,2,20,128]{4,3,2,1,0:T(8,128)S(1)}, f32[2,2,2,20,128]{4,3,2,1,0:T(8,128)S(1)}, u32[]{:S(2)}, u32[]{:S(2)}) collective-permute-start(f32[2,2,2,20,128]{4,3,2,1,0:T(8,128)S(1)} %pad_maximum_fusion.crossed), channel_id=1, source_target_pairs={{0,2},{2,0},{4,6},{6,4},{8,10},{10,8},{12,14},{14,12},{16,18},{18,... | collective-permute-start | bytes 245768 | tf_op jit(solution)/shard_map/ppermute | solution.py:415
  45.2 0.9 %collective-permute-done.15.partner = f32[2,2,2,20,128]{4,3,2,1,0:T(8,128)S(1)} collective-permute-done((f32[2,2,2,20,128]{4,3,2,1,0:T(8,128)S(1)}, f32[2,2,2,20,128]{4,3,2,1,0:T(8,128)S(1)}, u32[]{:S(2)}, u32[]{:S(2)}) %collective-permute-start.15) | collective-permute-done | bytes 81952 | tf_op jit(solution)/shard_map/ppermute | solution.py:415
  46.2 0.0 collective-permute-done.10.from_left.from_right
  46.2 1.4 %second_sweep.1 = f32[320,128]{1,0:T(8,128)S(1)} custom-call(f32[2112,128]{1,0:T(8,128)S(1)} %get-tuple-element.50.lines, f32[320,128]{1,0:T(8,128)S(1)} %get-tuple-element.51.value, f32[320,128]{1,0:T(8,128)S(1)} %get-tuple-element.52.swapped, f32[320,128]{1,0:T(8,128)S(1)} %collective-permute-done.10.from_left.from_right, ...), custom_call_target="tpu_custom_call" | custom-call | tf_op jit(solution)/shard_map/second_sweep/pallas_call | solution.py:416
  47.6 7.8 %all_to_all.5.value = f32[8,40,128]{2,1,0:T(8,128)S(1)} all-to-all(f32[8,40,128]{2,1,0:T(8,128)S(1)} %bitcast.15), channel_id=1, replica_groups={{0,2,4,6,8,10,12,14},{16,18,20,22,24,26,28,30},{1,3,5,7,9,11,13,15},{17..., dimensions={0} | all-to-all | bytes 327680 | tf_op jit(solution)/shard_map/all_to_all | solution.py:428
  55.4 1.0 %unpack.1 = f32[2,5,15,2,128]{4,3,2,1,0:T(2,128)} custom-call(f32[8,40,128]{2,1,0:T(8,128)S(1)} %all_to_all.5.value), custom_call_target="tpu_custom_call" | custom-call | tf_op jit(solution)/shard_map/unpack/pallas_call | solution.py:431
  (4 shorter events, 0.0 us)
Async XLA Ops:
  0.0 7.7 %collective-permute-start.2 = (f32[2,5,15,2,128]{4,3,2,1,0:T(2,128)}, f32[2,5,15,2,128]{4,3,2,1,0:T(2,128)S(1)}, u32[]{:S(2)}, u32[]{:S(2)}) collective-permute-start(f32[2,5,15,2,128]{4,3,2,1,0:T(2,128)} %bitcast.18), channel_id=1, source_target_pairs={{16,15},{17,14}} | collective-permute-start | bytes 460808 | tf_op jit(solution)/shard_map/ppermute | solution.py:337
  0.7 7.1 %collective-permute-start.1 = (f32[2,5,15,2,128]{4,3,2,1,0:T(2,128)}, f32[2,5,15,2,128]{4,3,2,1,0:T(2,128)S(1)}, u32[]{:S(2)}, u32[]{:S(2)}) collective-permute-start(f32[2,5,15,2,128]{4,3,2,1,0:T(2,128)} %bitcast.19), channel_id=1, source_target_pairs={{16,14},{17,15}} | collective-permute-start | bytes 460808 | tf_op jit(solution)/shard_map/ppermute | solution.py:337
  1.3 7.2 %collective-permute-start = (f32[2,5,15,2,128]{4,3,2,1,0:T(2,128)}, f32[2,5,15,2,128]{4,3,2,1,0:T(2,128)S(1)}, u32[]{:S(2)}, u32[]{:S(2)}) collective-permute-start(f32[2,5,15,2,128]{4,3,2,1,0:T(2,128)} %bitcast.20), channel_id=1, source_target_pairs={{0,1},{1,0},{2,3},{3,2},{4,5},{5,4},{6,7},{7,6},{8,9},{9,8},{10,11... | collective-permute-start | bytes 460808 | tf_op jit(solution)/shard_map/ppermute | solution.py:324
  10.0 10.3 %collective-permute-start.3 = (f32[304,128]{1,0:T(8,128)S(1)}, f32[304,128]{1,0:T(8,128)S(1)}, u32[]{:S(2)}, u32[]{:S(2)}) collective-permute-start(f32[304,128]{1,0:T(8,128)S(1)} %get-tuple-element.42), channel_id=1, source_target_pairs={{0,12},{2,14},{4,8},{6,10},{8,4},{10,6},{12,0},{14,2},{16,28},{18,... | collective-permute-start | bytes 466952 | tf_op jit(solution)/shard_map/ppermute | solution.py:384
  15.5 8.5 %collective-permute-start.4 = (f32[304,128]{1,0:T(8,128)S(1)}, f32[304,128]{1,0:T(8,128)S(1)}, u32[]{:S(2)}, u32[]{:S(2)}) collective-permute-start(f32[304,128]{1,0:T(8,128)S(1)} %get-tuple-element.43), channel_id=1, source_target_pairs={{0,4},{2,6},{4,0},{6,2},{8,12},{10,14},{12,8},{14,10},{16,20},{18,... | collective-permute-start | bytes 466952 | tf_op jit(solution)/shard_map/ppermute | solution.py:384
  15.5 8.5 %collective-permute-start.5 = (f32[304,128]{1,0:T(8,128)S(1)}, f32[304,128]{1,0:T(8,128)S(1)}, u32[]{:S(2)}, u32[]{:S(2)}) collective-permute-start(f32[304,128]{1,0:T(8,128)S(1)} %get-tuple-element.44), channel_id=1, source_target_pairs={{0,8},{2,10},{4,12},{6,14},{8,0},{10,2},{12,4},{14,6},{16,24},{18,... | collective-permute-start | bytes 466952 | tf_op jit(solution)/shard_map/ppermute | solution.py:384
  16.1 10.5 %collective-permute-start.6 = (f32[304,128]{1,0:T(8,128)S(1)}, f32[304,128]{1,0:T(8,128)S(1)}, u32[]{:S(2)}, u32[]{:S(2)}) collective-permute-start(f32[304,128]{1,0:T(8,128)S(1)} %get-tuple-element.46), channel_id=1, source_target_pairs={{0,14},{2,12},{4,10},{6,8},{8,6},{10,4},{12,2},{14,0},{16,30},{18,... | collective-permute-start | bytes 466952 | tf_op jit(solution)/shard_map/ppermute | solution.py:384
  17.9 11.8 %collective-permute-start.7 = (f32[304,128]{1,0:T(8,128)S(1)}, f32[304,128]{1,0:T(8,128)S(1)}, u32[]{:S(2)}, u32[]{:S(2)}) collective-permute-start(f32[304,128]{1,0:T(8,128)S(1)} %get-tuple-element.47), channel_id=1, source_target_pairs={{0,6},{2,4},{4,2},{6,0},{8,14},{10,12},{12,10},{14,8},{16,22},{18,... | collective-permute-start | bytes 466952 | tf_op jit(solution)/shard_map/ppermute | solution.py:384
  20.3 9.4 %collective-permute-start.8 = (f32[304,128]{1,0:T(8,128)S(1)}, f32[304,128]{1,0:T(8,128)S(1)}, u32[]{:S(2)}, u32[]{:S(2)}) collective-permute-start(f32[304,128]{1,0:T(8,128)S(1)} %get-tuple-element.48), channel_id=1, source_target_pairs={{0,10},{2,8},{4,14},{6,12},{8,2},{10,0},{12,6},{14,4},{16,26},{18,... | collective-permute-start | bytes 466952 | tf_op jit(solution)/shard_map/ppermute | solution.py:384
  24.0 5.7 %collective-permute-start.9 = (f32[304,128]{1,0:T(8,128)S(1)}, f32[304,128]{1,0:T(8,128)S(1)}, u32[]{:S(2)}, u32[]{:S(2)}) collective-permute-start(f32[304,128]{1,0:T(8,128)S(1)} %get-tuple-element.49), channel_id=1, source_target_pairs={{0,2},{2,0},{4,6},{6,4},{8,10},{10,8},{12,14},{14,12},{16,18},{18,... | collective-permute-start | bytes 466952 | tf_op jit(solution)/shard_map/ppermute | solution.py:384
  30.2 3.8 %collective-permute-start.11 = (f32[20,128]{1,0:T(8,128)S(1)}, f32[20,128]{1,0:T(8,128)S(1)}, u32[]{:S(2)}, u32[]{:S(2)}) collective-permute-start(f32[20,128]{1,0:T(8,128)S(1)} %get-tuple-element.54), channel_id=1, source_target_pairs={{0,1},{1,0},{2,3},{3,2},{4,5},{5,4},{6,7},{7,6},{8,9},{9,8},{10,11... | collective-permute-start | bytes 30728 | tf_op jit(solution)/shard_map/ppermute | solution.py:399
  33.9 1.2 %collective-permute-start.12 = (f32[2,20,128]{2,1,0:T(8,128)S(1)}, f32[2,20,128]{2,1,0:T(8,128)S(1)}, u32[]{:S(2)}, u32[]{:S(2)}) collective-permute-start(f32[2,20,128]{2,1,0:T(8,128)S(1)} %get-tuple-element.56), channel_id=1, source_target_pairs={{0,2},{2,0},{4,6},{6,4},{8,10},{10,8},{12,14},{14,12},{16,18},{18,... | collective-permute-start | bytes 61448 | tf_op jit(solution)/shard_map/ppermute | solution.py:403
  35.1 8.3 %collective-permute-start.14 = (f32[2,2,20,128]{3,2,1,0:T(8,128)S(1)}, f32[2,2,20,128]{3,2,1,0:T(8,128)S(1)}, u32[]{:S(2)}, u32[]{:S(2)}) collective-permute-start(f32[2,2,20,128]{3,2,1,0:T(8,128)S(1)} %pad_maximum_fusion.1), channel_id=1, source_target_pairs={{16,8},{18,14},{20,12},{22,10},{24,0},{26,6},{28,4},{30,2},{17,9},... | collective-permute-start | bytes 122888 | tf_op jit(solution)/shard_map/ppermute | solution.py:407
  36.4 8.2 %collective-permute-start.13 = (f32[2,2,20,128]{3,2,1,0:T(8,128)S(1)}, f32[2,2,20,128]{3,2,1,0:T(8,128)S(1)}, u32[]{:S(2)}, u32[]{:S(2)}) collective-permute-start(f32[2,2,20,128]{3,2,1,0:T(8,128)S(1)} %pad_maximum_fusion.1), channel_id=1, source_target_pairs={{16,0},{18,6},{20,4},{22,2},{24,8},{26,14},{28,12},{30,10},{17,1},... | collective-permute-start | bytes 122888 | tf_op jit(solution)/shard_map/ppermute | solution.py:407
  37.7 8.5 %collective-permute-start.10 = (f32[320,128]{1,0:T(8,128)S(1)}, f32[320,128]{1,0:T(8,128)S(1)}, u32[]{:S(2)}, u32[]{:S(2)}) collective-permute-start(f32[320,128]{1,0:T(8,128)S(1)} %get-tuple-element.52.swapped), channel_id=1, source_target_pairs={{0,1},{1,0},{2,3},{3,2},{4,5},{5,4},{6,7},{7,6},{8,9},{9,8},{10,11... | collective-permute-start | bytes 491528 | tf_op jit(solution)/shard_map/ppermute | solution.py:324
  44.6 1.5 %collective-permute-start.15 = (f32[2,2,2,20,128]{4,3,2,1,0:T(8,128)S(1)}, f32[2,2,2,20,128]{4,3,2,1,0:T(8,128)S(1)}, u32[]{:S(2)}, u32[]{:S(2)}) collective-permute-start(f32[2,2,2,20,128]{4,3,2,1,0:T(8,128)S(1)} %pad_maximum_fusion.crossed), channel_id=1, source_target_pairs={{0,2},{2,0},{4,6},{6,4},{8,10},{10,8},{12,14},{14,12},{16,18},{18,... | collective-permute-start | bytes 245768 | tf_op jit(solution)/shard_map/ppermute | solution.py:415

commit v3 on v2

--- a/solution.py
+++ b/solution.py
@@ -47,85 +47,84 @@
                 emit(k, at, block[j * size : (j + 1) * size])
 
 
-def pack_kernel(n, source_in, prev_in, diag_in, coupling_in, spectral_in, face_in, *rest):
-    outs, (source, prev, coupling, spectral, face) = rest[:n], rest[n : n + 5]
-    cells, turned, diag, sems = rest[n + 5 :]
-    copies = [
-        pltpu.make_async_copy(a, b, sems.at[i])
-        for i, (a, b) in enumerate(
-            (
-                (diag_in, diag),
-                (coupling_in, coupling),
-                (source_in, source),
-                (prev_in, prev),
-                (spectral_in, spectral),
-                (face_in, face),
-            )
-        )
-    ]
+def fetch_kernel(*refs):
+    count = len(refs) // 2
+    sources, targets, sems = refs[: count - 1], refs[count - 1 : -1], refs[-1]
+    pairs = list(zip(sources, targets)) + [(sources[1].at[0], targets[-1])]
+    copies = [pltpu.make_async_copy(a, b, sems.at[i]) for i, (a, b) in enumerate(pairs)]
     for copy in copies:
         copy.start()
+    for copy in copies:
+        copy.wait()
+
+
+def pack_kernel(n, source, prev, diag, coupling, spectral, *rest):
+    outs, base = rest[:n], rest[n]
+    cells, turned, mix, prod = rest[n + 1 :]
     planes, _, inst, rows, _ = source.shape
     size = planes * ITEMS
     cells[:, HP - 1, :] = jnp.zeros((rows * size, LANES), jnp.float32)
-    for copy in copies:
-        copy.wait()
     for j in range(rows):
         for a in range(planes):
-            base = (j * planes + a) * ITEMS
+            start = (j * planes + a) * ITEMS
             for f in range(F):
                 for g in range(F):
-                    cells[base + f * F + g, 0:inst, :] = diag[a, f, g, :, j, :].astype(jnp.float32)
+                    cells[start + f * F + g, 0:inst, :] = diag[a, f, g, :, j, :].astype(jnp.float32)
             for k in range(3):
-                cells[base + LOWER + k, 0:inst, :] = coupling[k, a, :, j, :]
-            for f in range(F):
-                cells[base + SOURCE + f, 0:inst, :] = source[a, f, :, j, :]
-
-    def emit(k, at, block):
-        outs[k][at : at + size, :] = block
-
-    turn(n, rows, size, cells, turned, emit)
-
-
-def right_kernel(n, azim, source, prev, left, right, coupling, spectral, face, *rest):
-    facing, outs = rest[:azim], rest[azim + n : azim + 2 * n]
-    cells, turned, mix, prod, held, sems = rest[azim + 2 * n :]
-    planes, _, inst, rows, _ = source.shape
-    mine = lax.axis_index("azim")
-    cells[:, HP - 1, :] = jnp.zeros((rows * planes * F, LANES), jnp.float32)
+                cells[start + LOWER + k, 0:inst, :] = coupling[k, a, :, j, :]
+            for f in range(F):
+                cells[start + SOURCE + f, 0:inst, :] = source[a, f, :, j, :]
     mix[...] = jnp.zeros_like(mix)
     mix[0:inst, 0:inst] = spectral[...]
     prod[HP - 1 :, :] = jnp.zeros((1, prod.shape[1]), jnp.float32)
     for a in range(planes):
         for j in range(rows):
             for f in range(F):
-                at = ((a * rows + j) * F + f) * LANES
+                at = ((j * planes + a) * F + f) * LANES
                 prod[0:inst, at : at + LANES] = prev[a, f, :, j, :]
-    prod[...] = jnp.dot(mix[...], prod[...], precision=HIGHEST, preferred_element_type=jnp.float32)
-    picked = []
+    mixed = jnp.dot(mix[...], prod[...], precision=HIGHEST, preferred_element_type=jnp.float32)
+    for j in range(rows):
+        for a in range(planes):
+            for f in range(F):
+                at = (j * planes + a) * F + f
+                base[at, 0:inst, :] = (
+                    source[a, f, :, j, :] - mixed[0:inst, at * LANES : (at + 1) * LANES]
+                )
+                base[at, HP - 1 :, :] = jnp.zeros((1, LANES), jnp.float32)
+
+    def emit(k, at, block):
+        outs[k][at : at + size, :] = block
+
+    turn(n, rows, size, cells, turned, emit)
+
+
+def right_kernel(n, azim, *refs):
+    facing, (left, right, prev, coupling, base, face) = refs[:azim], refs[azim : azim + 6]
+    outs, (cells, turned, held, sems) = refs[azim + 6 + n : azim + 6 + 2 * n], refs[azim + 6 + 2 * n :]
+    planes, _, inst, rows, _ = prev.shape
+    mine = lax.axis_index("azim")
     for j in range(rows):
         cell = jnp.broadcast_to(face[j : j + 1, :], (inst, LANES))
-        accs = [jnp.zeros((inst, LANES), jnp.float32)] * F
+        picked = [jnp.zeros((inst, LANES), jnp.float32)] * F
         for k in range(azim):
             origin = lax.rem(mine - k + azim, azim) * rows
             for p in range(rows):
                 here = lax.shift_right_logical(cell, 7) == origin + p
-                accs = [
-                    jnp.where(here, jnp.take_along_axis(facing[k][0, f, :, p, :], cell & 127, axis=1), accs[f])
+                picked = [
+                    jnp.where(here, jnp.take_along_axis(facing[k][f, :, p, :], cell & 127, axis=1), picked[f])
                     for f in range(F)
                 ]
-        picked.append(accs)
-    for j in range(rows):
         for a in range(planes):
             side = coupling[2, a, :, j, :]
             for f in range(F):
-                at = ((a * rows + j) * F + f) * LANES
                 lower = left[a, f, :, rows - 1, :] if j == 0 else prev[a, f, :, j - 1, :]
                 upper = right[a, f, :, 0, :] if j == rows - 1 else prev[a, f, :, j + 1, :]
-                value = source[a, f, :, j, :] + side * (lower + upper) - prod[0:inst, at : at + LANES]
+                at = (j * planes + a) * F + f
+                value = base[at, 0:inst, :] + side * (lower + upper)
                 if a == planes - 1:
-                    value = value - coupling[1, a, :, j, :] * picked[j][f]
-                cells[(j * planes + a) * F + f, 0:inst, :] = value
+                    value = value - coupling[1, a, :, j, :] * picked[f]
+                cells[at, 0:inst, :] = value
+                cells[at, HP - 1 :, :] = jnp.zeros((1, LANES), jnp.float32)
     size, count = planes * F, held.shape[1]
 
     def emit(k, at, block):
@@ -195,12 +194,8 @@
     sweep(read, lambda a: [read_right(a, f) for f in range(F)], n * planes, group, fronts, emit)
 
 
-def second_kernel(
-    planes, group, halves, part, azim, lines, value, swapped, from_left, from_right, spectral, face,
-    crossed, partner, out, fronts, mix, spread, prod,
-):
+def middle_kernel(planes, group, halves, part, lines, value, swapped, spectral, out, mix, spread, prod):
     read = reader(lines, group, planes, ITEMS)
-    last = lines.shape[0] // (group * planes * ITEMS) * planes
     inst = spectral.shape[0]
     wide = halves * LANES
     mix[...] = jnp.zeros_like(mix)
@@ -226,6 +221,21 @@
     mixed = jnp.dot(whole, spread[...], precision=HIGHEST, preferred_element_type=jnp.float32)
     for half in range(halves):
         prod[pl.ds(half, count, stride=halves), :] = mixed[:, half * LANES : (half + 1) * LANES]
+    for a in range(value.shape[0] // (F * group)):
+        side = read(a, SIDE)
+        for f in range(F):
+            at = (a * F + f) * group
+            out[at : at + group, :] = (
+                read(a, SOURCE + f) + side * swapped[at : at + group, :] - prod[at : at + group, :]
+            )
+
+
+def second_kernel(planes, group, halves, part, azim, lines, ready, from_left, from_right, face, *rest):
+    *pieces, out, fronts = rest
+    crossed, partner = pieces[: len(pieces) // 2], pieces[len(pieces) // 2 :]
+    read = reader(lines, group, planes, ITEMS)
+    last = lines.shape[0] // (group * planes * ITEMS) * planes
+    shift = part.bit_length() - 1
     rows = group // halves
     count = F * group
     mine, axial = lax.axis_index("azim"), lax.axis_index("axial")
@@ -238,20 +248,21 @@
     for j in range(rows):
         own = jnp.broadcast_to(face[j : j + 1, :], (count, LANES))
         cell = jnp.take_along_axis(own, me * part + (lane_at & (part - 1)), axis=1)
-        cells.append((lax.shift_right_logical(cell, shift) - row_cell * owners, (lane_at & (LANES - part)) + (cell & (part - 1))))
+        block = jnp.where(axial < owners, lax.shift_right_logical(cell, shift) - row_cell * owners, -1)
+        cells.append((block, (lane_at & (LANES - part)) + (cell & (part - 1))))
         accs.append(jnp.zeros((count, LANES), jnp.float32))
-    for side, buffer in enumerate((crossed, partner)):
+    for side, buffers in enumerate((crossed, partner)):
         sender = core ^ side
-        for k in range(buffer.shape[0]):
+        for at, buffer in enumerate(buffers):
+            k, i = at // azim, at % azim
             for q in range(2):
-                for i in range(azim):
-                    owner = (chip ^ (2 * k + sender)) * 2 + (sender ^ q)
-                    block = lax.rem(mine - i + azim, azim) * (rows * owners) + owner
-                    values = buffer[k, q, i]
-                    for j in range(rows):
-                        accs[j] = jnp.where(
-                            cells[j][0] == block, jnp.take_along_axis(values, cells[j][1], axis=1), accs[j]
-                        )
+                owner = (chip ^ (2 * k + sender)) * 2 + (sender ^ q)
+                block = lax.rem(mine - i + azim, azim) * (rows * owners) + owner
+                values = buffer[q]
+                for j in range(rows):
+                    accs[j] = jnp.where(
+                        cells[j][0] == block, jnp.take_along_axis(values, cells[j][1], axis=1), accs[j]
+                    )
     picked = [
         [
             sum(accs[j][(f * rows + p) * halves : (f * rows + p + 1) * halves] for p in range(rows))
@@ -267,8 +278,7 @@
         for f in range(F):
             at = (a * F + f) * group
             halo = jnp.where(first, from_left[at : at + group, :], from_right[at : at + group, :])
-            around = swapped[at : at + group, :] + halo
-            entry = read(a, SOURCE + f) + side * around - prod[at : at + group, :]
+            entry = ready[at : at + group, :] + side * halo
             if a == last - 1:
                 face_rows = jnp.concatenate([picked[j][f] for j in range(rows)], axis=0)
                 entry = entry - read(a, UPPER) * face_rows
@@ -332,53 +342,55 @@
         return jax.ShapeDtypeStruct(lead or x.shape, x.dtype)
 
     face = face_map.reshape(rows, radial)
-    left, right = around(prev, prev)
-    facing = [
-        lax.ppermute(
-            prev, both, [(n * azim + y, (n - 1) * azim + (y + k) % azim) for y in range(azim)]
-        )
-        for k in range(azim)
-    ]
     size, count = planes * ITEMS, planes * F
     block = jax.ShapeDtypeStruct((group * (size + count), LANES), f32)
     hbm, vmem, anywhere = (
         pl.BlockSpec(memory_space=space) for space in (pltpu.HBM, pltpu.VMEM, pl.ANY)
     )
-
-    def like(x):
-        return jax.ShapeDtypeStruct(x.shape, x.dtype)
-
     inputs = (source, prev, diag, coupling, spectral, face)
-    *packed, source, prev, coupling, spectral, face = pl.pallas_call(
+    source, prev, diag, coupling, spectral, face, first = pl.pallas_call(
+        fetch_kernel,
+        in_specs=[hbm] * 6,
+        out_shape=[jax.ShapeDtypeStruct(x.shape, x.dtype) for x in inputs]
+        + [jax.ShapeDtypeStruct(prev.shape[1:], f32)],
+        scratch_shapes=[pltpu.SemaphoreType.DMA((7,))],
+        compiler_params=params(),
+        name="fetch",
+    )(*(pltpu.with_memory_space_constraint(x, pltpu.HBM) for x in inputs))
+    left, right = around(prev, prev)
+    facing = [
+        lax.ppermute(
+            first, both, [(n * azim + y, (n - 1) * azim + (y + k) % azim) for y in range(azim)]
+        )
+        for k in range(azim)
+    ]
+    *packed, base = pl.pallas_call(
         functools.partial(pack_kernel, n),
-        in_specs=[hbm] * 6,
-        out_shape=[block] * n + [like(x) for x in (source, prev, coupling, spectral, face)],
+        out_shape=[block] * n + [jax.ShapeDtypeStruct((rows * count, HP, LANES), f32)],
         scratch_shapes=[
             pltpu.VMEM((rows * size, HP, LANES), f32),
             pltpu.VMEM((n, halves, LANES, rows * size), f32),
-            pltpu.VMEM(diag.shape, diag.dtype),
-            pltpu.SemaphoreType.DMA((6,)),
+            pltpu.VMEM((HP, HP), f32),
+            pltpu.VMEM((HP, rows * count * LANES), f32),
         ],
         compiler_params=params(),
         name="pack",
-    )(*(pltpu.with_memory_space_constraint(x, pltpu.HBM) for x in inputs))
+    )(source, prev, diag, coupling, spectral)
     packed = pl.pallas_call(
         functools.partial(right_kernel, n, azim),
-        in_specs=[vmem] * (7 + azim) + [anywhere] * n,
+        in_specs=[vmem] * (6 + azim) + [anywhere] * n,
         out_specs=[anywhere] * n,
         out_shape=[block] * n,
         scratch_shapes=[
             pltpu.VMEM((rows * count, HP, LANES), f32),
             pltpu.VMEM((n, halves, LANES, rows * count), f32),
-            pltpu.VMEM((HP, HP), f32),
-            pltpu.VMEM((HP, rows * count * LANES), f32),
             pltpu.VMEM((n, group * count, LANES), f32),
             pltpu.SemaphoreType.DMA((n,)),
         ],
-        input_output_aliases={7 + azim + k: k for k in range(n)},
+        input_output_aliases={6 + azim + k: k for k in range(n)},
         compiler_params=params(),
         name="right_side",
-    )(source, prev, left, right, coupling, spectral, face, *facing, *packed)
+    )(*facing, left, right, prev, coupling, base, face, *packed)
     order = sorted(range(n), key=lambda k: (k & 1, -bin(k & ~1).count("1"), k))
     blocks = [
         lax.ppermute(packed[k], "axial", [(i, i ^ k) for i in range(2 * n)]) if k else packed[k]
@@ -395,36 +407,38 @@
     )(*blocks)
     from_left, from_right = around(swapped, swapped)
     piece = value[: F * group]
-    pieces = [piece] + [
-        lax.ppermute(piece, "azim", [(y, (y + k) % azim) for y in range(azim)]) for k in range(1, azim)
-    ]
-    piece = jnp.stack(pieces)
     core = [(i, i ^ 1) for i in range(2 * n)]
     chip = jnp.stack([piece, lax.ppermute(piece, "axial", core)])
     chips = n // 2
-    crossed = jnp.stack(
-        [
-            lax.ppermute(
-                chip,
-                "axial",
-                [(n + 2 * c + b, 2 * (c ^ (2 * k + b)) + b) for c in range(chips) for b in range(2)],
-            )
-            for k in range(chips // 2)
-        ]
-    )
-    partner = lax.ppermute(crossed, "axial", core)
-    value = pl.pallas_call(
-        functools.partial(second_kernel, planes, group, halves, part, azim),
+    crossed = []
+    for k in range(chips // 2):
+        for i in range(azim):
+            there = [
+                ((n + 2 * c + b) * azim + y, (2 * (c ^ (2 * k + b)) + b) * azim + (y + i) % azim)
+                for c in range(chips)
+                for b in range(2)
+                for y in range(azim)
+            ]
+            crossed.append(lax.ppermute(chip, both, there + [(b, a) for a, b in there]))
+    partner = [lax.ppermute(x, "axial", core) for x in crossed]
+    ready = pl.pallas_call(
+        functools.partial(middle_kernel, planes, group, halves, part),
         out_shape=shape,
         scratch_shapes=[
-            scratch,
             pltpu.VMEM((HP, HP), f32),
             pltpu.VMEM((halves * LANES, halves * LANES), f32),
             pltpu.VMEM((last * F * group, LANES), f32),
         ],
         compiler_params=params(),
+        name="spectral_term",
+    )(lines, value, swapped, spectral)
+    value = pl.pallas_call(
+        functools.partial(second_kernel, planes, group, halves, part, azim),
+        out_shape=shape,
+        scratch_shapes=[scratch],
+        compiler_params=params(),
         name="second_sweep",
-    )(lines, value, swapped, from_left, from_right, spectral, face, crossed, partner)
+    )(lines, ready, from_left, from_right, face, *crossed, *partner)
     value = lax.all_to_all(
         value.reshape(n, planes * F * group, LANES), "axial", 0, 0, axis_index_groups=axial, tiled=True
     )

time: 56.7 us -> 51.3 us (0.905)
  waiting for transfers between devices: 21.4 us -> 6.68 us
  starting transfers between devices: 19.4 us -> 28.6 us
    ppermute x6 -> x10, waiting for transfers between devices: 8.43 us -> 1.64 us  [the longest x4 1.63 us: shards(): crossed.append(lax.ppermute(chip, both, there + [(b, a) for a, b in there]))]
    ppermute x7, waiting for transfers between devices: 11 us -> 4.63 us  [shards(): lax.ppermute(packed[k], 'axial', [(i, i ^ k) for i in range(2 * n)])]
    ppermute x7, starting transfers between devices: 8.67 us -> 13.4 us  [shards(): lax.ppermute(packed[k], 'axial', [(i, i ^ k) for i in range(2 * n)])]
    ppermute x6 -> x10, starting transfers between devices: 6.09 us -> 10.5 us  [the longest x4 7.71 us: shards(): crossed.append(lax.ppermute(chip, both, there + [(b, a) for a, b in there]))]
    pallas_call x1 -> x3, Pallas kernels: 3.35 us -> 4.63 us  [the longest x1 2.23 us: shards(): pl.pallas_call(functools.partial(pack_kernel, n), out_shape=[block] * n +...]
    ppermute x1, waiting for transfers between devices: 1.19 us -> 0.01 us  [shards(): chip = jnp.stack([piece, lax.ppermute(piece, 'axial', core)])]
    pallas_call x1, Pallas kernels: 1.39 us -> 0.55 us  [shards(): pl.pallas_call(functools.partial(second_kernel, planes, group, halves, pa...]
  transfers between devices with their start and end apart: 16 -> 20, of which waited for: 10 -> 5; matrix products, arithmetic and copies ran while one was open for 0% -> 0% of each run, Pallas kernels for 6% -> 7%
where the time goes in v3:
time: 51.3 us; the launch traced here: 51.1 us
  starting transfers between devices  28.6 us (56%)
  Pallas kernels  7.87 us (15%)
  blocking collectives  7.84 us (15%)
  waiting for transfers between devices  6.68 us (13%)
    ppermute x7, starting transfers between devices, shards(): lax.ppermute(packed[k], 'axial', [(i, i ^ k) for i in range(2 * n)])  13.4 us
    all_to_all x1, blocking collectives, shards(): lax.all_to_all(value.reshape(n, planes * F * group, LANES), 'axial', 0, 0...  7.84 us
    ppermute x4, starting transfers between devices, shards(): crossed.append(lax.ppermute(chip, both, there + [(b, a) for a, b in there]))  7.71 us
    ppermute x2, starting transfers between devices, around(): got = lax.ppermute(up, 'azim', forward)  4.68 us
    ppermute x7, waiting for transfers between devices, shards(): lax.ppermute(packed[k], 'axial', [(i, i ^ k) for i in range(2 * n)])  4.63 us
    pallas_call x1, Pallas kernels, shards(): pl.pallas_call(functools.partial(pack_kernel, n), out_shape=[block] * n +...  2.23 us
    ppermute x4, waiting for transfers between devices, shards(): crossed.append(lax.ppermute(chip, both, there + [(b, a) for a, b in there]))  1.63 us
    ppermute x4, starting transfers between devices, shards(): partner = [lax.ppermute(x, 'axial', core) for x in crossed]  1.42 us
  transfers between devices with their start and end apart: 20, of which 5 were waited for; matrix products, arithmetic and copies ran while one was open for 0% of the time, Pallas kernels for 7%

profile of v3, /device:TPU:0, one launch (start us, length us, event | category | flops | bytes accessed | tf_op | source)
XLA Modules:
  0.0 51.1 jit_solution(5297581687305987088)
XLA Ops:
  0.0 1.3 %fetch.1 = (f32[2,5,15,2,128]{4,3,2,1,0:T(2,128)S(1)}, f32[2,5,15,2,128]{4,3,2,1,0:T(2,128)S(1)}, bf16[2,5,5,15,2,128]{5,4,3,2,1,0:T(2,128)(2,1)S(1)}, f32[3,2,1...) custom-call(f32[2,5,15,2,128]{4,3,2,1,0:T(2,128)} %bitcast.12, ...), custom_call_target="tpu_custom_call" | custom-call | tf_op jit(solution)/shard_map/fetch/pallas_call | solution.py:351
  1.3 3.0 %collective-permute-start.2 = (f32[2,5,15,2,128]{4,3,2,1,0:T(2,128)S(1)}, f32[2,5,15,2,128]{4,3,2,1,0:T(2,128)S(1)}, u32[]{:S(2)}, u32[]{:S(2)}) collective-permute-start(f32[2,5,15,2,128]{4,3,2,1,0:T(2,128)S(1)} %get-tuple-element.33.prev.refs_4_), channel_id=1, source_target_pairs={{0,1},{1,0},{2,3},{3,2},{4,5},{5,4},{6,7},{7,6},{8,9},{9,8},{10,11... | collective-permute-start | bytes 460808 | tf_op jit(solution)/shard_map/ppermute | solution.py:334
  4.3 0.7 %collective-permute-start.1 = (f32[5,15,2,128]{3,2,1,0:T(2,128)S(1)}, f32[5,15,2,128]{3,2,1,0:T(2,128)S(1)}, u32[]{:S(2)}, u32[]{:S(2)}) collective-permute-start(f32[5,15,2,128]{3,2,1,0:T(2,128)S(1)} %get-tuple-element.32), channel_id=1, source_target_pairs={{16,15},{17,14}} | collective-permute-start | bytes 230408 | tf_op jit(solution)/shard_map/ppermute | solution.py:362
  5.0 0.7 %collective-permute-start = (f32[5,15,2,128]{3,2,1,0:T(2,128)S(1)}, f32[5,15,2,128]{3,2,1,0:T(2,128)S(1)}, u32[]{:S(2)}, u32[]{:S(2)}) collective-permute-start(f32[5,15,2,128]{3,2,1,0:T(2,128)S(1)} %get-tuple-element.32), channel_id=1, source_target_pairs={{16,14},{17,15}} | collective-permute-start | bytes 230408 | tf_op jit(solution)/shard_map/ppermute | solution.py:362
  5.6 2.2 %pack.1 = (f32[304,128]{1,0:T(8,128)S(1)}, f32[304,128]{1,0:T(8,128)S(1)}, f32[304,128]{1,0:T(8,128)S(1)}, f32[304,128]{1,0:T(8,128)S(1)}, f32[304,128]{1,0:T(8,...) custom-call(f32[2,5,15,2,128]{4,3,2,1,0:T(2,128)S(1)} %get-tuple-ele, ...), custom_call_target="tpu_custom_call" | custom-call | tf_op jit(solution)/shard_map/pack/pallas_call | solution.py:367
  7.9 0.0 collective-permute-done.1.refs_1_
  7.9 0.0 collective-permute-done.refs_0_
  7.9 0.4 collective-permute-done.2.refs_2_.refs_3_
  8.3 1.2 %right_side.1 = (f32[304,128]{1,0:T(8,128)S(1)}, f32[304,128]{1,0:T(8,128)S(1)}, f32[304,128]{1,0:T(8,128)S(1)}, f32[304,128]{1,0:T(8,128)S(1)}, f32[304,128]{1,...) custom-call(f32[5,15,2,128]{3,2,1,0:T(2,128)S(1)} %collective-permut, ...), custom_call_target="tpu_custom_call", output_to_operand_aliasing={{0}: (8, {}), {1}: (9, {}), {2}: (10, {}), {3}: (11, {}), {... | custom-call | tf_op jit(solution)/shard_map/right_side/pallas_call | solution.py:379
  9.6 2.8 %collective-permute-start.3 = (f32[304,128]{1,0:T(8,128)S(1)}, f32[304,128]{1,0:T(8,128)S(1)}, u32[]{:S(2)}, u32[]{:S(2)}) collective-permute-start(f32[304,128]{1,0:T(8,128)S(1)} %get-tuple-element.48), channel_id=1, source_target_pairs={{0,12},{2,14},{4,8},{6,10},{8,4},{10,6},{12,0},{14,2},{16,28},{18,... | collective-permute-start | bytes 466952 | tf_op jit(solution)/shard_map/ppermute | solution.py:396
  12.3 0.5 %collective-permute-start.4 = (f32[304,128]{1,0:T(8,128)S(1)}, f32[304,128]{1,0:T(8,128)S(1)}, u32[]{:S(2)}, u32[]{:S(2)}) collective-permute-start(f32[304,128]{1,0:T(8,128)S(1)} %get-tuple-element.49), channel_id=1, source_target_pairs={{0,4},{2,6},{4,0},{6,2},{8,12},{10,14},{12,8},{14,10},{16,20},{18,... | collective-permute-start | bytes 466952 | tf_op jit(solution)/shard_map/ppermute | solution.py:396
  12.9 0.2 collective-permute-start.5
  13.1 4.7 %collective-permute-start.6 = (f32[304,128]{1,0:T(8,128)S(1)}, f32[304,128]{1,0:T(8,128)S(1)}, u32[]{:S(2)}, u32[]{:S(2)}) collective-permute-start(f32[304,128]{1,0:T(8,128)S(1)} %get-tuple-element.52), channel_id=1, source_target_pairs={{0,14},{2,12},{4,10},{6,8},{8,6},{10,4},{12,2},{14,0},{16,30},{18,... | collective-permute-start | bytes 466952 | tf_op jit(solution)/shard_map/ppermute | solution.py:396
  17.8 0.0 collective-permute-start.7
  17.8 0.0 collective-permute-done.3.refs_0_
  17.9 0.6 %collective-permute-start.8 = (f32[304,128]{1,0:T(8,128)S(1)}, f32[304,128]{1,0:T(8,128)S(1)}, u32[]{:S(2)}, u32[]{:S(2)}) collective-permute-start(f32[304,128]{1,0:T(8,128)S(1)} %get-tuple-element.54), channel_id=1, source_target_pairs={{0,10},{2,8},{4,14},{6,12},{8,2},{10,0},{12,6},{14,4},{16,26},{18,... | collective-permute-start | bytes 466952 | tf_op jit(solution)/shard_map/ppermute | solution.py:396
  18.5 1.5 %collective-permute-done.4.refs_1_ = f32[304,128]{1,0:T(8,128)S(1)} collective-permute-done((f32[304,128]{1,0:T(8,128)S(1)}, f32[304,128]{1,0:T(8,128)S(1)}, u32[]{:S(2)}, u32[]{:S(2)}) %collective-permute-start.4) | collective-permute-done | bytes 155680 | tf_op jit(solution)/shard_map/ppermute | solution.py:396
  20.0 4.5 %collective-permute-start.9 = (f32[304,128]{1,0:T(8,128)S(1)}, f32[304,128]{1,0:T(8,128)S(1)}, u32[]{:S(2)}, u32[]{:S(2)}) collective-permute-start(f32[304,128]{1,0:T(8,128)S(1)} %get-tuple-element.55), channel_id=1, source_target_pairs={{0,2},{2,0},{4,6},{6,4},{8,10},{10,8},{12,14},{14,12},{16,18},{18,... | collective-permute-start | bytes 466952 | tf_op jit(solution)/shard_map/ppermute | solution.py:396
  24.5 0.0 collective-permute-done.5.refs_2_
  24.5 1.4 %collective-permute-done.6.refs_4_ = f32[304,128]{1,0:T(8,128)S(1)} collective-permute-done((f32[304,128]{1,0:T(8,128)S(1)}, f32[304,128]{1,0:T(8,128)S(1)}, u32[]{:S(2)}, u32[]{:S(2)}) %collective-permute-start.6) | collective-permute-done | bytes 155680 | tf_op jit(solution)/shard_map/ppermute | solution.py:396
  25.9 1.7 %collective-permute-done.7.refs_5_ = f32[304,128]{1,0:T(8,128)S(1)} collective-permute-done((f32[304,128]{1,0:T(8,128)S(1)}, f32[304,128]{1,0:T(8,128)S(1)}, u32[]{:S(2)}, u32[]{:S(2)}) %collective-permute-start.7) | collective-permute-done | bytes 155680 | tf_op jit(solution)/shard_map/ppermute | solution.py:396
  27.6 0.0 collective-permute-done.8.refs_6_
  27.6 0.0 collective-permute-done.9.refs_7_
  27.6 0.4 first_sweep.1
  28.0 0.1 collective-permute-start.11
  28.1 1.6 %collective-permute-start.10 = (f32[320,128]{1,0:T(8,128)S(1)}, f32[320,128]{1,0:T(8,128)S(1)}, u32[]{:S(2)}, u32[]{:S(2)}) collective-permute-start(f32[320,128]{1,0:T(8,128)S(1)} %get-tuple-element.58.swapped), channel_id=1, source_target_pairs={{0,1},{1,0},{2,3},{3,2},{4,5},{5,4},{6,7},{7,6},{8,9},{9,8},{10,11... | collective-permute-start | bytes 491528 | tf_op jit(solution)/shard_map/ppermute | solution.py:334
  29.7 0.0 collective-permute-done.11
  29.8 1.7 %collective-permute-start.15 = (f32[2,20,128]{2,1,0:T(8,128)S(1)}, f32[2,20,128]{2,1,0:T(8,128)S(1)}, u32[]{:S(2)}, u32[]{:S(2)}) collective-permute-start(f32[2,20,128]{2,1,0:T(8,128)S(1)} %pad_maximum_fusion), channel_id=1, source_target_pairs={{16,9},{17,8},{18,15},{19,14},{20,13},{21,12},{22,11},{23,10},{24,... | collective-permute-start | bytes 61448 | tf_op jit(solution)/shard_map/ppermute | solution.py:422
  31.4 2.7 %collective-permute-start.14 = (f32[2,20,128]{2,1,0:T(8,128)S(1)}, f32[2,20,128]{2,1,0:T(8,128)S(1)}, u32[]{:S(2)}, u32[]{:S(2)}) collective-permute-start(f32[2,20,128]{2,1,0:T(8,128)S(1)} %pad_maximum_fusion), channel_id=1, source_target_pairs={{16,8},{17,9},{18,14},{19,15},{20,12},{21,13},{22,10},{23,11},{24,... | collective-permute-start | bytes 61448 | tf_op jit(solution)/shard_map/ppermute | solution.py:422
  34.1 0.0 collective-permute-start.13
  34.1 3.4 %collective-permute-start.12 = (f32[2,20,128]{2,1,0:T(8,128)S(1)}, f32[2,20,128]{2,1,0:T(8,128)S(1)}, u32[]{:S(2)}, u32[]{:S(2)}) collective-permute-start(f32[2,20,128]{2,1,0:T(8,128)S(1)} %pad_maximum_fusion), channel_id=1, source_target_pairs={{16,0},{17,1},{18,6},{19,7},{20,4},{21,5},{22,2},{23,3},{24,8},{25... | collective-permute-start | bytes 61448 | tf_op jit(solution)/shard_map/ppermute | solution.py:422
  37.5 0.0 collective-permute-done.15.rest_3_
  37.5 0.8 %collective-permute-start.19 = (f32[2,20,128]{2,1,0:T(8,128)S(1)}, f32[2,20,128]{2,1,0:T(8,128)S(1)}, u32[]{:S(2)}, u32[]{:S(2)}) collective-permute-start(f32[2,20,128]{2,1,0:T(8,128)S(1)} %collective-permute-done.15.rest_3_), channel_id=1, source_target_pairs={{0,2},{2,0},{4,6},{6,4},{8,10},{10,8},{12,14},{14,12},{16,18},{18,... | collective-permute-start | bytes 61448 | tf_op jit(solution)/shard_map/ppermute | solution.py:423
  38.3 0.0 collective-permute-done.14.rest_2_
  38.3 0.1 collective-permute-start.18
  38.4 1.6 %collective-permute-done.13.rest_1_ = f32[2,20,128]{2,1,0:T(8,128)S(1)} collective-permute-done((f32[2,20,128]{2,1,0:T(8,128)S(1)}, f32[2,20,128]{2,1,0:T(8,128)S(1)}, u32[]{:S(2)}, u32[]{:S(2)}) %collective-permute-start.13) | collective-permute-done | bytes 20512 | tf_op jit(solution)/shard_map/ppermute | solution.py:422
  40.0 0.2 collective-permute-start.17
  40.2 0.0 collective-permute-done.12.rest_0_
  40.2 0.3 collective-permute-start.16
  40.5 1.1 %spectral_term.1.ready = f32[320,128]{1,0:T(8,128)S(1)} custom-call(f32[2112,128]{1,0:T(8,128)S(1)} %get-tuple-element.56.lines, f32[320,128]{1,0:T(8,128)S(1)} %get-tuple-element.57.value, f32[320,128]{1,0:T(8,128)S(1)} %get-tuple-element.58.swapped, f32[15,15]{1,0:T(8,128)S(1)} %get-tuple-element.37.spectral), custom_call_target="tpu_custom_call" | custom-call | tf_op jit(solution)/shard_map/spectral_term/pallas_call | solution.py:424
  41.7 0.0 collective-permute-done.19.rest_7_
  41.7 0.0 collective-permute-done.18.rest_6_
  41.7 0.0 collective-permute-done.17.rest_5_
  41.7 0.0 collective-permute-done.16.rest_4_
  41.7 0.0 collective-permute-done.10.from_left.from_right
  41.7 0.5 %second_sweep.1 = f32[320,128]{1,0:T(8,128)S(1)} custom-call(f32[2112,128]{1,0:T(8,128)S(1)} %get-tuple-element.56.lines, f32[320,128]{1,0:T(8,128)S(1)} %spectral_term.1.ready, f32[320,128]{1,0:T(8,128)S(1)} %collective-permute-done.10.from_left.from_right, f32[320,128]{1,0:T(8,128)S(1)} %collective-permute-done.10.from_left.from_right, ...), custom_call_target="tpu_custom_call" | custom-call | tf_op jit(solution)/shard_map/second_sweep/pallas_call | solution.py:435
  42.3 7.8 %all_to_all.5.value = f32[8,40,128]{2,1,0:T(8,128)S(1)} all-to-all(f32[8,40,128]{2,1,0:T(8,128)S(1)} %bitcast.10), channel_id=1, replica_groups={{0,2,4,6,8,10,12,14},{16,18,20,22,24,26,28,30},{1,3,5,7,9,11,13,15},{17..., dimensions={0} | all-to-all | bytes 327680 | tf_op jit(solution)/shard_map/all_to_all | solution.py:442
  50.1 1.0 %unpack.1 = f32[2,5,15,2,128]{4,3,2,1,0:T(2,128)} custom-call(f32[8,40,128]{2,1,0:T(8,128)S(1)} %all_to_all.5.value), custom_call_target="tpu_custom_call" | custom-call | tf_op jit(solution)/shard_map/unpack/pallas_call | solution.py:445
  (2 shorter events, 0.0 us)
Async XLA Ops:
  1.3 7.0 %collective-permute-start.2 = (f32[2,5,15,2,128]{4,3,2,1,0:T(2,128)S(1)}, f32[2,5,15,2,128]{4,3,2,1,0:T(2,128)S(1)}, u32[]{:S(2)}, u32[]{:S(2)}) collective-permute-start(f32[2,5,15,2,128]{4,3,2,1,0:T(2,128)S(1)} %get-tuple-element.33.prev.refs_4_), channel_id=1, source_target_pairs={{0,1},{1,0},{2,3},{3,2},{4,5},{5,4},{6,7},{7,6},{8,9},{9,8},{10,11... | collective-permute-start | bytes 460808 | tf_op jit(solution)/shard_map/ppermute | solution.py:334
  4.3 3.6 %collective-permute-start.1 = (f32[5,15,2,128]{3,2,1,0:T(2,128)S(1)}, f32[5,15,2,128]{3,2,1,0:T(2,128)S(1)}, u32[]{:S(2)}, u32[]{:S(2)}) collective-permute-start(f32[5,15,2,128]{3,2,1,0:T(2,128)S(1)} %get-tuple-element.32), channel_id=1, source_target_pairs={{16,15},{17,14}} | collective-permute-start | bytes 230408 | tf_op jit(solution)/shard_map/ppermute | solution.py:362
  5.0 2.9 %collective-permute-start = (f32[5,15,2,128]{3,2,1,0:T(2,128)S(1)}, f32[5,15,2,128]{3,2,1,0:T(2,128)S(1)}, u32[]{:S(2)}, u32[]{:S(2)}) collective-permute-start(f32[5,15,2,128]{3,2,1,0:T(2,128)S(1)} %get-tuple-element.32), channel_id=1, source_target_pairs={{16,14},{17,15}} | collective-permute-start | bytes 230408 | tf_op jit(solution)/shard_map/ppermute | solution.py:362
  9.6 8.3 %collective-permute-start.3 = (f32[304,128]{1,0:T(8,128)S(1)}, f32[304,128]{1,0:T(8,128)S(1)}, u32[]{:S(2)}, u32[]{:S(2)}) collective-permute-start(f32[304,128]{1,0:T(8,128)S(1)} %get-tuple-element.48), channel_id=1, source_target_pairs={{0,12},{2,14},{4,8},{6,10},{8,4},{10,6},{12,0},{14,2},{16,28},{18,... | collective-permute-start | bytes 466952 | tf_op jit(solution)/shard_map/ppermute | solution.py:396
  12.3 7.7 %collective-permute-start.4 = (f32[304,128]{1,0:T(8,128)S(1)}, f32[304,128]{1,0:T(8,128)S(1)}, u32[]{:S(2)}, u32[]{:S(2)}) collective-permute-start(f32[304,128]{1,0:T(8,128)S(1)} %get-tuple-element.49), channel_id=1, source_target_pairs={{0,4},{2,6},{4,0},{6,2},{8,12},{10,14},{12,8},{14,10},{16,20},{18,... | collective-permute-start | bytes 466952 | tf_op jit(solution)/shard_map/ppermute | solution.py:396
  12.9 11.6 %collective-permute-start.5 = (f32[304,128]{1,0:T(8,128)S(1)}, f32[304,128]{1,0:T(8,128)S(1)}, u32[]{:S(2)}, u32[]{:S(2)}) collective-permute-start(f32[304,128]{1,0:T(8,128)S(1)} %get-tuple-element.50), channel_id=1, source_target_pairs={{0,8},{2,10},{4,12},{6,14},{8,0},{10,2},{12,4},{14,6},{16,24},{18,... | collective-permute-start | bytes 466952 | tf_op jit(solution)/shard_map/ppermute | solution.py:396
  13.1 12.8 %collective-permute-start.6 = (f32[304,128]{1,0:T(8,128)S(1)}, f32[304,128]{1,0:T(8,128)S(1)}, u32[]{:S(2)}, u32[]{:S(2)}) collective-permute-start(f32[304,128]{1,0:T(8,128)S(1)} %get-tuple-element.52), channel_id=1, source_target_pairs={{0,14},{2,12},{4,10},{6,8},{8,6},{10,4},{12,2},{14,0},{16,30},{18,... | collective-permute-start | bytes 466952 | tf_op jit(solution)/shard_map/ppermute | solution.py:396
  17.8 9.7 %collective-permute-start.7 = (f32[304,128]{1,0:T(8,128)S(1)}, f32[304,128]{1,0:T(8,128)S(1)}, u32[]{:S(2)}, u32[]{:S(2)}) collective-permute-start(f32[304,128]{1,0:T(8,128)S(1)} %get-tuple-element.53), channel_id=1, source_target_pairs={{0,6},{2,4},{4,2},{6,0},{8,14},{10,12},{12,10},{14,8},{16,22},{18,... | collective-permute-start | bytes 466952 | tf_op jit(solution)/shard_map/ppermute | solution.py:396
  17.9 9.7 %collective-permute-start.8 = (f32[304,128]{1,0:T(8,128)S(1)}, f32[304,128]{1,0:T(8,128)S(1)}, u32[]{:S(2)}, u32[]{:S(2)}) collective-permute-start(f32[304,128]{1,0:T(8,128)S(1)} %get-tuple-element.54), channel_id=1, source_target_pairs={{0,10},{2,8},{4,14},{6,12},{8,2},{10,0},{12,6},{14,4},{16,26},{18,... | collective-permute-start | bytes 466952 | tf_op jit(solution)/shard_map/ppermute | solution.py:396
  20.0 7.6 %collective-permute-start.9 = (f32[304,128]{1,0:T(8,128)S(1)}, f32[304,128]{1,0:T(8,128)S(1)}, u32[]{:S(2)}, u32[]{:S(2)}) collective-permute-start(f32[304,128]{1,0:T(8,128)S(1)} %get-tuple-element.55), channel_id=1, source_target_pairs={{0,2},{2,0},{4,6},{6,4},{8,10},{10,8},{12,14},{14,12},{16,18},{18,... | collective-permute-start | bytes 466952 | tf_op jit(solution)/shard_map/ppermute | solution.py:396
  28.0 1.7 %collective-permute-start.11 = (f32[20,128]{1,0:T(8,128)S(1)}, f32[20,128]{1,0:T(8,128)S(1)}, u32[]{:S(2)}, u32[]{:S(2)}) collective-permute-start(f32[20,128]{1,0:T(8,128)S(1)} %get-tuple-element.60), channel_id=1, source_target_pairs={{0,2},{2,0},{4,6},{6,4},{8,10},{10,8},{12,14},{14,12},{16,18},{18,... | collective-permute-start | bytes 30728 | tf_op jit(solution)/shard_map/ppermute | solution.py:411
  28.1 13.6 %collective-permute-start.10 = (f32[320,128]{1,0:T(8,128)S(1)}, f32[320,128]{1,0:T(8,128)S(1)}, u32[]{:S(2)}, u32[]{:S(2)}) collective-permute-start(f32[320,128]{1,0:T(8,128)S(1)} %get-tuple-element.58.swapped), channel_id=1, source_target_pairs={{0,1},{1,0},{2,3},{3,2},{4,5},{5,4},{6,7},{7,6},{8,9},{9,8},{10,11... | collective-permute-start | bytes 491528 | tf_op jit(solution)/shard_map/ppermute | solution.py:334
  29.8 7.7 %collective-permute-start.15 = (f32[2,20,128]{2,1,0:T(8,128)S(1)}, f32[2,20,128]{2,1,0:T(8,128)S(1)}, u32[]{:S(2)}, u32[]{:S(2)}) collective-permute-start(f32[2,20,128]{2,1,0:T(8,128)S(1)} %pad_maximum_fusion), channel_id=1, source_target_pairs={{16,9},{17,8},{18,15},{19,14},{20,13},{21,12},{22,11},{23,10},{24,... | collective-permute-start | bytes 61448 | tf_op jit(solution)/shard_map/ppermute | solution.py:422
  31.4 6.9 %collective-permute-start.14 = (f32[2,20,128]{2,1,0:T(8,128)S(1)}, f32[2,20,128]{2,1,0:T(8,128)S(1)}, u32[]{:S(2)}, u32[]{:S(2)}) collective-permute-start(f32[2,20,128]{2,1,0:T(8,128)S(1)} %pad_maximum_fusion), channel_id=1, source_target_pairs={{16,8},{17,9},{18,14},{19,15},{20,12},{21,13},{22,10},{23,11},{24,... | collective-permute-start | bytes 61448 | tf_op jit(solution)/shard_map/ppermute | solution.py:422
  34.1 5.9 %collective-permute-start.13 = (f32[2,20,128]{2,1,0:T(8,128)S(1)}, f32[2,20,128]{2,1,0:T(8,128)S(1)}, u32[]{:S(2)}, u32[]{:S(2)}) collective-permute-start(f32[2,20,128]{2,1,0:T(8,128)S(1)} %pad_maximum_fusion), channel_id=1, source_target_pairs={{16,1},{17,0},{18,7},{19,6},{20,5},{21,4},{22,3},{23,2},{24,9},{25... | collective-permute-start | bytes 61448 | tf_op jit(solution)/shard_map/ppermute | solution.py:422
  34.1 6.1 %collective-permute-start.12 = (f32[2,20,128]{2,1,0:T(8,128)S(1)}, f32[2,20,128]{2,1,0:T(8,128)S(1)}, u32[]{:S(2)}, u32[]{:S(2)}) collective-permute-start(f32[2,20,128]{2,1,0:T(8,128)S(1)} %pad_maximum_fusion), channel_id=1, source_target_pairs={{16,0},{17,1},{18,6},{19,7},{20,4},{21,5},{22,2},{23,3},{24,8},{25... | collective-permute-start | bytes 61448 | tf_op jit(solution)/shard_map/ppermute | solution.py:422
  37.5 4.2 %collective-permute-start.19 = (f32[2,20,128]{2,1,0:T(8,128)S(1)}, f32[2,20,128]{2,1,0:T(8,128)S(1)}, u32[]{:S(2)}, u32[]{:S(2)}) collective-permute-start(f32[2,20,128]{2,1,0:T(8,128)S(1)} %collective-permute-done.15.rest_3_), channel_id=1, source_target_pairs={{0,2},{2,0},{4,6},{6,4},{8,10},{10,8},{12,14},{14,12},{16,18},{18,... | collective-permute-start | bytes 61448 | tf_op jit(solution)/shard_map/ppermute | solution.py:423
  38.3 3.3 %collective-permute-start.18 = (f32[2,20,128]{2,1,0:T(8,128)S(1)}, f32[2,20,128]{2,1,0:T(8,128)S(1)}, u32[]{:S(2)}, u32[]{:S(2)}) collective-permute-start(f32[2,20,128]{2,1,0:T(8,128)S(1)} %collective-permute-done.14.rest_2_), channel_id=1, source_target_pairs={{0,2},{2,0},{4,6},{6,4},{8,10},{10,8},{12,14},{14,12},{16,18},{18,... | collective-permute-start | bytes 61448 | tf_op jit(solution)/shard_map/ppermute | solution.py:423
  40.0 1.7 %collective-permute-start.17 = (f32[2,20,128]{2,1,0:T(8,128)S(1)}, f32[2,20,128]{2,1,0:T(8,128)S(1)}, u32[]{:S(2)}, u32[]{:S(2)}) collective-permute-start(f32[2,20,128]{2,1,0:T(8,128)S(1)} %collective-permute-done.13.rest_1_), channel_id=1, source_target_pairs={{0,2},{2,0},{4,6},{6,4},{8,10},{10,8},{12,14},{14,12},{16,18},{18,... | collective-permute-start | bytes 61448 | tf_op jit(solution)/shard_map/ppermute | solution.py:423
  40.2 1.5 %collective-permute-start.16 = (f32[2,20,128]{2,1,0:T(8,128)S(1)}, f32[2,20,128]{2,1,0:T(8,128)S(1)}, u32[]{:S(2)}, u32[]{:S(2)}) collective-permute-start(f32[2,20,128]{2,1,0:T(8,128)S(1)} %collective-permute-done.12.rest_0_), channel_id=1, source_target_pairs={{0,2},{2,0},{4,6},{6,4},{8,10},{10,8},{12,14},{14,12},{16,18},{18,... | collective-permute-start | bytes 61448 | tf_op jit(solution)/shard_map/ppermute | solution.py:423

commit v4 on v3

--- a/solution.py
+++ b/solution.py
@@ -152,17 +152,22 @@
     return read
 
 
-def sweep(read, right, last, group, fronts, emit):
+def forward(read, right, last, group, fronts):
     carried = [jnp.zeros((group, LANES), jnp.float32)] * F
     for a in range(last):
-        lower = read(a, LOWER)
         vector = right(a)
         if a:
+            lower = read(a, LOWER)
             vector = [vector[g] + lower * carried[g] for g in range(F)]
-        carried = matvec(functools.partial(read, a), vector)
         if a < last - 1:
+            carried = matvec(functools.partial(read, a), vector)
             for f in range(F):
                 fronts[a, f] = carried[f]
+    return vector
+
+
+def backward(read, vector, last, fronts, emit):
+    carried = matvec(functools.partial(read, last - 1), vector)
     emit(last - 1, carried)
     for a in reversed(range(last - 1)):
         upper = read(a, UPPER)
@@ -191,10 +196,14 @@
             swapped[at : at + halves, :] = values[f][halves:]
             swapped[at + halves : at + group, :] = values[f][:halves]
 
-    sweep(read, lambda a: [read_right(a, f) for f in range(F)], n * planes, group, fronts, emit)
-
-
-def middle_kernel(planes, group, halves, part, lines, value, swapped, spectral, out, mix, spread, prod):
+    last = n * planes
+    vector = forward(read, lambda a: [read_right(a, f) for f in range(F)], last, group, fronts)
+    backward(read, vector, last, fronts, emit)
+
+
+def middle_kernel(
+    planes, group, halves, part, lines, value, swapped, spectral, ready, mix, spread, prod
+):
     read = reader(lines, group, planes, ITEMS)
     inst = spectral.shape[0]
     wide = halves * LANES
@@ -225,14 +234,21 @@
         side = read(a, SIDE)
         for f in range(F):
             at = (a * F + f) * group
-            out[at : at + group, :] = (
+            ready[at : at + group, :] = (
                 read(a, SOURCE + f) + side * swapped[at : at + group, :] - prod[at : at + group, :]
             )
 
 
-def second_kernel(planes, group, halves, part, azim, lines, ready, from_left, from_right, face, *rest):
-    *pieces, out, fronts = rest
-    crossed, partner = pieces[: len(pieces) // 2], pieces[len(pieces) // 2 :]
+def collect_kernel(waited, *refs):
+    *pieces, out = refs
+    for i, piece in enumerate(pieces):
+        out[i] = piece[...]
+
+
+def second_kernel(
+    planes, group, halves, part, azim, lines, ready, from_left, from_right, face, crossed, partner,
+    out, fronts,
+):
     read = reader(lines, group, planes, ITEMS)
     last = lines.shape[0] // (group * planes * ITEMS) * planes
     shift = part.bit_length() - 1
@@ -253,12 +269,12 @@
         accs.append(jnp.zeros((count, LANES), jnp.float32))
     for side, buffers in enumerate((crossed, partner)):
         sender = core ^ side
-        for at, buffer in enumerate(buffers):
+        for at in range(buffers.shape[0]):
             k, i = at // azim, at % azim
             for q in range(2):
                 owner = (chip ^ (2 * k + sender)) * 2 + (sender ^ q)
                 block = lax.rem(mine - i + azim, azim) * (rows * owners) + owner
-                values = buffer[q]
+                values = buffers[at, q]
                 for j in range(rows):
                     accs[j] = jnp.where(
                         cells[j][0] == block, jnp.take_along_axis(values, cells[j][1], axis=1), accs[j]
@@ -285,12 +301,14 @@
             result.append(entry)
         return result
 
+    vector = forward(read, right, last, group, fronts)
+
     def emit(a, values):
         for f in range(F):
             at = (a * F + f) * group
             out[at : at + group, :] = values[f]
 
-    sweep(read, right, last, group, fronts, emit)
+    backward(read, vector, last, fronts, emit)
 
 
 def unpack_kernel(halves, part, value, out, turned, block):
@@ -347,6 +365,7 @@
     hbm, vmem, anywhere = (
         pl.BlockSpec(memory_space=space) for space in (pltpu.HBM, pltpu.VMEM, pl.ANY)
     )
+    left, right = around(prev, prev)
     inputs = (source, prev, diag, coupling, spectral, face)
     source, prev, diag, coupling, spectral, face, first = pl.pallas_call(
         fetch_kernel,
@@ -357,7 +376,6 @@
         compiler_params=params(),
         name="fetch",
     )(*(pltpu.with_memory_space_constraint(x, pltpu.HBM) for x in inputs))
-    left, right = around(prev, prev)
     facing = [
         lax.ppermute(
             first, both, [(n * azim + y, (n - 1) * azim + (y + k) % azim) for y in range(azim)]
@@ -420,7 +438,6 @@
                 for y in range(azim)
             ]
             crossed.append(lax.ppermute(chip, both, there + [(b, a) for a, b in there]))
-    partner = [lax.ppermute(x, "axial", core) for x in crossed]
     ready = pl.pallas_call(
         functools.partial(middle_kernel, planes, group, halves, part),
         out_shape=shape,
@@ -432,13 +449,21 @@
         compiler_params=params(),
         name="spectral_term",
     )(lines, value, swapped, spectral)
+    crossed = pl.pallas_call(
+        collect_kernel,
+        in_specs=[pl.BlockSpec(memory_space=pl.ANY)] + [vmem] * len(crossed),
+        out_shape=jax.ShapeDtypeStruct((len(crossed),) + chip.shape, f32),
+        compiler_params=params(),
+        name="collect",
+    )(ready, *crossed)
+    partner = lax.ppermute(crossed, "axial", core)
     value = pl.pallas_call(
         functools.partial(second_kernel, planes, group, halves, part, azim),
         out_shape=shape,
         scratch_shapes=[scratch],
         compiler_params=params(),
         name="second_sweep",
-    )(lines, ready, from_left, from_right, face, *crossed, *partner)
+    )(lines, ready, from_left, from_right, face, crossed, partner)
     value = lax.all_to_all(
         value.reshape(n, planes * F * group, LANES), "axial", 0, 0, axis_index_groups=axial, tiled=True
     )

time: 51.3 us -> 50.8 us (level)
  starting transfers between devices: 28.6 us -> 26.6 us
  waiting for transfers between devices: 6.68 us -> 7.61 us
  blocking collectives: 7.84 us -> 8.43 us
    ppermute x4 -> x1, starting transfers between devices: 1.42 us -> 0.28 us  [shards(): partner = lax.ppermute(crossed, 'axial', core)]
    ppermute x4 -> x1, waiting for transfers between devices: 0.01 us -> 1.09 us  [shards(): partner = lax.ppermute(crossed, 'axial', core)]
    ppermute x7, starting transfers between devices: 13.4 us -> 12.5 us  [shards(): lax.ppermute(packed[k], 'axial', [(i, i ^ k) for i in range(2 * n)])]
    ppermute x7, waiting for transfers between devices: 4.63 us -> 5.33 us  [shards(): lax.ppermute(packed[k], 'axial', [(i, i ^ k) for i in range(2 * n)])]
    all_to_all x1, blocking collectives: 7.84 us -> 8.43 us  [shards(): lax.all_to_all(value.reshape(n, planes * F * group, LANES), 'axial', 0, 0...]
  transfers between devices with their start and end apart: 20 -> 17, of which waited for: 5 -> 5; matrix products, arithmetic and copies ran while one was open for 0% -> 0% of each run, Pallas kernels for 7% -> 9%
where the time goes in v4:
time: 50.8 us; the launch traced here: 50.6 us
  starting transfers between devices  26.6 us (52%)
  blocking collectives  8.43 us (17%)
  Pallas kernels  7.86 us (15%)
  waiting for transfers between devices  7.61 us (15%)
    ppermute x7, starting transfers between devices, shards(): lax.ppermute(packed[k], 'axial', [(i, i ^ k) for i in range(2 * n)])  12.5 us
    all_to_all x1, blocking collectives, shards(): lax.all_to_all(value.reshape(n, planes * F * group, LANES), 'axial', 0, 0...  8.43 us
    ppermute x4, starting transfers between devices, shards(): crossed.append(lax.ppermute(chip, both, there + [(b, a) for a, b in there]))  7.71 us
    ppermute x7, waiting for transfers between devices, shards(): lax.ppermute(packed[k], 'axial', [(i, i ^ k) for i in range(2 * n)])  5.33 us
    ppermute x2, starting transfers between devices, around(): got = lax.ppermute(up, 'azim', forward)  4.64 us
    pallas_call x1, Pallas kernels, shards(): pl.pallas_call(functools.partial(pack_kernel, n), out_shape=[block] * n +...  2.23 us
    ppermute x2, starting transfers between devices, shards(): lax.ppermute(first, both, [(n * azim + y, (n - 1) * azim + (y + k) % azim...  1.33 us
    pallas_call x1, Pallas kernels, shards(): pl.pallas_call(fetch_kernel, in_specs=[hbm] * 6, out_shape=[jax.ShapeDtyp...  1.27 us
  transfers between devices with their start and end apart: 17, of which 5 were waited for; matrix products, arithmetic and copies ran while one was open for 0% of the time, Pallas kernels for 9%

profile of v4, /device:TPU:0, one launch (start us, length us, event | category | flops | bytes accessed | tf_op | source)
XLA Modules:
  0.0 50.6 jit_solution(4415494917085314986)
XLA Ops:
  0.0 3.0 %collective-permute-start.2 = (f32[2,5,15,2,128]{4,3,2,1,0:T(2,128)}, f32[2,5,15,2,128]{4,3,2,1,0:T(2,128)S(1)}, u32[]{:S(2)}, u32[]{:S(2)}) collective-permute-start(f32[2,5,15,2,128]{4,3,2,1,0:T(2,128)} %bitcast.13), channel_id=1, source_target_pairs={{0,1},{1,0},{2,3},{3,2},{4,5},{5,4},{6,7},{7,6},{8,9},{9,8},{10,11... | collective-permute-start | bytes 460808 | tf_op jit(solution)/shard_map/ppermute | solution.py:352
  3.0 1.3 %fetch.1 = (f32[2,5,15,2,128]{4,3,2,1,0:T(2,128)S(1)}, f32[2,5,15,2,128]{4,3,2,1,0:T(2,128)S(1)}, bf16[2,5,5,15,2,128]{5,4,3,2,1,0:T(2,128)(2,1)S(1)}, f32[3,2,1...) custom-call(f32[2,5,15,2,128]{4,3,2,1,0:T(2,128)} %bitcast.12, ...), custom_call_target="tpu_custom_call" | custom-call | tf_op jit(solution)/shard_map/fetch/pallas_call | solution.py:370
  4.2 0.7 %collective-permute-start.1 = (f32[5,15,2,128]{3,2,1,0:T(2,128)S(1)}, f32[5,15,2,128]{3,2,1,0:T(2,128)S(1)}, u32[]{:S(2)}, u32[]{:S(2)}) collective-permute-start(f32[5,15,2,128]{3,2,1,0:T(2,128)S(1)} %get-tuple-element.32), channel_id=1, source_target_pairs={{16,15},{17,14}} | collective-permute-start | bytes 230408 | tf_op jit(solution)/shard_map/ppermute | solution.py:380
  4.9 0.7 %collective-permute-start = (f32[5,15,2,128]{3,2,1,0:T(2,128)S(1)}, f32[5,15,2,128]{3,2,1,0:T(2,128)S(1)}, u32[]{:S(2)}, u32[]{:S(2)}) collective-permute-start(f32[5,15,2,128]{3,2,1,0:T(2,128)S(1)} %get-tuple-element.32), channel_id=1, source_target_pairs={{16,14},{17,15}} | collective-permute-start | bytes 230408 | tf_op jit(solution)/shard_map/ppermute | solution.py:380
  5.6 2.2 %pack.1 = (f32[304,128]{1,0:T(8,128)S(1)}, f32[304,128]{1,0:T(8,128)S(1)}, f32[304,128]{1,0:T(8,128)S(1)}, f32[304,128]{1,0:T(8,128)S(1)}, f32[304,128]{1,0:T(8,...) custom-call(f32[2,5,15,2,128]{4,3,2,1,0:T(2,128)S(1)} %get-tuple-ele, ...), custom_call_target="tpu_custom_call" | custom-call | tf_op jit(solution)/shard_map/pack/pallas_call | solution.py:385
  7.8 0.0 collective-permute-done.1.refs_1_
  7.8 0.0 collective-permute-done.refs_0_
  7.8 0.0 collective-permute-done.2.refs_2_.refs_3_
  7.9 1.3 %right_side.1 = (f32[304,128]{1,0:T(8,128)S(1)}, f32[304,128]{1,0:T(8,128)S(1)}, f32[304,128]{1,0:T(8,128)S(1)}, f32[304,128]{1,0:T(8,128)S(1)}, f32[304,128]{1,...) custom-call(f32[5,15,2,128]{3,2,1,0:T(2,128)S(1)} %collective-permut, ...), custom_call_target="tpu_custom_call", output_to_operand_aliasing={{0}: (8, {}), {1}: (9, {}), {2}: (10, {}), {3}: (11, {}), {... | custom-call | tf_op jit(solution)/shard_map/right_side/pallas_call | solution.py:397
  9.1 2.6 %collective-permute-start.3 = (f32[304,128]{1,0:T(8,128)S(1)}, f32[304,128]{1,0:T(8,128)S(1)}, u32[]{:S(2)}, u32[]{:S(2)}) collective-permute-start(f32[304,128]{1,0:T(8,128)S(1)} %get-tuple-element.48), channel_id=1, source_target_pairs={{0,12},{2,14},{4,8},{6,10},{8,4},{10,6},{12,0},{14,2},{16,28},{18,... | collective-permute-start | bytes 466952 | tf_op jit(solution)/shard_map/ppermute | solution.py:414
  11.7 0.5 %collective-permute-start.4 = (f32[304,128]{1,0:T(8,128)S(1)}, f32[304,128]{1,0:T(8,128)S(1)}, u32[]{:S(2)}, u32[]{:S(2)}) collective-permute-start(f32[304,128]{1,0:T(8,128)S(1)} %get-tuple-element.49), channel_id=1, source_target_pairs={{0,4},{2,6},{4,0},{6,2},{8,12},{10,14},{12,8},{14,10},{16,20},{18,... | collective-permute-start | bytes 466952 | tf_op jit(solution)/shard_map/ppermute | solution.py:414
  12.2 0.4 collective-permute-start.5
  12.7 5.1 %collective-permute-start.6 = (f32[304,128]{1,0:T(8,128)S(1)}, f32[304,128]{1,0:T(8,128)S(1)}, u32[]{:S(2)}, u32[]{:S(2)}) collective-permute-start(f32[304,128]{1,0:T(8,128)S(1)} %get-tuple-element.52), channel_id=1, source_target_pairs={{0,14},{2,12},{4,10},{6,8},{8,6},{10,4},{12,2},{14,0},{16,30},{18,... | collective-permute-start | bytes 466952 | tf_op jit(solution)/shard_map/ppermute | solution.py:414
  17.8 0.0 collective-permute-start.7
  17.8 0.0 collective-permute-done.3.refs_0_
  17.8 0.6 %collective-permute-start.8 = (f32[304,128]{1,0:T(8,128)S(1)}, f32[304,128]{1,0:T(8,128)S(1)}, u32[]{:S(2)}, u32[]{:S(2)}) collective-permute-start(f32[304,128]{1,0:T(8,128)S(1)} %get-tuple-element.54), channel_id=1, source_target_pairs={{0,10},{2,8},{4,14},{6,12},{8,2},{10,0},{12,6},{14,4},{16,26},{18,... | collective-permute-start | bytes 466952 | tf_op jit(solution)/shard_map/ppermute | solution.py:414
  18.4 0.0 collective-permute-done.4.refs_1_
  18.4 3.2 %collective-permute-start.9 = (f32[304,128]{1,0:T(8,128)S(1)}, f32[304,128]{1,0:T(8,128)S(1)}, u32[]{:S(2)}, u32[]{:S(2)}) collective-permute-start(f32[304,128]{1,0:T(8,128)S(1)} %get-tuple-element.55), channel_id=1, source_target_pairs={{0,2},{2,0},{4,6},{6,4},{8,10},{10,8},{12,14},{14,12},{16,18},{18,... | collective-permute-start | bytes 466952 | tf_op jit(solution)/shard_map/ppermute | solution.py:414
  21.7 0.0 collective-permute-done.5.refs_2_
  21.7 4.4 %collective-permute-done.6.refs_4_ = f32[304,128]{1,0:T(8,128)S(1)} collective-permute-done((f32[304,128]{1,0:T(8,128)S(1)}, f32[304,128]{1,0:T(8,128)S(1)}, u32[]{:S(2)}, u32[]{:S(2)}) %collective-permute-start.6) | collective-permute-done | bytes 155680 | tf_op jit(solution)/shard_map/ppermute | solution.py:414
  26.1 0.9 %collective-permute-done.7.refs_5_ = f32[304,128]{1,0:T(8,128)S(1)} collective-permute-done((f32[304,128]{1,0:T(8,128)S(1)}, f32[304,128]{1,0:T(8,128)S(1)}, u32[]{:S(2)}, u32[]{:S(2)}) %collective-permute-start.7) | collective-permute-done | bytes 155680 | tf_op jit(solution)/shard_map/ppermute | solution.py:414
  27.0 0.0 collective-permute-done.8.refs_6_
  27.0 0.0 collective-permute-done.9.refs_7_
  27.0 0.4 first_sweep.1
  27.4 0.1 collective-permute-start.11
  27.5 1.7 %collective-permute-start.10 = (f32[320,128]{1,0:T(8,128)S(1)}, f32[320,128]{1,0:T(8,128)S(1)}, u32[]{:S(2)}, u32[]{:S(2)}) collective-permute-start(f32[320,128]{1,0:T(8,128)S(1)} %get-tuple-element.58.swapped), channel_id=1, source_target_pairs={{0,1},{1,0},{2,3},{3,2},{4,5},{5,4},{6,7},{7,6},{8,9},{9,8},{10,11... | collective-permute-start | bytes 491528 | tf_op jit(solution)/shard_map/ppermute | solution.py:352
  29.2 0.0 collective-permute-done.11
  29.2 1.9 %collective-permute-start.15 = (f32[2,20,128]{2,1,0:T(8,128)S(1)}, f32[2,20,128]{2,1,0:T(8,128)S(1)}, u32[]{:S(2)}, u32[]{:S(2)}) collective-permute-start(f32[2,20,128]{2,1,0:T(8,128)S(1)} %pad_maximum_fusion), channel_id=1, source_target_pairs={{16,9},{17,8},{18,15},{19,14},{20,13},{21,12},{22,11},{23,10},{24,... | collective-permute-start | bytes 61448 | tf_op jit(solution)/shard_map/ppermute | solution.py:440
  31.1 2.4 %collective-permute-start.14 = (f32[2,20,128]{2,1,0:T(8,128)S(1)}, f32[2,20,128]{2,1,0:T(8,128)S(1)}, u32[]{:S(2)}, u32[]{:S(2)}) collective-permute-start(f32[2,20,128]{2,1,0:T(8,128)S(1)} %pad_maximum_fusion), channel_id=1, source_target_pairs={{16,8},{17,9},{18,14},{19,15},{20,12},{21,13},{22,10},{23,11},{24,... | collective-permute-start | bytes 61448 | tf_op jit(solution)/shard_map/ppermute | solution.py:440
  33.5 0.0 collective-permute-start.13
  33.5 3.4 %collective-permute-start.12 = (f32[2,20,128]{2,1,0:T(8,128)S(1)}, f32[2,20,128]{2,1,0:T(8,128)S(1)}, u32[]{:S(2)}, u32[]{:S(2)}) collective-permute-start(f32[2,20,128]{2,1,0:T(8,128)S(1)} %pad_maximum_fusion), channel_id=1, source_target_pairs={{16,0},{17,1},{18,6},{19,7},{20,4},{21,5},{22,2},{23,3},{24,8},{25... | collective-permute-start | bytes 61448 | tf_op jit(solution)/shard_map/ppermute | solution.py:440
  36.9 1.1 %spectral_term.1.waited.ready = f32[320,128]{1,0:T(8,128)S(1)} custom-call(f32[2112,128]{1,0:T(8,128)S(1)} %get-tuple-element.56.lines, f32[320,128]{1,0:T(8,128)S(1)} %get-tuple-element.57.value, f32[320,128]{1,0:T(8,128)S(1)} %get-tuple-element.58.swapped, f32[15,15]{1,0:T(8,128)S(1)} %get-tuple-element.37.spectral), custom_call_target="tpu_custom_call" | custom-call | tf_op jit(solution)/shard_map/spectral_term/pallas_call | solution.py:441
  38.0 0.0 collective-permute-done.15.refs_3_
  38.0 0.0 collective-permute-done.14.refs_2_
  38.1 1.1 %collective-permute-done.13.refs_1_ = f32[2,20,128]{2,1,0:T(8,128)S(1)} collective-permute-done((f32[2,20,128]{2,1,0:T(8,128)S(1)}, f32[2,20,128]{2,1,0:T(8,128)S(1)}, u32[]{:S(2)}, u32[]{:S(2)}) %collective-permute-start.13) | collective-permute-done | bytes 20512 | tf_op jit(solution)/shard_map/ppermute | solution.py:440
  39.2 0.1 collective-permute-done.12.refs_0_
  39.2 0.3 collective-permute-start.16
  39.5 1.1 %collective-permute-done.16.partner = f32[4,2,20,128]{3,2,1,0:T(8,128)S(1)} collective-permute-done((f32[4,2,20,128]{3,2,1,0:T(8,128)S(1)}, f32[4,2,20,128]{3,2,1,0:T(8,128)S(1)}, u32[]{:S(2)}, u32[]{:S(2)}) %collective-permute-start.16) | collective-permute-done | bytes 81952 | tf_op jit(solution)/shard_map/ppermute | solution.py:459
  40.6 0.0 collective-permute-done.10.from_left.from_right
  40.6 0.5 %second_sweep.1 = f32[320,128]{1,0:T(8,128)S(1)} custom-call(f32[2112,128]{1,0:T(8,128)S(1)} %get-tuple-element.56.lines, f32[320,128]{1,0:T(8,128)S(1)} %spectral_term.1.waited.ready, f32[320,128]{1,0:T(8,128)S(1)} %collective-permute-done.10.from_left.from_right, f32[320,128]{1,0:T(8,128)S(1)} %collective-permute-done.10.from_left.from_right, ...), custom_call_target="tpu_custom_call" | custom-call | tf_op jit(solution)/shard_map/second_sweep/pallas_call | solution.py:460
  41.1 8.4 %all_to_all.5.value = f32[8,40,128]{2,1,0:T(8,128)S(1)} all-to-all(f32[8,40,128]{2,1,0:T(8,128)S(1)} %bitcast.10), channel_id=1, replica_groups={{0,2,4,6,8,10,12,14},{16,18,20,22,24,26,28,30},{1,3,5,7,9,11,13,15},{17..., dimensions={0} | all-to-all | bytes 327680 | tf_op jit(solution)/shard_map/all_to_all | solution.py:467
  49.6 1.0 %unpack.1 = f32[2,5,15,2,128]{4,3,2,1,0:T(2,128)} custom-call(f32[8,40,128]{2,1,0:T(8,128)S(1)} %all_to_all.5.value), custom_call_target="tpu_custom_call" | custom-call | tf_op jit(solution)/shard_map/unpack/pallas_call | solution.py:470
  (3 shorter events, 0.0 us)
Async XLA Ops:
  0.0 7.8 %collective-permute-start.2 = (f32[2,5,15,2,128]{4,3,2,1,0:T(2,128)}, f32[2,5,15,2,128]{4,3,2,1,0:T(2,128)S(1)}, u32[]{:S(2)}, u32[]{:S(2)}) collective-permute-start(f32[2,5,15,2,128]{4,3,2,1,0:T(2,128)} %bitcast.13), channel_id=1, source_target_pairs={{0,1},{1,0},{2,3},{3,2},{4,5},{5,4},{6,7},{7,6},{8,9},{9,8},{10,11... | collective-permute-start | bytes 460808 | tf_op jit(solution)/shard_map/ppermute | solution.py:352
  4.2 3.6 %collective-permute-start.1 = (f32[5,15,2,128]{3,2,1,0:T(2,128)S(1)}, f32[5,15,2,128]{3,2,1,0:T(2,128)S(1)}, u32[]{:S(2)}, u32[]{:S(2)}) collective-permute-start(f32[5,15,2,128]{3,2,1,0:T(2,128)S(1)} %get-tuple-element.32), channel_id=1, source_target_pairs={{16,15},{17,14}} | collective-permute-start | bytes 230408 | tf_op jit(solution)/shard_map/ppermute | solution.py:380
  4.9 2.9 %collective-permute-start = (f32[5,15,2,128]{3,2,1,0:T(2,128)S(1)}, f32[5,15,2,128]{3,2,1,0:T(2,128)S(1)}, u32[]{:S(2)}, u32[]{:S(2)}) collective-permute-start(f32[5,15,2,128]{3,2,1,0:T(2,128)S(1)} %get-tuple-element.32), channel_id=1, source_target_pairs={{16,14},{17,15}} | collective-permute-start | bytes 230408 | tf_op jit(solution)/shard_map/ppermute | solution.py:380
  9.1 8.7 %collective-permute-start.3 = (f32[304,128]{1,0:T(8,128)S(1)}, f32[304,128]{1,0:T(8,128)S(1)}, u32[]{:S(2)}, u32[]{:S(2)}) collective-permute-start(f32[304,128]{1,0:T(8,128)S(1)} %get-tuple-element.48), channel_id=1, source_target_pairs={{0,12},{2,14},{4,8},{6,10},{8,4},{10,6},{12,0},{14,2},{16,28},{18,... | collective-permute-start | bytes 466952 | tf_op jit(solution)/shard_map/ppermute | solution.py:414
  11.7 6.8 %collective-permute-start.4 = (f32[304,128]{1,0:T(8,128)S(1)}, f32[304,128]{1,0:T(8,128)S(1)}, u32[]{:S(2)}, u32[]{:S(2)}) collective-permute-start(f32[304,128]{1,0:T(8,128)S(1)} %get-tuple-element.49), channel_id=1, source_target_pairs={{0,4},{2,6},{4,0},{6,2},{8,12},{10,14},{12,8},{14,10},{16,20},{18,... | collective-permute-start | bytes 466952 | tf_op jit(solution)/shard_map/ppermute | solution.py:414
  12.2 9.4 %collective-permute-start.5 = (f32[304,128]{1,0:T(8,128)S(1)}, f32[304,128]{1,0:T(8,128)S(1)}, u32[]{:S(2)}, u32[]{:S(2)}) collective-permute-start(f32[304,128]{1,0:T(8,128)S(1)} %get-tuple-element.50), channel_id=1, source_target_pairs={{0,8},{2,10},{4,12},{6,14},{8,0},{10,2},{12,4},{14,6},{16,24},{18,... | collective-permute-start | bytes 466952 | tf_op jit(solution)/shard_map/ppermute | solution.py:414
  12.7 13.4 %collective-permute-start.6 = (f32[304,128]{1,0:T(8,128)S(1)}, f32[304,128]{1,0:T(8,128)S(1)}, u32[]{:S(2)}, u32[]{:S(2)}) collective-permute-start(f32[304,128]{1,0:T(8,128)S(1)} %get-tuple-element.52), channel_id=1, source_target_pairs={{0,14},{2,12},{4,10},{6,8},{8,6},{10,4},{12,2},{14,0},{16,30},{18,... | collective-permute-start | bytes 466952 | tf_op jit(solution)/shard_map/ppermute | solution.py:414
  17.8 9.2 %collective-permute-start.7 = (f32[304,128]{1,0:T(8,128)S(1)}, f32[304,128]{1,0:T(8,128)S(1)}, u32[]{:S(2)}, u32[]{:S(2)}) collective-permute-start(f32[304,128]{1,0:T(8,128)S(1)} %get-tuple-element.53), channel_id=1, source_target_pairs={{0,6},{2,4},{4,2},{6,0},{8,14},{10,12},{12,10},{14,8},{16,22},{18,... | collective-permute-start | bytes 466952 | tf_op jit(solution)/shard_map/ppermute | solution.py:414
  17.8 9.2 %collective-permute-start.8 = (f32[304,128]{1,0:T(8,128)S(1)}, f32[304,128]{1,0:T(8,128)S(1)}, u32[]{:S(2)}, u32[]{:S(2)}) collective-permute-start(f32[304,128]{1,0:T(8,128)S(1)} %get-tuple-element.54), channel_id=1, source_target_pairs={{0,10},{2,8},{4,14},{6,12},{8,2},{10,0},{12,6},{14,4},{16,26},{18,... | collective-permute-start | bytes 466952 | tf_op jit(solution)/shard_map/ppermute | solution.py:414
  18.4 8.6 %collective-permute-start.9 = (f32[304,128]{1,0:T(8,128)S(1)}, f32[304,128]{1,0:T(8,128)S(1)}, u32[]{:S(2)}, u32[]{:S(2)}) collective-permute-start(f32[304,128]{1,0:T(8,128)S(1)} %get-tuple-element.55), channel_id=1, source_target_pairs={{0,2},{2,0},{4,6},{6,4},{8,10},{10,8},{12,14},{14,12},{16,18},{18,... | collective-permute-start | bytes 466952 | tf_op jit(solution)/shard_map/ppermute | solution.py:414
  27.4 1.8 %collective-permute-start.11 = (f32[20,128]{1,0:T(8,128)S(1)}, f32[20,128]{1,0:T(8,128)S(1)}, u32[]{:S(2)}, u32[]{:S(2)}) collective-permute-start(f32[20,128]{1,0:T(8,128)S(1)} %get-tuple-element.60), channel_id=1, source_target_pairs={{0,2},{2,0},{4,6},{6,4},{8,10},{10,8},{12,14},{14,12},{16,18},{18,... | collective-permute-start | bytes 30728 | tf_op jit(solution)/shard_map/ppermute | solution.py:429
  27.5 13.1 %collective-permute-start.10 = (f32[320,128]{1,0:T(8,128)S(1)}, f32[320,128]{1,0:T(8,128)S(1)}, u32[]{:S(2)}, u32[]{:S(2)}) collective-permute-start(f32[320,128]{1,0:T(8,128)S(1)} %get-tuple-element.58.swapped), channel_id=1, source_target_pairs={{0,1},{1,0},{2,3},{3,2},{4,5},{5,4},{6,7},{7,6},{8,9},{9,8},{10,11... | collective-permute-start | bytes 491528 | tf_op jit(solution)/shard_map/ppermute | solution.py:352
  29.2 8.8 %collective-permute-start.15 = (f32[2,20,128]{2,1,0:T(8,128)S(1)}, f32[2,20,128]{2,1,0:T(8,128)S(1)}, u32[]{:S(2)}, u32[]{:S(2)}) collective-permute-start(f32[2,20,128]{2,1,0:T(8,128)S(1)} %pad_maximum_fusion), channel_id=1, source_target_pairs={{16,9},{17,8},{18,15},{19,14},{20,13},{21,12},{22,11},{23,10},{24,... | collective-permute-start | bytes 61448 | tf_op jit(solution)/shard_map/ppermute | solution.py:440
  31.1 6.9 %collective-permute-start.14 = (f32[2,20,128]{2,1,0:T(8,128)S(1)}, f32[2,20,128]{2,1,0:T(8,128)S(1)}, u32[]{:S(2)}, u32[]{:S(2)}) collective-permute-start(f32[2,20,128]{2,1,0:T(8,128)S(1)} %pad_maximum_fusion), channel_id=1, source_target_pairs={{16,8},{17,9},{18,14},{19,15},{20,12},{21,13},{22,10},{23,11},{24,... | collective-permute-start | bytes 61448 | tf_op jit(solution)/shard_map/ppermute | solution.py:440
  33.5 5.6 %collective-permute-start.13 = (f32[2,20,128]{2,1,0:T(8,128)S(1)}, f32[2,20,128]{2,1,0:T(8,128)S(1)}, u32[]{:S(2)}, u32[]{:S(2)}) collective-permute-start(f32[2,20,128]{2,1,0:T(8,128)S(1)} %pad_maximum_fusion), channel_id=1, source_target_pairs={{16,1},{17,0},{18,7},{19,6},{20,5},{21,4},{22,3},{23,2},{24,9},{25... | collective-permute-start | bytes 61448 | tf_op jit(solution)/shard_map/ppermute | solution.py:440
  33.5 5.7 %collective-permute-start.12 = (f32[2,20,128]{2,1,0:T(8,128)S(1)}, f32[2,20,128]{2,1,0:T(8,128)S(1)}, u32[]{:S(2)}, u32[]{:S(2)}) collective-permute-start(f32[2,20,128]{2,1,0:T(8,128)S(1)} %pad_maximum_fusion), channel_id=1, source_target_pairs={{16,0},{17,1},{18,6},{19,7},{20,4},{21,5},{22,2},{23,3},{24,8},{25... | collective-permute-start | bytes 61448 | tf_op jit(solution)/shard_map/ppermute | solution.py:440
  39.2 1.4 %collective-permute-start.16 = (f32[4,2,20,128]{3,2,1,0:T(8,128)S(1)}, f32[4,2,20,128]{3,2,1,0:T(8,128)S(1)}, u32[]{:S(2)}, u32[]{:S(2)}) collective-permute-start(f32[4,2,20,128]{3,2,1,0:T(8,128)S(1)} %collect.1.crossed), channel_id=1, source_target_pairs={{0,2},{2,0},{4,6},{6,4},{8,10},{10,8},{12,14},{14,12},{16,18},{18,... | collective-permute-start | bytes 245768 | tf_op jit(solution)/shard_map/ppermute | solution.py:459

commit v5 on v4

--- a/solution.py
+++ b/solution.py
@@ -100,7 +100,7 @@
 
 def right_kernel(n, azim, *refs):
     facing, (left, right, prev, coupling, base, face) = refs[:azim], refs[azim : azim + 6]
-    outs, (cells, turned, held, sems) = refs[azim + 6 + n : azim + 6 + 2 * n], refs[azim + 6 + 2 * n :]
+    packed, outs, (cells, turned) = refs[azim + 6 : -n - 2], refs[-n - 2 : -2], refs[-2:]
     planes, _, inst, rows, _ = prev.shape
     mine = lax.axis_index("azim")
     for j in range(rows):
@@ -125,22 +125,14 @@
                     value = value - coupling[1, a, :, j, :] * picked[f]
                 cells[at, 0:inst, :] = value
                 cells[at, HP - 1 :, :] = jnp.zeros((1, LANES), jnp.float32)
-    size, count = planes * F, held.shape[1]
+    size, before = planes * F, packed[0].shape[0]
+    for k in range(n):
+        outs[k][0:before, :] = packed[k][...]
 
     def emit(k, at, block):
-        held[k, at : at + size, :] = block
+        outs[k][before + at : before + at + size, :] = block
 
     turn(n, rows, size, cells, turned, emit)
-    copies = [
-        pltpu.make_async_copy(
-            held.at[k], outs[k].at[pl.ds(outs[k].shape[0] - count, count), :], sems.at[k]
-        )
-        for k in range(n)
-    ]
-    for copy in copies:
-        copy.start()
-    for copy in copies:
-        copy.wait()
 
 
 def reader(lines, group, planes, items):
@@ -362,9 +354,7 @@
     face = face_map.reshape(rows, radial)
     size, count = planes * ITEMS, planes * F
     block = jax.ShapeDtypeStruct((group * (size + count), LANES), f32)
-    hbm, vmem, anywhere = (
-        pl.BlockSpec(memory_space=space) for space in (pltpu.HBM, pltpu.VMEM, pl.ANY)
-    )
+    hbm, vmem = pl.BlockSpec(memory_space=pltpu.HBM), pl.BlockSpec(memory_space=pltpu.VMEM)
     left, right = around(prev, prev)
     inputs = (source, prev, diag, coupling, spectral, face)
     source, prev, diag, coupling, spectral, face, first = pl.pallas_call(
@@ -384,7 +374,8 @@
     ]
     *packed, base = pl.pallas_call(
         functools.partial(pack_kernel, n),
-        out_shape=[block] * n + [jax.ShapeDtypeStruct((rows * count, HP, LANES), f32)],
+        out_shape=[jax.ShapeDtypeStruct((group * size, LANES), f32)] * n
+        + [jax.ShapeDtypeStruct((rows * count, HP, LANES), f32)],
         scratch_shapes=[
             pltpu.VMEM((rows * size, HP, LANES), f32),
             pltpu.VMEM((n, halves, LANES, rows * size), f32),
@@ -396,16 +387,11 @@
     )(source, prev, diag, coupling, spectral)
     packed = pl.pallas_call(
         functools.partial(right_kernel, n, azim),
-        in_specs=[vmem] * (6 + azim) + [anywhere] * n,
-        out_specs=[anywhere] * n,
         out_shape=[block] * n,
         scratch_shapes=[
             pltpu.VMEM((rows * count, HP, LANES), f32),
             pltpu.VMEM((n, halves, LANES, rows * count), f32),
-            pltpu.VMEM((n, group * count, LANES), f32),
-            pltpu.SemaphoreType.DMA((n,)),
         ],
-        input_output_aliases={6 + azim + k: k for k in range(n)},
         compiler_params=params(),
         name="right_side",
     )(*facing, left, right, prev, coupling, base, face, *packed)

time: 50.8 us -> 50.5 us (level)
  no operation moved by 1% of the time
where the time goes in v5:
time: 50.5 us; the launch traced here: 50.3 us
  starting transfers between devices  26.6 us (53%)
  blocking collectives  8.43 us (17%)
  Pallas kernels  7.61 us (15%)
  waiting for transfers between devices  7.61 us (15%)
    ppermute x7, starting transfers between devices, shards(): lax.ppermute(packed[k], 'axial', [(i, i ^ k) for i in range(2 * n)])  12.5 us
    all_to_all x1, blocking collectives, shards(): lax.all_to_all(value.reshape(n, planes * F * group, LANES), 'axial', 0, 0...  8.43 us
    ppermute x4, starting transfers between devices, shards(): crossed.append(lax.ppermute(chip, both, there + [(b, a) for a, b in there]))  7.71 us
    ppermute x7, waiting for transfers between devices, shards(): lax.ppermute(packed[k], 'axial', [(i, i ^ k) for i in range(2 * n)])  5.33 us
    ppermute x2, starting transfers between devices, around(): got = lax.ppermute(up, 'azim', forward)  4.64 us
    pallas_call x1, Pallas kernels, shards(): pl.pallas_call(functools.partial(pack_kernel, n), out_shape=[jax.ShapeDty...  2.22 us
    ppermute x2, starting transfers between devices, shards(): lax.ppermute(first, both, [(n * azim + y, (n - 1) * azim + (y + k) % azim...  1.33 us
    pallas_call x1, Pallas kernels, shards(): pl.pallas_call(fetch_kernel, in_specs=[hbm] * 6, out_shape=[jax.ShapeDtyp...  1.27 us
  transfers between devices with their start and end apart: 17, of which 5 were waited for; matrix products, arithmetic and copies ran while one was open for 0% of the time, Pallas kernels for 9%

profile of v5, /device:TPU:0, one launch (start us, length us, event | category | flops | bytes accessed | tf_op | source)
XLA Modules:
  0.0 50.3 jit_solution(6032626394153059392)
XLA Ops:
  0.0 3.0 %collective-permute-start.2 = (f32[2,5,15,2,128]{4,3,2,1,0:T(2,128)}, f32[2,5,15,2,128]{4,3,2,1,0:T(2,128)S(1)}, u32[]{:S(2)}, u32[]{:S(2)}) collective-permute-start(f32[2,5,15,2,128]{4,3,2,1,0:T(2,128)} %bitcast.13), channel_id=1, source_target_pairs={{0,1},{1,0},{2,3},{3,2},{4,5},{5,4},{6,7},{7,6},{8,9},{9,8},{10,11... | collective-permute-start | bytes 460808 | tf_op jit(solution)/shard_map/ppermute | solution.py:344
  3.0 1.3 %fetch.1 = (f32[2,5,15,2,128]{4,3,2,1,0:T(2,128)S(1)}, f32[2,5,15,2,128]{4,3,2,1,0:T(2,128)S(1)}, bf16[2,5,5,15,2,128]{5,4,3,2,1,0:T(2,128)(2,1)S(1)}, f32[3,2,1...) custom-call(f32[2,5,15,2,128]{4,3,2,1,0:T(2,128)} %bitcast.12, ...), custom_call_target="tpu_custom_call" | custom-call | tf_op jit(solution)/shard_map/fetch/pallas_call | solution.py:360
  4.2 0.7 %collective-permute-start.1 = (f32[5,15,2,128]{3,2,1,0:T(2,128)S(1)}, f32[5,15,2,128]{3,2,1,0:T(2,128)S(1)}, u32[]{:S(2)}, u32[]{:S(2)}) collective-permute-start(f32[5,15,2,128]{3,2,1,0:T(2,128)S(1)} %get-tuple-element.32), channel_id=1, source_target_pairs={{16,15},{17,14}} | collective-permute-start | bytes 230408 | tf_op jit(solution)/shard_map/ppermute | solution.py:370
  4.9 0.7 %collective-permute-start = (f32[5,15,2,128]{3,2,1,0:T(2,128)S(1)}, f32[5,15,2,128]{3,2,1,0:T(2,128)S(1)}, u32[]{:S(2)}, u32[]{:S(2)}) collective-permute-start(f32[5,15,2,128]{3,2,1,0:T(2,128)S(1)} %get-tuple-element.32), channel_id=1, source_target_pairs={{16,14},{17,15}} | collective-permute-start | bytes 230408 | tf_op jit(solution)/shard_map/ppermute | solution.py:370
  5.6 2.2 %pack.1 = (f32[264,128]{1,0:T(8,128)S(1)}, f32[264,128]{1,0:T(8,128)S(1)}, f32[264,128]{1,0:T(8,128)S(1)}, f32[264,128]{1,0:T(8,128)S(1)}, f32[264,128]{1,0:T(8,...) custom-call(f32[2,5,15,2,128]{4,3,2,1,0:T(2,128)S(1)} %get-tuple-ele, ...), custom_call_target="tpu_custom_call" | custom-call | tf_op jit(solution)/shard_map/pack/pallas_call | solution.py:375
  7.8 0.0 collective-permute-done.1.refs_1_
  7.8 0.0 collective-permute-done.refs_0_
  7.8 0.0 collective-permute-done.2.refs_2_.refs_3_
  7.8 1.0 %right_side.1 = (f32[304,128]{1,0:T(8,128)S(1)}, f32[304,128]{1,0:T(8,128)S(1)}, f32[304,128]{1,0:T(8,128)S(1)}, f32[304,128]{1,0:T(8,128)S(1)}, f32[304,128]{1,...) custom-call(f32[5,15,2,128]{3,2,1,0:T(2,128)S(1)} %collective-permute-done.refs_0_, ...), custom_call_target="tpu_custom_call" | custom-call | tf_op jit(solution)/shard_map/right_side/pallas_call | solution.py:388
  8.9 2.6 %collective-permute-start.3 = (f32[304,128]{1,0:T(8,128)S(1)}, f32[304,128]{1,0:T(8,128)S(1)}, u32[]{:S(2)}, u32[]{:S(2)}) collective-permute-start(f32[304,128]{1,0:T(8,128)S(1)} %get-tuple-element.48), channel_id=1, source_target_pairs={{0,12},{2,14},{4,8},{6,10},{8,4},{10,6},{12,0},{14,2},{16,28},{18,... | collective-permute-start | bytes 466952 | tf_op jit(solution)/shard_map/ppermute | solution.py:400
  11.4 0.5 %collective-permute-start.4 = (f32[304,128]{1,0:T(8,128)S(1)}, f32[304,128]{1,0:T(8,128)S(1)}, u32[]{:S(2)}, u32[]{:S(2)}) collective-permute-start(f32[304,128]{1,0:T(8,128)S(1)} %get-tuple-element.49), channel_id=1, source_target_pairs={{0,4},{2,6},{4,0},{6,2},{8,12},{10,14},{12,8},{14,10},{16,20},{18,... | collective-permute-start | bytes 466952 | tf_op jit(solution)/shard_map/ppermute | solution.py:400
  11.9 0.4 collective-permute-start.5
  12.4 5.1 %collective-permute-start.6 = (f32[304,128]{1,0:T(8,128)S(1)}, f32[304,128]{1,0:T(8,128)S(1)}, u32[]{:S(2)}, u32[]{:S(2)}) collective-permute-start(f32[304,128]{1,0:T(8,128)S(1)} %get-tuple-element.52), channel_id=1, source_target_pairs={{0,14},{2,12},{4,10},{6,8},{8,6},{10,4},{12,2},{14,0},{16,30},{18,... | collective-permute-start | bytes 466952 | tf_op jit(solution)/shard_map/ppermute | solution.py:400
  17.5 0.0 collective-permute-start.7
  17.5 0.0 collective-permute-done.3.refs_0_
  17.5 0.6 %collective-permute-start.8 = (f32[304,128]{1,0:T(8,128)S(1)}, f32[304,128]{1,0:T(8,128)S(1)}, u32[]{:S(2)}, u32[]{:S(2)}) collective-permute-start(f32[304,128]{1,0:T(8,128)S(1)} %get-tuple-element.54), channel_id=1, source_target_pairs={{0,10},{2,8},{4,14},{6,12},{8,2},{10,0},{12,6},{14,4},{16,26},{18,... | collective-permute-start | bytes 466952 | tf_op jit(solution)/shard_map/ppermute | solution.py:400
  18.2 0.0 collective-permute-done.4.refs_1_
  18.2 3.2 %collective-permute-start.9 = (f32[304,128]{1,0:T(8,128)S(1)}, f32[304,128]{1,0:T(8,128)S(1)}, u32[]{:S(2)}, u32[]{:S(2)}) collective-permute-start(f32[304,128]{1,0:T(8,128)S(1)} %get-tuple-element.55), channel_id=1, source_target_pairs={{0,2},{2,0},{4,6},{6,4},{8,10},{10,8},{12,14},{14,12},{16,18},{18,... | collective-permute-start | bytes 466952 | tf_op jit(solution)/shard_map/ppermute | solution.py:400
  21.4 0.0 collective-permute-done.5.refs_2_
  21.4 4.4 %collective-permute-done.6.refs_4_ = f32[304,128]{1,0:T(8,128)S(1)} collective-permute-done((f32[304,128]{1,0:T(8,128)S(1)}, f32[304,128]{1,0:T(8,128)S(1)}, u32[]{:S(2)}, u32[]{:S(2)}) %collective-permute-start.6) | collective-permute-done | bytes 155680 | tf_op jit(solution)/shard_map/ppermute | solution.py:400
  25.8 0.9 %collective-permute-done.7.refs_5_ = f32[304,128]{1,0:T(8,128)S(1)} collective-permute-done((f32[304,128]{1,0:T(8,128)S(1)}, f32[304,128]{1,0:T(8,128)S(1)}, u32[]{:S(2)}, u32[]{:S(2)}) %collective-permute-start.7) | collective-permute-done | bytes 155680 | tf_op jit(solution)/shard_map/ppermute | solution.py:400
  26.7 0.0 collective-permute-done.8.refs_6_
  26.7 0.0 collective-permute-done.9.refs_7_
  26.7 0.4 first_sweep.1
  27.1 0.1 collective-permute-start.11
  27.2 1.7 %collective-permute-start.10 = (f32[320,128]{1,0:T(8,128)S(1)}, f32[320,128]{1,0:T(8,128)S(1)}, u32[]{:S(2)}, u32[]{:S(2)}) collective-permute-start(f32[320,128]{1,0:T(8,128)S(1)} %get-tuple-element.58.swapped), channel_id=1, source_target_pairs={{0,1},{1,0},{2,3},{3,2},{4,5},{5,4},{6,7},{7,6},{8,9},{9,8},{10,11... | collective-permute-start | bytes 491528 | tf_op jit(solution)/shard_map/ppermute | solution.py:344
  28.9 0.0 collective-permute-done.11
  28.9 1.9 %collective-permute-start.15 = (f32[2,20,128]{2,1,0:T(8,128)S(1)}, f32[2,20,128]{2,1,0:T(8,128)S(1)}, u32[]{:S(2)}, u32[]{:S(2)}) collective-permute-start(f32[2,20,128]{2,1,0:T(8,128)S(1)} %pad_maximum_fusion), channel_id=1, source_target_pairs={{16,9},{17,8},{18,15},{19,14},{20,13},{21,12},{22,11},{23,10},{24,... | collective-permute-start | bytes 61448 | tf_op jit(solution)/shard_map/ppermute | solution.py:426
  30.8 2.4 %collective-permute-start.14 = (f32[2,20,128]{2,1,0:T(8,128)S(1)}, f32[2,20,128]{2,1,0:T(8,128)S(1)}, u32[]{:S(2)}, u32[]{:S(2)}) collective-permute-start(f32[2,20,128]{2,1,0:T(8,128)S(1)} %pad_maximum_fusion), channel_id=1, source_target_pairs={{16,8},{17,9},{18,14},{19,15},{20,12},{21,13},{22,10},{23,11},{24,... | collective-permute-start | bytes 61448 | tf_op jit(solution)/shard_map/ppermute | solution.py:426
  33.3 0.0 collective-permute-start.13
  33.3 3.4 %collective-permute-start.12 = (f32[2,20,128]{2,1,0:T(8,128)S(1)}, f32[2,20,128]{2,1,0:T(8,128)S(1)}, u32[]{:S(2)}, u32[]{:S(2)}) collective-permute-start(f32[2,20,128]{2,1,0:T(8,128)S(1)} %pad_maximum_fusion), channel_id=1, source_target_pairs={{16,0},{17,1},{18,6},{19,7},{20,4},{21,5},{22,2},{23,3},{24,8},{25... | collective-permute-start | bytes 61448 | tf_op jit(solution)/shard_map/ppermute | solution.py:426
  36.6 1.1 %spectral_term.1.waited.ready = f32[320,128]{1,0:T(8,128)S(1)} custom-call(f32[2112,128]{1,0:T(8,128)S(1)} %get-tuple-element.56.lines, f32[320,128]{1,0:T(8,128)S(1)} %get-tuple-element.57.value, f32[320,128]{1,0:T(8,128)S(1)} %get-tuple-element.58.swapped, f32[15,15]{1,0:T(8,128)S(1)} %get-tuple-element.37.spectral), custom_call_target="tpu_custom_call" | custom-call | tf_op jit(solution)/shard_map/spectral_term/pallas_call | solution.py:427
  37.8 0.0 collective-permute-done.15.refs_3_
  37.8 0.0 collective-permute-done.14.refs_2_
  37.8 1.1 %collective-permute-done.13.refs_1_ = f32[2,20,128]{2,1,0:T(8,128)S(1)} collective-permute-done((f32[2,20,128]{2,1,0:T(8,128)S(1)}, f32[2,20,128]{2,1,0:T(8,128)S(1)}, u32[]{:S(2)}, u32[]{:S(2)}) %collective-permute-start.13) | collective-permute-done | bytes 20512 | tf_op jit(solution)/shard_map/ppermute | solution.py:426
  38.9 0.1 collective-permute-done.12.refs_0_
  39.0 0.3 collective-permute-start.16
  39.2 1.1 %collective-permute-done.16.partner = f32[4,2,20,128]{3,2,1,0:T(8,128)S(1)} collective-permute-done((f32[4,2,20,128]{3,2,1,0:T(8,128)S(1)}, f32[4,2,20,128]{3,2,1,0:T(8,128)S(1)}, u32[]{:S(2)}, u32[]{:S(2)}) %collective-permute-start.16) | collective-permute-done | bytes 81952 | tf_op jit(solution)/shard_map/ppermute | solution.py:445
  40.3 0.0 collective-permute-done.10.from_left.from_right
  40.3 0.5 %second_sweep.1 = f32[320,128]{1,0:T(8,128)S(1)} custom-call(f32[2112,128]{1,0:T(8,128)S(1)} %get-tuple-element.56.lines, f32[320,128]{1,0:T(8,128)S(1)} %spectral_term.1.waited.ready, f32[320,128]{1,0:T(8,128)S(1)} %collective-permute-done.10.from_left.from_right, f32[320,128]{1,0:T(8,128)S(1)} %collective-permute-done.10.from_left.from_right, ...), custom_call_target="tpu_custom_call" | custom-call | tf_op jit(solution)/shard_map/second_sweep/pallas_call | solution.py:446
  40.9 8.4 %all_to_all.5.value = f32[8,40,128]{2,1,0:T(8,128)S(1)} all-to-all(f32[8,40,128]{2,1,0:T(8,128)S(1)} %bitcast.10), channel_id=1, replica_groups={{0,2,4,6,8,10,12,14},{16,18,20,22,24,26,28,30},{1,3,5,7,9,11,13,15},{17..., dimensions={0} | all-to-all | bytes 327680 | tf_op jit(solution)/shard_map/all_to_all | solution.py:453
  49.3 1.0 %unpack.1 = f32[2,5,15,2,128]{4,3,2,1,0:T(2,128)} custom-call(f32[8,40,128]{2,1,0:T(8,128)S(1)} %all_to_all.5.value), custom_call_target="tpu_custom_call" | custom-call | tf_op jit(solution)/shard_map/unpack/pallas_call | solution.py:456
  (3 shorter events, 0.0 us)
Async XLA Ops:
  0.0 7.8 %collective-permute-start.2 = (f32[2,5,15,2,128]{4,3,2,1,0:T(2,128)}, f32[2,5,15,2,128]{4,3,2,1,0:T(2,128)S(1)}, u32[]{:S(2)}, u32[]{:S(2)}) collective-permute-start(f32[2,5,15,2,128]{4,3,2,1,0:T(2,128)} %bitcast.13), channel_id=1, source_target_pairs={{0,1},{1,0},{2,3},{3,2},{4,5},{5,4},{6,7},{7,6},{8,9},{9,8},{10,11... | collective-permute-start | bytes 460808 | tf_op jit(solution)/shard_map/ppermute | solution.py:344
  4.2 3.6 %collective-permute-start.1 = (f32[5,15,2,128]{3,2,1,0:T(2,128)S(1)}, f32[5,15,2,128]{3,2,1,0:T(2,128)S(1)}, u32[]{:S(2)}, u32[]{:S(2)}) collective-permute-start(f32[5,15,2,128]{3,2,1,0:T(2,128)S(1)} %get-tuple-element.32), channel_id=1, source_target_pairs={{16,15},{17,14}} | collective-permute-start | bytes 230408 | tf_op jit(solution)/shard_map/ppermute | solution.py:370
  4.9 2.9 %collective-permute-start = (f32[5,15,2,128]{3,2,1,0:T(2,128)S(1)}, f32[5,15,2,128]{3,2,1,0:T(2,128)S(1)}, u32[]{:S(2)}, u32[]{:S(2)}) collective-permute-start(f32[5,15,2,128]{3,2,1,0:T(2,128)S(1)} %get-tuple-element.32), channel_id=1, source_target_pairs={{16,14},{17,15}} | collective-permute-start | bytes 230408 | tf_op jit(solution)/shard_map/ppermute | solution.py:370
  8.9 8.7 %collective-permute-start.3 = (f32[304,128]{1,0:T(8,128)S(1)}, f32[304,128]{1,0:T(8,128)S(1)}, u32[]{:S(2)}, u32[]{:S(2)}) collective-permute-start(f32[304,128]{1,0:T(8,128)S(1)} %get-tuple-element.48), channel_id=1, source_target_pairs={{0,12},{2,14},{4,8},{6,10},{8,4},{10,6},{12,0},{14,2},{16,28},{18,... | collective-permute-start | bytes 466952 | tf_op jit(solution)/shard_map/ppermute | solution.py:400
  11.4 6.8 %collective-permute-start.4 = (f32[304,128]{1,0:T(8,128)S(1)}, f32[304,128]{1,0:T(8,128)S(1)}, u32[]{:S(2)}, u32[]{:S(2)}) collective-permute-start(f32[304,128]{1,0:T(8,128)S(1)} %get-tuple-element.49), channel_id=1, source_target_pairs={{0,4},{2,6},{4,0},{6,2},{8,12},{10,14},{12,8},{14,10},{16,20},{18,... | collective-permute-start | bytes 466952 | tf_op jit(solution)/shard_map/ppermute | solution.py:400
  11.9 9.4 %collective-permute-start.5 = (f32[304,128]{1,0:T(8,128)S(1)}, f32[304,128]{1,0:T(8,128)S(1)}, u32[]{:S(2)}, u32[]{:S(2)}) collective-permute-start(f32[304,128]{1,0:T(8,128)S(1)} %get-tuple-element.50), channel_id=1, source_target_pairs={{0,8},{2,10},{4,12},{6,14},{8,0},{10,2},{12,4},{14,6},{16,24},{18,... | collective-permute-start | bytes 466952 | tf_op jit(solution)/shard_map/ppermute | solution.py:400
  12.4 13.4 %collective-permute-start.6 = (f32[304,128]{1,0:T(8,128)S(1)}, f32[304,128]{1,0:T(8,128)S(1)}, u32[]{:S(2)}, u32[]{:S(2)}) collective-permute-start(f32[304,128]{1,0:T(8,128)S(1)} %get-tuple-element.52), channel_id=1, source_target_pairs={{0,14},{2,12},{4,10},{6,8},{8,6},{10,4},{12,2},{14,0},{16,30},{18,... | collective-permute-start | bytes 466952 | tf_op jit(solution)/shard_map/ppermute | solution.py:400
  17.5 9.2 %collective-permute-start.7 = (f32[304,128]{1,0:T(8,128)S(1)}, f32[304,128]{1,0:T(8,128)S(1)}, u32[]{:S(2)}, u32[]{:S(2)}) collective-permute-start(f32[304,128]{1,0:T(8,128)S(1)} %get-tuple-element.53), channel_id=1, source_target_pairs={{0,6},{2,4},{4,2},{6,0},{8,14},{10,12},{12,10},{14,8},{16,22},{18,... | collective-permute-start | bytes 466952 | tf_op jit(solution)/shard_map/ppermute | solution.py:400
  17.5 9.2 %collective-permute-start.8 = (f32[304,128]{1,0:T(8,128)S(1)}, f32[304,128]{1,0:T(8,128)S(1)}, u32[]{:S(2)}, u32[]{:S(2)}) collective-permute-start(f32[304,128]{1,0:T(8,128)S(1)} %get-tuple-element.54), channel_id=1, source_target_pairs={{0,10},{2,8},{4,14},{6,12},{8,2},{10,0},{12,6},{14,4},{16,26},{18,... | collective-permute-start | bytes 466952 | tf_op jit(solution)/shard_map/ppermute | solution.py:400
  18.2 8.5 %collective-permute-start.9 = (f32[304,128]{1,0:T(8,128)S(1)}, f32[304,128]{1,0:T(8,128)S(1)}, u32[]{:S(2)}, u32[]{:S(2)}) collective-permute-start(f32[304,128]{1,0:T(8,128)S(1)} %get-tuple-element.55), channel_id=1, source_target_pairs={{0,2},{2,0},{4,6},{6,4},{8,10},{10,8},{12,14},{14,12},{16,18},{18,... | collective-permute-start | bytes 466952 | tf_op jit(solution)/shard_map/ppermute | solution.py:400
  27.1 1.8 %collective-permute-start.11 = (f32[20,128]{1,0:T(8,128)S(1)}, f32[20,128]{1,0:T(8,128)S(1)}, u32[]{:S(2)}, u32[]{:S(2)}) collective-permute-start(f32[20,128]{1,0:T(8,128)S(1)} %get-tuple-element.60), channel_id=1, source_target_pairs={{0,2},{2,0},{4,6},{6,4},{8,10},{10,8},{12,14},{14,12},{16,18},{18,... | collective-permute-start | bytes 30728 | tf_op jit(solution)/shard_map/ppermute | solution.py:415
  27.2 13.1 %collective-permute-start.10 = (f32[320,128]{1,0:T(8,128)S(1)}, f32[320,128]{1,0:T(8,128)S(1)}, u32[]{:S(2)}, u32[]{:S(2)}) collective-permute-start(f32[320,128]{1,0:T(8,128)S(1)} %get-tuple-element.58.swapped), channel_id=1, source_target_pairs={{0,1},{1,0},{2,3},{3,2},{4,5},{5,4},{6,7},{7,6},{8,9},{9,8},{10,11... | collective-permute-start | bytes 491528 | tf_op jit(solution)/shard_map/ppermute | solution.py:344
  28.9 8.8 %collective-permute-start.15 = (f32[2,20,128]{2,1,0:T(8,128)S(1)}, f32[2,20,128]{2,1,0:T(8,128)S(1)}, u32[]{:S(2)}, u32[]{:S(2)}) collective-permute-start(f32[2,20,128]{2,1,0:T(8,128)S(1)} %pad_maximum_fusion), channel_id=1, source_target_pairs={{16,9},{17,8},{18,15},{19,14},{20,13},{21,12},{22,11},{23,10},{24,... | collective-permute-start | bytes 61448 | tf_op jit(solution)/shard_map/ppermute | solution.py:426
  30.8 6.9 %collective-permute-start.14 = (f32[2,20,128]{2,1,0:T(8,128)S(1)}, f32[2,20,128]{2,1,0:T(8,128)S(1)}, u32[]{:S(2)}, u32[]{:S(2)}) collective-permute-start(f32[2,20,128]{2,1,0:T(8,128)S(1)} %pad_maximum_fusion), channel_id=1, source_target_pairs={{16,8},{17,9},{18,14},{19,15},{20,12},{21,13},{22,10},{23,11},{24,... | collective-permute-start | bytes 61448 | tf_op jit(solution)/shard_map/ppermute | solution.py:426
  33.3 5.6 %collective-permute-start.13 = (f32[2,20,128]{2,1,0:T(8,128)S(1)}, f32[2,20,128]{2,1,0:T(8,128)S(1)}, u32[]{:S(2)}, u32[]{:S(2)}) collective-permute-start(f32[2,20,128]{2,1,0:T(8,128)S(1)} %pad_maximum_fusion), channel_id=1, source_target_pairs={{16,1},{17,0},{18,7},{19,6},{20,5},{21,4},{22,3},{23,2},{24,9},{25... | collective-permute-start | bytes 61448 | tf_op jit(solution)/shard_map/ppermute | solution.py:426
  33.3 5.7 %collective-permute-start.12 = (f32[2,20,128]{2,1,0:T(8,128)S(1)}, f32[2,20,128]{2,1,0:T(8,128)S(1)}, u32[]{:S(2)}, u32[]{:S(2)}) collective-permute-start(f32[2,20,128]{2,1,0:T(8,128)S(1)} %pad_maximum_fusion), channel_id=1, source_target_pairs={{16,0},{17,1},{18,6},{19,7},{20,4},{21,5},{22,2},{23,3},{24,8},{25... | collective-permute-start | bytes 61448 | tf_op jit(solution)/shard_map/ppermute | solution.py:426
  39.0 1.4 %collective-permute-start.16 = (f32[4,2,20,128]{3,2,1,0:T(8,128)S(1)}, f32[4,2,20,128]{3,2,1,0:T(8,128)S(1)}, u32[]{:S(2)}, u32[]{:S(2)}) collective-permute-start(f32[4,2,20,128]{3,2,1,0:T(8,128)S(1)} %collect.1.crossed), channel_id=1, source_target_pairs={{0,2},{2,0},{4,6},{6,4},{8,10},{10,8},{12,14},{14,12},{16,18},{18,... | collective-permute-start | bytes 245768 | tf_op jit(solution)/shard_map/ppermute | solution.py:445

commit v6 on v5

--- a/solution.py
+++ b/solution.py
@@ -237,9 +237,27 @@
         out[i] = piece[...]
 
 
+def forward_kernel(planes, group, halves, lines, ready, from_left, from_right, fronts, end):
+    read = reader(lines, group, planes, ITEMS)
+    last = lines.shape[0] // (group * planes * ITEMS) * planes
+    first = lax.broadcasted_iota(jnp.int32, (group, LANES), 0) < halves
+
+    def right(a):
+        side = read(a, SIDE)
+        result = []
+        for f in range(F):
+            at = (a * F + f) * group
+            halo = jnp.where(first, from_left[at : at + group, :], from_right[at : at + group, :])
+            result.append(ready[at : at + group, :] + side * halo)
+        return result
+
+    vector = forward(read, right, last, group, fronts)
+    for f in range(F):
+        end[f] = vector[f]
+
+
 def second_kernel(
-    planes, group, halves, part, azim, lines, ready, from_left, from_right, face, crossed, partner,
-    out, fronts,
+    planes, group, halves, part, azim, lines, fronts, end, face, crossed, partner, out
 ):
     read = reader(lines, group, planes, ITEMS)
     last = lines.shape[0] // (group * planes * ITEMS) * planes
@@ -278,22 +296,10 @@
         ]
         for j in range(rows)
     ]
-    first = lax.broadcasted_iota(jnp.int32, (group, LANES), 0) < halves
-
-    def right(a):
-        side = read(a, SIDE)
-        result = []
-        for f in range(F):
-            at = (a * F + f) * group
-            halo = jnp.where(first, from_left[at : at + group, :], from_right[at : at + group, :])
-            entry = ready[at : at + group, :] + side * halo
-            if a == last - 1:
-                face_rows = jnp.concatenate([picked[j][f] for j in range(rows)], axis=0)
-                entry = entry - read(a, UPPER) * face_rows
-            result.append(entry)
-        return result
-
-    vector = forward(read, right, last, group, fronts)
+    upper = read(last - 1, UPPER)
+    vector = [
+        end[f] - upper * jnp.concatenate([picked[j][f] for j in range(rows)], axis=0) for f in range(F)
+    ]
 
     def emit(a, values):
         for f in range(F):
@@ -443,13 +449,21 @@
         name="collect",
     )(ready, *crossed)
     partner = lax.ppermute(crossed, "axial", core)
+    fronts, end = pl.pallas_call(
+        functools.partial(forward_kernel, planes, group, halves),
+        out_shape=(
+            jax.ShapeDtypeStruct((last, F, group, LANES), f32),
+            jax.ShapeDtypeStruct((F, group, LANES), f32),
+        ),
+        compiler_params=params(),
+        name="second_forward",
+    )(lines, ready, from_left, from_right)
     value = pl.pallas_call(
         functools.partial(second_kernel, planes, group, halves, part, azim),
         out_shape=shape,
-        scratch_shapes=[scratch],
-        compiler_params=params(),
-        name="second_sweep",
-    )(lines, ready, from_left, from_right, face, crossed, partner)
+        compiler_params=params(),
+        name="second_backward",
+    )(lines, fronts, end, face, crossed, partner)
     value = lax.all_to_all(
         value.reshape(n, planes * F * group, LANES), "axial", 0, 0, axis_index_groups=axial, tiled=True
     )

time: 50.5 us -> 50.5 us (level)
  transfers between devices with their start and end apart: 17 -> 17, of which waited for: 5 -> 5; matrix products, arithmetic and copies ran while one was open for 0% -> 0% of each run, Pallas kernels for 9% -> 10%
where the time goes in v6:
time: 50.5 us; the launch traced here: 50.3 us
  starting transfers between devices  26.6 us (53%)
  blocking collectives  8.43 us (17%)
  Pallas kernels  7.77 us (15%)
  waiting for transfers between devices  7.42 us (15%)
    ppermute x7, starting transfers between devices, shards(): lax.ppermute(packed[k], 'axial', [(i, i ^ k) for i in range(2 * n)])  12.5 us
    all_to_all x1, blocking collectives, shards(): lax.all_to_all(value.reshape(n, planes * F * group, LANES), 'axial', 0, 0...  8.43 us
    ppermute x4, starting transfers between devices, shards(): crossed.append(lax.ppermute(chip, both, there + [(b, a) for a, b in there]))  7.71 us
    ppermute x7, waiting for transfers between devices, shards(): lax.ppermute(packed[k], 'axial', [(i, i ^ k) for i in range(2 * n)])  5.33 us
    ppermute x2, starting transfers between devices, around(): got = lax.ppermute(up, 'azim', forward)  4.64 us
    pallas_call x1, Pallas kernels, shards(): pl.pallas_call(functools.partial(pack_kernel, n), out_shape=[jax.ShapeDty...  2.22 us
    ppermute x2, starting transfers between devices, shards(): lax.ppermute(first, both, [(n * azim + y, (n - 1) * azim + (y + k) % azim...  1.33 us
    pallas_call x1, Pallas kernels, shards(): pl.pallas_call(fetch_kernel, in_specs=[hbm] * 6, out_shape=[jax.ShapeDtyp...  1.27 us
  transfers between devices with their start and end apart: 17, of which 5 were waited for; matrix products, arithmetic and copies ran while one was open for 0% of the time, Pallas kernels for 10%

profile of v6, /device:TPU:0, one launch (start us, length us, event | category | flops | bytes accessed | tf_op | source)
XLA Modules:
  0.0 50.3 jit_solution(12155858663581768118)
XLA Ops:
  0.0 3.0 %collective-permute-start.2 = (f32[2,5,15,2,128]{4,3,2,1,0:T(2,128)}, f32[2,5,15,2,128]{4,3,2,1,0:T(2,128)S(1)}, u32[]{:S(2)}, u32[]{:S(2)}) collective-permute-start(f32[2,5,15,2,128]{4,3,2,1,0:T(2,128)} %bitcast.13), channel_id=1, source_target_pairs={{0,1},{1,0},{2,3},{3,2},{4,5},{5,4},{6,7},{7,6},{8,9},{9,8},{10,11... | collective-permute-start | bytes 460808 | tf_op jit(solution)/shard_map/ppermute | solution.py:350
  3.0 1.3 %fetch.1 = (f32[2,5,15,2,128]{4,3,2,1,0:T(2,128)S(1)}, f32[2,5,15,2,128]{4,3,2,1,0:T(2,128)S(1)}, bf16[2,5,5,15,2,128]{5,4,3,2,1,0:T(2,128)(2,1)S(1)}, f32[3,2,1...) custom-call(f32[2,5,15,2,128]{4,3,2,1,0:T(2,128)} %bitcast.12, ...), custom_call_target="tpu_custom_call" | custom-call | tf_op jit(solution)/shard_map/fetch/pallas_call | solution.py:366
  4.2 0.7 %collective-permute-start.1 = (f32[5,15,2,128]{3,2,1,0:T(2,128)S(1)}, f32[5,15,2,128]{3,2,1,0:T(2,128)S(1)}, u32[]{:S(2)}, u32[]{:S(2)}) collective-permute-start(f32[5,15,2,128]{3,2,1,0:T(2,128)S(1)} %get-tuple-element.34), channel_id=1, source_target_pairs={{16,15},{17,14}} | collective-permute-start | bytes 230408 | tf_op jit(solution)/shard_map/ppermute | solution.py:376
  4.9 0.7 %collective-permute-start = (f32[5,15,2,128]{3,2,1,0:T(2,128)S(1)}, f32[5,15,2,128]{3,2,1,0:T(2,128)S(1)}, u32[]{:S(2)}, u32[]{:S(2)}) collective-permute-start(f32[5,15,2,128]{3,2,1,0:T(2,128)S(1)} %get-tuple-element.34), channel_id=1, source_target_pairs={{16,14},{17,15}} | collective-permute-start | bytes 230408 | tf_op jit(solution)/shard_map/ppermute | solution.py:376
  5.6 2.2 %pack.1 = (f32[264,128]{1,0:T(8,128)S(1)}, f32[264,128]{1,0:T(8,128)S(1)}, f32[264,128]{1,0:T(8,128)S(1)}, f32[264,128]{1,0:T(8,128)S(1)}, f32[264,128]{1,0:T(8,...) custom-call(f32[2,5,15,2,128]{4,3,2,1,0:T(2,128)S(1)} %get-tuple-ele, ...), custom_call_target="tpu_custom_call" | custom-call | tf_op jit(solution)/shard_map/pack/pallas_call | solution.py:381
  7.8 0.0 collective-permute-done.1.refs_1_
  7.8 0.0 collective-permute-done.refs_0_
  7.8 0.0 collective-permute-done.2.refs_2_.refs_3_
  7.8 1.0 %right_side.1 = (f32[304,128]{1,0:T(8,128)S(1)}, f32[304,128]{1,0:T(8,128)S(1)}, f32[304,128]{1,0:T(8,128)S(1)}, f32[304,128]{1,0:T(8,128)S(1)}, f32[304,128]{1,...) custom-call(f32[5,15,2,128]{3,2,1,0:T(2,128)S(1)} %collective-permute-done.refs_0_, ...), custom_call_target="tpu_custom_call" | custom-call | tf_op jit(solution)/shard_map/right_side/pallas_call | solution.py:394
  8.9 2.6 %collective-permute-start.3 = (f32[304,128]{1,0:T(8,128)S(1)}, f32[304,128]{1,0:T(8,128)S(1)}, u32[]{:S(2)}, u32[]{:S(2)}) collective-permute-start(f32[304,128]{1,0:T(8,128)S(1)} %get-tuple-element.50), channel_id=1, source_target_pairs={{0,12},{2,14},{4,8},{6,10},{8,4},{10,6},{12,0},{14,2},{16,28},{18,... | collective-permute-start | bytes 466952 | tf_op jit(solution)/shard_map/ppermute | solution.py:406
  11.4 0.5 %collective-permute-start.4 = (f32[304,128]{1,0:T(8,128)S(1)}, f32[304,128]{1,0:T(8,128)S(1)}, u32[]{:S(2)}, u32[]{:S(2)}) collective-permute-start(f32[304,128]{1,0:T(8,128)S(1)} %get-tuple-element.51), channel_id=1, source_target_pairs={{0,4},{2,6},{4,0},{6,2},{8,12},{10,14},{12,8},{14,10},{16,20},{18,... | collective-permute-start | bytes 466952 | tf_op jit(solution)/shard_map/ppermute | solution.py:406
  11.9 0.4 collective-permute-start.5
  12.4 5.1 %collective-permute-start.6 = (f32[304,128]{1,0:T(8,128)S(1)}, f32[304,128]{1,0:T(8,128)S(1)}, u32[]{:S(2)}, u32[]{:S(2)}) collective-permute-start(f32[304,128]{1,0:T(8,128)S(1)} %get-tuple-element.54), channel_id=1, source_target_pairs={{0,14},{2,12},{4,10},{6,8},{8,6},{10,4},{12,2},{14,0},{16,30},{18,... | collective-permute-start | bytes 466952 | tf_op jit(solution)/shard_map/ppermute | solution.py:406
  17.5 0.0 collective-permute-start.7
  17.5 0.0 collective-permute-done.3.refs_0_
  17.5 0.6 %collective-permute-start.8 = (f32[304,128]{1,0:T(8,128)S(1)}, f32[304,128]{1,0:T(8,128)S(1)}, u32[]{:S(2)}, u32[]{:S(2)}) collective-permute-start(f32[304,128]{1,0:T(8,128)S(1)} %get-tuple-element.56), channel_id=1, source_target_pairs={{0,10},{2,8},{4,14},{6,12},{8,2},{10,0},{12,6},{14,4},{16,26},{18,... | collective-permute-start | bytes 466952 | tf_op jit(solution)/shard_map/ppermute | solution.py:406
  18.2 0.0 collective-permute-done.4.refs_1_
  18.2 3.2 %collective-permute-start.9 = (f32[304,128]{1,0:T(8,128)S(1)}, f32[304,128]{1,0:T(8,128)S(1)}, u32[]{:S(2)}, u32[]{:S(2)}) collective-permute-start(f32[304,128]{1,0:T(8,128)S(1)} %get-tuple-element.57), channel_id=1, source_target_pairs={{0,2},{2,0},{4,6},{6,4},{8,10},{10,8},{12,14},{14,12},{16,18},{18,... | collective-permute-start | bytes 466952 | tf_op jit(solution)/shard_map/ppermute | solution.py:406
  21.4 0.0 collective-permute-done.5.refs_2_
  21.4 4.4 %collective-permute-done.6.refs_4_ = f32[304,128]{1,0:T(8,128)S(1)} collective-permute-done((f32[304,128]{1,0:T(8,128)S(1)}, f32[304,128]{1,0:T(8,128)S(1)}, u32[]{:S(2)}, u32[]{:S(2)}) %collective-permute-start.6) | collective-permute-done | bytes 155680 | tf_op jit(solution)/shard_map/ppermute | solution.py:406
  25.8 0.9 %collective-permute-done.7.refs_5_ = f32[304,128]{1,0:T(8,128)S(1)} collective-permute-done((f32[304,128]{1,0:T(8,128)S(1)}, f32[304,128]{1,0:T(8,128)S(1)}, u32[]{:S(2)}, u32[]{:S(2)}) %collective-permute-start.7) | collective-permute-done | bytes 155680 | tf_op jit(solution)/shard_map/ppermute | solution.py:406
  26.7 0.0 collective-permute-done.8.refs_6_
  26.7 0.0 collective-permute-done.9.refs_7_
  26.7 0.4 first_sweep.1
  27.1 0.1 collective-permute-start.11
  27.2 1.7 %collective-permute-start.10 = (f32[320,128]{1,0:T(8,128)S(1)}, f32[320,128]{1,0:T(8,128)S(1)}, u32[]{:S(2)}, u32[]{:S(2)}) collective-permute-start(f32[320,128]{1,0:T(8,128)S(1)} %get-tuple-element.60.swapped), channel_id=1, source_target_pairs={{0,1},{1,0},{2,3},{3,2},{4,5},{5,4},{6,7},{7,6},{8,9},{9,8},{10,11... | collective-permute-start | bytes 491528 | tf_op jit(solution)/shard_map/ppermute | solution.py:350
  28.9 0.0 collective-permute-done.11
  28.9 1.9 %collective-permute-start.15 = (f32[2,20,128]{2,1,0:T(8,128)S(1)}, f32[2,20,128]{2,1,0:T(8,128)S(1)}, u32[]{:S(2)}, u32[]{:S(2)}) collective-permute-start(f32[2,20,128]{2,1,0:T(8,128)S(1)} %pad_maximum_fusion), channel_id=1, source_target_pairs={{16,9},{17,8},{18,15},{19,14},{20,13},{21,12},{22,11},{23,10},{24,... | collective-permute-start | bytes 61448 | tf_op jit(solution)/shard_map/ppermute | solution.py:432
  30.8 2.4 %collective-permute-start.14 = (f32[2,20,128]{2,1,0:T(8,128)S(1)}, f32[2,20,128]{2,1,0:T(8,128)S(1)}, u32[]{:S(2)}, u32[]{:S(2)}) collective-permute-start(f32[2,20,128]{2,1,0:T(8,128)S(1)} %pad_maximum_fusion), channel_id=1, source_target_pairs={{16,8},{17,9},{18,14},{19,15},{20,12},{21,13},{22,10},{23,11},{24,... | collective-permute-start | bytes 61448 | tf_op jit(solution)/shard_map/ppermute | solution.py:432
  33.3 0.0 collective-permute-start.13
  33.3 3.4 %collective-permute-start.12 = (f32[2,20,128]{2,1,0:T(8,128)S(1)}, f32[2,20,128]{2,1,0:T(8,128)S(1)}, u32[]{:S(2)}, u32[]{:S(2)}) collective-permute-start(f32[2,20,128]{2,1,0:T(8,128)S(1)} %pad_maximum_fusion), channel_id=1, source_target_pairs={{16,0},{17,1},{18,6},{19,7},{20,4},{21,5},{22,2},{23,3},{24,8},{25... | collective-permute-start | bytes 61448 | tf_op jit(solution)/shard_map/ppermute | solution.py:432
  36.6 1.1 %spectral_term.1.ready.waited = f32[320,128]{1,0:T(8,128)S(1)} custom-call(f32[2112,128]{1,0:T(8,128)S(1)} %get-tuple-element.58.lines, f32[320,128]{1,0:T(8,128)S(1)} %get-tuple-element.59.value, f32[320,128]{1,0:T(8,128)S(1)} %get-tuple-element.60.swapped, f32[15,15]{1,0:T(8,128)S(1)} %get-tuple-element.39.spectral), custom_call_target="tpu_custom_call" | custom-call | tf_op jit(solution)/shard_map/spectral_term/pallas_call | solution.py:433
  37.8 0.0 collective-permute-done.15.refs_3_
  37.8 0.0 collective-permute-done.14.refs_2_
  37.8 1.1 %collective-permute-done.13.refs_1_ = f32[2,20,128]{2,1,0:T(8,128)S(1)} collective-permute-done((f32[2,20,128]{2,1,0:T(8,128)S(1)}, f32[2,20,128]{2,1,0:T(8,128)S(1)}, u32[]{:S(2)}, u32[]{:S(2)}) %collective-permute-start.13) | collective-permute-done | bytes 20512 | tf_op jit(solution)/shard_map/ppermute | solution.py:432
  38.9 0.1 collective-permute-done.12.refs_0_
  39.0 0.3 collective-permute-start.16
  39.2 0.0 collective-permute-done.10.from_left.from_right
  39.2 0.2 second_forward.1
  39.4 0.9 %collective-permute-done.16.partner = f32[4,2,20,128]{3,2,1,0:T(8,128)S(1)} collective-permute-done((f32[4,2,20,128]{3,2,1,0:T(8,128)S(1)}, f32[4,2,20,128]{3,2,1,0:T(8,128)S(1)}, u32[]{:S(2)}, u32[]{:S(2)}) %collective-permute-start.16) | collective-permute-done | bytes 81952 | tf_op jit(solution)/shard_map/ppermute | solution.py:451
  40.3 0.5 %second_backward.1 = f32[320,128]{1,0:T(8,128)S(1)} custom-call(f32[2112,128]{1,0:T(8,128)S(1)} %get-tuple-element.58.lines, f32[16,5,4,128]{3,2,1,0:T(4,128)S(1)} %get-tuple-element.61.fronts, f32[5,4,128]{2,1,0:T(4,128)S(1)} %get-tuple-element.62.end, s32[2,128]{1,0:T(2,128)S(1)} %get-tuple-element.41.refs_7_.face, f32[4,2,20,128]{3,2,1,0:T(8,128)S(1)} %collect.1.crossed, ...), custom_call_target="tpu_custom_call" | custom-call | tf_op jit(solution)/shard_map/second_backward/pallas_call | solution.py:461
  40.8 8.4 %all_to_all.5.value = f32[8,40,128]{2,1,0:T(8,128)S(1)} all-to-all(f32[8,40,128]{2,1,0:T(8,128)S(1)} %bitcast.10), channel_id=1, replica_groups={{0,2,4,6,8,10,12,14},{16,18,20,22,24,26,28,30},{1,3,5,7,9,11,13,15},{17..., dimensions={0} | all-to-all | bytes 327680 | tf_op jit(solution)/shard_map/all_to_all | solution.py:467
  49.3 1.0 %unpack.1 = f32[2,5,15,2,128]{4,3,2,1,0:T(2,128)} custom-call(f32[8,40,128]{2,1,0:T(8,128)S(1)} %all_to_all.5.value), custom_call_target="tpu_custom_call" | custom-call | tf_op jit(solution)/shard_map/unpack/pallas_call | solution.py:470
  (3 shorter events, 0.0 us)
Async XLA Ops:
  0.0 7.8 %collective-permute-start.2 = (f32[2,5,15,2,128]{4,3,2,1,0:T(2,128)}, f32[2,5,15,2,128]{4,3,2,1,0:T(2,128)S(1)}, u32[]{:S(2)}, u32[]{:S(2)}) collective-permute-start(f32[2,5,15,2,128]{4,3,2,1,0:T(2,128)} %bitcast.13), channel_id=1, source_target_pairs={{0,1},{1,0},{2,3},{3,2},{4,5},{5,4},{6,7},{7,6},{8,9},{9,8},{10,11... | collective-permute-start | bytes 460808 | tf_op jit(solution)/shard_map/ppermute | solution.py:350
  4.2 3.6 %collective-permute-start.1 = (f32[5,15,2,128]{3,2,1,0:T(2,128)S(1)}, f32[5,15,2,128]{3,2,1,0:T(2,128)S(1)}, u32[]{:S(2)}, u32[]{:S(2)}) collective-permute-start(f32[5,15,2,128]{3,2,1,0:T(2,128)S(1)} %get-tuple-element.34), channel_id=1, source_target_pairs={{16,15},{17,14}} | collective-permute-start | bytes 230408 | tf_op jit(solution)/shard_map/ppermute | solution.py:376
  4.9 2.9 %collective-permute-start = (f32[5,15,2,128]{3,2,1,0:T(2,128)S(1)}, f32[5,15,2,128]{3,2,1,0:T(2,128)S(1)}, u32[]{:S(2)}, u32[]{:S(2)}) collective-permute-start(f32[5,15,2,128]{3,2,1,0:T(2,128)S(1)} %get-tuple-element.34), channel_id=1, source_target_pairs={{16,14},{17,15}} | collective-permute-start | bytes 230408 | tf_op jit(solution)/shard_map/ppermute | solution.py:376
  8.9 8.7 %collective-permute-start.3 = (f32[304,128]{1,0:T(8,128)S(1)}, f32[304,128]{1,0:T(8,128)S(1)}, u32[]{:S(2)}, u32[]{:S(2)}) collective-permute-start(f32[304,128]{1,0:T(8,128)S(1)} %get-tuple-element.50), channel_id=1, source_target_pairs={{0,12},{2,14},{4,8},{6,10},{8,4},{10,6},{12,0},{14,2},{16,28},{18,... | collective-permute-start | bytes 466952 | tf_op jit(solution)/shard_map/ppermute | solution.py:406
  11.4 6.8 %collective-permute-start.4 = (f32[304,128]{1,0:T(8,128)S(1)}, f32[304,128]{1,0:T(8,128)S(1)}, u32[]{:S(2)}, u32[]{:S(2)}) collective-permute-start(f32[304,128]{1,0:T(8,128)S(1)} %get-tuple-element.51), channel_id=1, source_target_pairs={{0,4},{2,6},{4,0},{6,2},{8,12},{10,14},{12,8},{14,10},{16,20},{18,... | collective-permute-start | bytes 466952 | tf_op jit(solution)/shard_map/ppermute | solution.py:406
  11.9 9.4 %collective-permute-start.5 = (f32[304,128]{1,0:T(8,128)S(1)}, f32[304,128]{1,0:T(8,128)S(1)}, u32[]{:S(2)}, u32[]{:S(2)}) collective-permute-start(f32[304,128]{1,0:T(8,128)S(1)} %get-tuple-element.52), channel_id=1, source_target_pairs={{0,8},{2,10},{4,12},{6,14},{8,0},{10,2},{12,4},{14,6},{16,24},{18,... | collective-permute-start | bytes 466952 | tf_op jit(solution)/shard_map/ppermute | solution.py:406
  12.4 13.4 %collective-permute-start.6 = (f32[304,128]{1,0:T(8,128)S(1)}, f32[304,128]{1,0:T(8,128)S(1)}, u32[]{:S(2)}, u32[]{:S(2)}) collective-permute-start(f32[304,128]{1,0:T(8,128)S(1)} %get-tuple-element.54), channel_id=1, source_target_pairs={{0,14},{2,12},{4,10},{6,8},{8,6},{10,4},{12,2},{14,0},{16,30},{18,... | collective-permute-start | bytes 466952 | tf_op jit(solution)/shard_map/ppermute | solution.py:406
  17.5 9.2 %collective-permute-start.7 = (f32[304,128]{1,0:T(8,128)S(1)}, f32[304,128]{1,0:T(8,128)S(1)}, u32[]{:S(2)}, u32[]{:S(2)}) collective-permute-start(f32[304,128]{1,0:T(8,128)S(1)} %get-tuple-element.55), channel_id=1, source_target_pairs={{0,6},{2,4},{4,2},{6,0},{8,14},{10,12},{12,10},{14,8},{16,22},{18,... | collective-permute-start | bytes 466952 | tf_op jit(solution)/shard_map/ppermute | solution.py:406
  17.5 9.2 %collective-permute-start.8 = (f32[304,128]{1,0:T(8,128)S(1)}, f32[304,128]{1,0:T(8,128)S(1)}, u32[]{:S(2)}, u32[]{:S(2)}) collective-permute-start(f32[304,128]{1,0:T(8,128)S(1)} %get-tuple-element.56), channel_id=1, source_target_pairs={{0,10},{2,8},{4,14},{6,12},{8,2},{10,0},{12,6},{14,4},{16,26},{18,... | collective-permute-start | bytes 466952 | tf_op jit(solution)/shard_map/ppermute | solution.py:406
  18.2 8.5 %collective-permute-start.9 = (f32[304,128]{1,0:T(8,128)S(1)}, f32[304,128]{1,0:T(8,128)S(1)}, u32[]{:S(2)}, u32[]{:S(2)}) collective-permute-start(f32[304,128]{1,0:T(8,128)S(1)} %get-tuple-element.57), channel_id=1, source_target_pairs={{0,2},{2,0},{4,6},{6,4},{8,10},{10,8},{12,14},{14,12},{16,18},{18,... | collective-permute-start | bytes 466952 | tf_op jit(solution)/shard_map/ppermute | solution.py:406
  27.1 1.8 %collective-permute-start.11 = (f32[20,128]{1,0:T(8,128)S(1)}, f32[20,128]{1,0:T(8,128)S(1)}, u32[]{:S(2)}, u32[]{:S(2)}) collective-permute-start(f32[20,128]{1,0:T(8,128)S(1)} %get-tuple-element.64), channel_id=1, source_target_pairs={{0,2},{2,0},{4,6},{6,4},{8,10},{10,8},{12,14},{14,12},{16,18},{18,... | collective-permute-start | bytes 30728 | tf_op jit(solution)/shard_map/ppermute | solution.py:421
  27.2 12.0 %collective-permute-start.10 = (f32[320,128]{1,0:T(8,128)S(1)}, f32[320,128]{1,0:T(8,128)S(1)}, u32[]{:S(2)}, u32[]{:S(2)}) collective-permute-start(f32[320,128]{1,0:T(8,128)S(1)} %get-tuple-element.60.swapped), channel_id=1, source_target_pairs={{0,1},{1,0},{2,3},{3,2},{4,5},{5,4},{6,7},{7,6},{8,9},{9,8},{10,11... | collective-permute-start | bytes 491528 | tf_op jit(solution)/shard_map/ppermute | solution.py:350
  28.9 8.8 %collective-permute-start.15 = (f32[2,20,128]{2,1,0:T(8,128)S(1)}, f32[2,20,128]{2,1,0:T(8,128)S(1)}, u32[]{:S(2)}, u32[]{:S(2)}) collective-permute-start(f32[2,20,128]{2,1,0:T(8,128)S(1)} %pad_maximum_fusion), channel_id=1, source_target_pairs={{16,9},{17,8},{18,15},{19,14},{20,13},{21,12},{22,11},{23,10},{24,... | collective-permute-start | bytes 61448 | tf_op jit(solution)/shard_map/ppermute | solution.py:432
  30.8 6.9 %collective-permute-start.14 = (f32[2,20,128]{2,1,0:T(8,128)S(1)}, f32[2,20,128]{2,1,0:T(8,128)S(1)}, u32[]{:S(2)}, u32[]{:S(2)}) collective-permute-start(f32[2,20,128]{2,1,0:T(8,128)S(1)} %pad_maximum_fusion), channel_id=1, source_target_pairs={{16,8},{17,9},{18,14},{19,15},{20,12},{21,13},{22,10},{23,11},{24,... | collective-permute-start | bytes 61448 | tf_op jit(solution)/shard_map/ppermute | solution.py:432
  33.3 5.6 %collective-permute-start.13 = (f32[2,20,128]{2,1,0:T(8,128)S(1)}, f32[2,20,128]{2,1,0:T(8,128)S(1)}, u32[]{:S(2)}, u32[]{:S(2)}) collective-permute-start(f32[2,20,128]{2,1,0:T(8,128)S(1)} %pad_maximum_fusion), channel_id=1, source_target_pairs={{16,1},{17,0},{18,7},{19,6},{20,5},{21,4},{22,3},{23,2},{24,9},{25... | collective-permute-start | bytes 61448 | tf_op jit(solution)/shard_map/ppermute | solution.py:432
  33.3 5.7 %collective-permute-start.12 = (f32[2,20,128]{2,1,0:T(8,128)S(1)}, f32[2,20,128]{2,1,0:T(8,128)S(1)}, u32[]{:S(2)}, u32[]{:S(2)}) collective-permute-start(f32[2,20,128]{2,1,0:T(8,128)S(1)} %pad_maximum_fusion), channel_id=1, source_target_pairs={{16,0},{17,1},{18,6},{19,7},{20,4},{21,5},{22,2},{23,3},{24,8},{25... | collective-permute-start | bytes 61448 | tf_op jit(solution)/shard_map/ppermute | solution.py:432
  39.0 1.4 %collective-permute-start.16 = (f32[4,2,20,128]{3,2,1,0:T(8,128)S(1)}, f32[4,2,20,128]{3,2,1,0:T(8,128)S(1)}, u32[]{:S(2)}, u32[]{:S(2)}) collective-permute-start(f32[4,2,20,128]{3,2,1,0:T(8,128)S(1)} %collect.1.crossed), channel_id=1, source_target_pairs={{0,2},{2,0},{4,6},{6,4},{8,10},{10,8},{12,14},{14,12},{16,18},{18,... | collective-permute-start | bytes 245768 | tf_op jit(solution)/shard_map/ppermute | solution.py:451
